TPU v7x, 128 devices: a whole 4x4x4 slice. The times are simulated.
128 devices in a mesh: ray: 4 (over y), mp: 32 (over x, z, core).
Axes of the slice: x: 4, y: 4, z: 4, core: 2. Of those that a mesh axis runs over, the one named last changes fastest.
Arguments:
- coeffs_start: float32 [131072, 128], P('mp', 'ray'), may hold values from -6 to 6
- observed: float32 [32768, 128], P('ray'), may hold values from -6 to 6
- jacobian_tiles: bfloat16 [4, 32, 384, 128, 128], P('ray', 'mp'), may hold values from -0.0625 to 0.0625
- tile_rows: int32 [4, 32, 384], P('ray', 'mp'), may hold values from 0 to 63, as said below
- tile_cols: int32 [4, 32, 384], P('ray', 'mp'), may hold values from 0 to 31, as said below
- tile_count: int32 [4, 32], P('ray', 'mp'), may hold values from 48 to 384, as said below
Outputs:
- coefficients: float32 [131072, 128], P('mp', 'ray')
- misfit: float32 [32768, 128], P(('ray', 'mp'))
Inputs may be any that keep to these rules, and one draw needn't show every extreme that they name: `tile_count`: every device has at least 48 live slots, and one device has all 384. `tile_rows`: the 384 slots of one device name distinct pairs of ray block and cell tile. `tile_cols`: the 384 slots of one device name distinct pairs of ray block and cell tile.
All inputs are finite; a program needn't handle non-finite values.
Results may differ from a plain program's by a relative error of at most 0.0053.
Values may be sent and summed in bfloat16 or wider, within the bound.
No kernel may reach another device: no remote copies, remote signals or barrier semaphores. Data moves between devices by JAX's collectives and lax.ppermute only.
A program may use at most 128 MiB of HBM per device.

v0:
```python
import math

import jax
import jax.numpy as jnp
from jax import lax
from jax.experimental import pallas as pl
from jax.experimental.pallas import tpu as pltpu
from jax.sharding import Mesh, PartitionSpec as P


LEVELS = 5
ITERS = 2
TILE = 128
GROUP = 48
CHUNK = 16
ROW_BLOCKS = 64
CELL_TILES = 32


root_three = math.sqrt(3.0)
norm_factor = 4.0 * math.sqrt(2.0)
low_pass = [
    (1.0 + root_three) / norm_factor,
    (3.0 + root_three) / norm_factor,
    (3.0 - root_three) / norm_factor,
    (1.0 - root_three) / norm_factor,
]
high_pass = [low_pass[3], -low_pass[2], low_pass[1], -low_pass[0]]
step_length = 0.5
threshold = 0.1

f32 = jnp.float32
bf16 = jnp.bfloat16

SEG_ROWS = [512, 256, 128, 64, 32, 32]
SEG_OFF = [0]
for n in SEG_ROWS:
    SEG_OFF.append(SEG_OFF[-1] + 8 + n)
STATE_ROWS = SEG_OFF[-1]
COEF_OFF = [0, 2048, 3072, 3584, 3840, 3968]

VM = pl.BlockSpec(memory_space=pltpu.VMEM)
SM = pl.BlockSpec(memory_space=pltpu.SMEM)
ANY = pl.BlockSpec(memory_space=pl.ANY)


def sds(shape, dtype):
    return jax.ShapeDtypeStruct(shape, dtype)


def call(kernel, in_specs, outs, scratch=(), mib=40):
    return pl.pallas_call(
        kernel,
        in_specs=in_specs,
        out_specs=[VM] * len(outs),
        out_shape=outs,
        scratch_shapes=list(scratch),
        compiler_params=pltpu.CompilerParams(vmem_limit_bytes=mib * 1024 * 1024),
    )


def lanes(shape):
    return lax.broadcasted_iota(jnp.int32, shape, 1)


def init_kernel(coeffs, state, tails):
    for g in range(6):
        n = SEG_ROWS[g]
        base = SEG_OFF[g]
        parts = [coeffs[:, COEF_OFF[g] + q * n : COEF_OFF[g] + (q + 1) * n] for q in range(4)]
        packed = jnp.concatenate(parts, axis=0).T
        state[base + 8 : base + 8 + n, :] = packed
        last = packed[n - 8 : n, :]
        state[base : base + 8, :] = pltpu.roll(last, 32, 1)
        tails[8 * g : 8 * g + 8, :] = last


def axes(place, core):
    first = jnp.where(core == 0, place[1], place[0])
    second = jnp.where(core == 0, place[0], place[1])
    step = jnp.where(core == 0, 1, 4)
    return first, second, step, 5 - step


def tile_copies(jac, jbuf, sems, live):
    def copy(i):
        part = pl.ds(i * CHUNK, CHUNK)
        return pltpu.make_async_copy(jac.at[part], jbuf.at[part], sems.at[i])

    groups = (live + GROUP - 1) // GROUP
    per = GROUP // CHUNK

    for i in range(jac.shape[0] // CHUNK):
        @pl.when(i < groups * per)
        def _():
            copy(i).start()

    def arrive(g):
        for i in range(per):
            copy(g * per + i).wait()

    return groups, arrive


def synth_from(state, bufs, model):
    src = None
    for level in reversed(range(LEVELS)):
        n = SEG_ROWS[level]
        base = SEG_OFF[level]
        if src is None:
            sm = state[SEG_OFF[5] + 4 : SEG_OFF[5] + 8 + n, :]
            sp = state[SEG_OFF[5] + 3 : SEG_OFF[5] + 7 + n, :]
        else:
            sm = src[4 : 8 + n, :]
            sp = src[3 : 7 + n, :]
        dm = state[base + 4 : base + 8 + n, :]
        dp = state[base + 3 : base + 7 + n, :]
        even = low_pass[0] * sm + high_pass[0] * dm + low_pass[2] * sp + high_pass[2] * dp
        odd = low_pass[1] * sm + high_pass[1] * dm + low_pass[3] * sp + high_pass[3] * dp
        dst = bufs[level]
        dst[pl.ds(0, n + 4, stride=2), :] = even
        dst[pl.ds(1, n + 4, stride=2), :] = odd
        src = dst
    model[...] = src[8:1032, :].astype(bf16)


SYNTH_BUFS = [pltpu.VMEM((8 + 2 * SEG_ROWS[l], 128), f32) for l in range(LEVELS)]


def early_kernel(state, model, *bufs):
    synth_from(state, bufs, model)


def synth_kernel(state_in, recv, state, fix, *scratch):
    state[...] = state_in[...]
    for g in range(6):
        base = SEG_OFF[g]
        own = state_in[base : base + 8, :]
        got = pltpu.roll(recv[8 * g : 8 * g + 8, :], 32, 1)
        state[base : base + 8, :] = jnp.where(lanes((8, 128)) < 32, got, own)
    model = scratch[-1]
    synth_from(state, scratch[:-1], model)
    fix[...] = model[0:128, :]


def first_kernel(rows, cols, cnt, place, f0, f1, f2, f3, *refs):
    fwd_kernel(rows, cols, cnt, place, *refs, fixes=(f0, f1, f2, f3))


def fwd_kernel(
    rows, cols, cnt, place, p0, p1, p2, p3, jac, keep, send, jbuf, model, acc, sems, fixes=None
):
    live = cnt[0]
    core = place[2]
    groups, arrive = tile_copies(jac, jbuf, sems, live)
    acc[...] = jnp.zeros(acc.shape, f32)
    for c in range(CELL_TILES):
        q, t = c // 8, c % 8
        pieces = fixes if c == 0 and fixes else (p0, p1, p2, p3)
        model[c] = jnp.concatenate(
            [p[128 * t : 128 * t + 128, 32 * q : 32 * q + 32] for p in pieces], axis=1
        )

    def group(g, carry):
        arrive(g)
        for v in range(GROUP):
            s = g * GROUP + v
            r = jnp.where(s < live, rows[s], ROW_BLOCKS)
            acc[r] += jnp.dot(jbuf[s], model[cols[s]], preferred_element_type=f32)
        return carry

    lax.fori_loop(0, groups, group, 0)
    for xz in range(16):
        for h in range(2):
            keep[2 * xz + h] = acc[4 * xz + 2 * core + h]
            send[2 * xz + h] = acc[4 * xz + 2 * (1 - core) + h].astype(bf16)


def split_kernel(place, keep, recv, own, s1, s2, s3):
    first, _, step, other = axes(place, place[2])
    for k, out in enumerate((own, s1, s2, s3)):
        for e in range(4):
            for h in range(2):
                b = 2 * (step * ((first + k) % 4) + other * e) + h
                out[2 * e + h] = (keep[b] + recv[b].astype(f32)).astype(out.dtype)


def gather_kernel(own, r1, r2, r3, total, sent):
    for i in range(8):
        s = own[i] + r1[i].astype(f32) + r2[i].astype(f32) + r3[i].astype(f32)
        total[i] = s
        sent[i] = s.astype(bf16)


def misfit_tile(own, r1, r2, r3, obs, i):
    return own[i] + r1[i].astype(f32) + r2[i].astype(f32) + r3[i].astype(f32) - obs[i]


def obs_kernel(place, obs, out):
    back = (128 - 32 * place[3]) % 128
    for i in range(8):
        out[i] = pltpu.roll(obs[i // 2, 128 * (i % 2) : 128 * (i % 2) + 128, :], back, 1)


def misfit_kernel(own, r1, r2, r3, obs, rounded):
    for i in range(8):
        rounded[i] = misfit_tile(own, r1, r2, r3, obs, i).T.astype(bf16)


def share_kernel(place, own, r1, r2, r3, obs, share):
    for h in range(2):
        tile = misfit_tile(own, r1, r2, r3, obs, 2 * axes(place, place[2])[1] + h)
        share[128 * h : 128 * h + 128, :] = pltpu.roll(tile, 32 * place[3], 1)


def bwd_kernel(rows, cols, cnt, place, *refs):
    jac, g0, g1, g2, g3, e0, e1, e2, e3, jbuf, mis, acc, sems = refs[8:]
    live = cnt[0]
    core = place[2]
    groups, arrive = tile_copies(jac, jbuf, sems, live)
    acc[...] = jnp.zeros(acc.shape, f32)
    for pieces, c in ((refs[0:4], core), (refs[4:8], 1 - core)):
        first, _, step, other = axes(place, c)
        for k in range(4):
            b = 4 * step * ((first + k) % 4) + 2 * c
            for e in range(4):
                for h in range(2):
                    mis[b + 4 * other * e + h] = pieces[k][2 * e + h]

    def group(g, carry):
        arrive(g)
        for v in range(GROUP):
            s = g * GROUP + v
            c = jnp.where(s < live, cols[s], CELL_TILES)
            acc[c] += jnp.dot(mis[rows[s]], jbuf[s], preferred_element_type=f32)
        return carry

    lax.fori_loop(0, groups, group, 0)
    for k, out in enumerate((e0, e1, e2, e3)):
        part = slice(32 * k, 32 * k + 32)
        edge = jnp.where(lanes((32, 128)) < 64, acc[0, part, :], acc[CELL_TILES - 1, part, :])
        out[...] = edge.astype(out.dtype)
    for k, out in enumerate((g0, g1, g2, g3)):
        for t in range(8):
            for q in range(4):
                out[t, 32 * q : 32 * q + 32, :] = acc[8 * q + t, 32 * k : 32 * k + 32, :].astype(out.dtype)


def edge_kernel(own, r1, r2, r3, edge):
    edge[...] = own[...] + r1[...].astype(f32) + r2[...].astype(f32) + r3[...].astype(f32)


def wave_update(own, r1, r2, r3, nxt, prv, state_in, state, ext, levels):
    for i in range(8):
        s = own[i] + r1[i].astype(f32) + r2[i].astype(f32) + r3[i].astype(f32)
        ext[64 + 128 * i : 192 + 128 * i, :] = s.T
    ln = lanes((64, 128))
    near = jnp.concatenate([prv[...], jnp.zeros((64, 128), f32), nxt[...]], axis=0).T
    ext[0:64, :] = jnp.where(ln < 32, near[64:, :], pltpu.roll(ext[1024:1088, :], 32, 1))
    ext[1088:1152, :] = jnp.where(ln >= 96, near[:64, :], pltpu.roll(ext[64:128, :], 96, 1))
    ext[1152:1160, :] = jnp.zeros((8, 128), f32)
    src = ext
    for level in range(LEVELS):
        count = [576, 288, 144, 72, 40][level]
        front = 64 >> (level + 1)
        n = SEG_ROWS[level]
        base = SEG_OFF[level]
        e0 = src[pl.ds(0, count, stride=2), :]
        o0 = src[pl.ds(1, count, stride=2), :]
        e1 = src[pl.ds(2, count, stride=2), :]
        o1 = src[pl.ds(3, count, stride=2), :]
        smooth = low_pass[0] * e0 + low_pass[1] * o0 + low_pass[2] * e1 + low_pass[3] * o1
        detail = high_pass[0] * e0 + high_pass[1] * o0 + high_pass[2] * e1 + high_pass[3] * o1
        lead = min(front, 8)
        part = detail[front - lead : front + n, :]
        moved = state_in[base + 8 - lead : base + 8 + n, :] - step_length * part
        state[base + 8 - lead : base + 8 + n, :] = moved - jnp.clip(moved, -threshold, threshold)
        if lead < 8:
            state[base : base + 8 - lead, :] = jnp.zeros((8 - lead, 128), f32)
        if level < LEVELS - 1:
            dst = levels[level]
            dst[0:count, :] = smooth
            dst[count:, :] = jnp.zeros((dst.shape[0] - count, 128), f32)
            src = dst
        else:
            base = SEG_OFF[5]
            part = smooth[front - lead : front + n, :]
            state[base + 8 - lead : base + 8 + n, :] = (
                state_in[base + 8 - lead : base + 8 + n, :] - step_length * part
            )
            state[base : base + 8 - lead, :] = jnp.zeros((8 - lead, 128), f32)


WAVE_BUFS = [pltpu.VMEM((1160, 128), f32)] + [
    pltpu.VMEM((rows, 128), f32) for rows in (584, 296, 152, 88)
]


def wave_kernel(
    own, r1, r2, r3, nxt, prv, state_in, state, model, ext, l0, l1, l2, l3, *bufs
):
    wave_update(own, r1, r2, r3, nxt, prv, state_in, state, ext, (l0, l1, l2, l3))
    synth_from(state, bufs, model)


def last_kernel(own, r1, r2, r3, nxt, prv, state_in, out, state, ext, l0, l1, l2, l3):
    wave_update(own, r1, r2, r3, nxt, prv, state_in, state, ext, (l0, l1, l2, l3))
    for g in range(6):
        n = SEG_ROWS[g]
        base = SEG_OFF[g]
        tile = state[base + 8 : base + 8 + n, :].T
        for q in range(4):
            out[:, COEF_OFF[g] + q * n : COEF_OFF[g] + (q + 1) * n] = tile[32 * q : 32 * q + 32, :]


def from_ahead(x, axis, by):
    n = lax.axis_size(axis)
    return lax.ppermute(x, axis, [(i, (i - by) % n) for i in range(n)])


def to_ahead(x, axis, by):
    n = lax.axis_size(axis)
    return lax.ppermute(x, axis, [(i, (i + by) % n) for i in range(n)])


def by_core(x, stage, by):
    pairs = []
    for i in range(4):
        for j in range(4):
            for c in range(2):
                to = (i, (j + by) % 4) if c == stage else ((i + by) % 4, j)
                pairs.append((8 * i + 2 * j + c, 8 * to[0] + 2 * to[1] + c))
    return lax.ppermute(x, MP, pairs)


MP = ("x", "z", "core")


def along(x, by):
    return lax.ppermute(x, MP, [(i, (i + by) % 32) for i in range(32)])


def body(coeffs_start, observed, jacobian_tiles, tile_rows, tile_cols, tile_count):
    jac = jacobian_tiles[0, 0]
    rows = tile_rows[0, 0]
    cols = tile_cols[0, 0]
    cnt = tile_count[0]
    n_slots = jac.shape[0]
    x, z, core, ray = (lax.axis_index(a) for a in ("x", "z", "core", "ray"))
    place = jnp.stack([x, z, core, ray]).astype(jnp.int32)
    tiles = sds((8, 128, 128), f32)
    tiles_b = sds((8, 128, 128), bf16)
    flat_b = sds((1024, 128), bf16)

    state, tails = call(
        init_kernel, [VM], [sds((STATE_ROWS, 128), f32), sds((48, 128), f32)]
    )(coeffs_start.T)
    obs_all = observed.reshape(4, 4, 2, 256, 128)
    obs_rows = lax.cond(
        core == 0,
        lambda a: lax.dynamic_slice(a, (0, z, 0, 0, 0), (4, 1, 1, 256, 128)).reshape(4, 256, 128),
        lambda a: lax.dynamic_slice(a, (x, 0, 1, 0, 0), (1, 4, 1, 256, 128)).reshape(4, 256, 128),
        obs_all,
    )
    (obs_t,) = call(obs_kernel, [SM, VM], [tiles])(place, obs_rows)
    recv = along(tails, 1)
    (model,) = call(early_kernel, [VM], [flat_b], SYNTH_BUFS)(state)
    state, fix = call(
        synth_kernel,
        [VM, VM],
        [sds((STATE_ROWS, 128), f32), sds((128, 128), bf16)],
        SYNTH_BUFS + [pltpu.VMEM((1024, 128), bf16)],
    )(state, recv)

    jac_scratch = pltpu.VMEM((n_slots, TILE, TILE), bf16)
    sems = pltpu.SemaphoreType.DMA((n_slots // CHUNK,))
    for sweep in range(ITERS):
        pieces = [model] + [from_ahead(model, "ray", k) for k in (1, 2, 3)]
        fixes = []
        if sweep == 0:
            fixes = [fix] + [from_ahead(fix, "ray", k) for k in (1, 2, 3)]
        keep, send = call(
            fwd_kernel if sweep else first_kernel,
            [SM] * 4 + [VM] * (4 + len(fixes)) + [ANY],
            [sds((32, 128, 128), f32), sds((32, 128, 128), bf16)],
            [jac_scratch, pltpu.VMEM((32, 128, 128), bf16), pltpu.VMEM((65, 128, 128), f32), sems],
        )(rows, cols, cnt, place, *fixes, *pieces, jac)
        got = to_ahead(send, "core", 1)
        own, s1, s2, s3 = call(
            split_kernel, [SM, VM, VM], [tiles, tiles_b, tiles_b, tiles_b]
        )(place, keep, got)
        r = [by_core(s, 0, k + 1) for k, s in enumerate((s1, s2, s3))]
        own, sent = call(gather_kernel, [VM] * 4, [tiles, tiles_b])(own, *r)
        r = [by_core(sent, 1, k) for k in (1, 2, 3)]
        (rounded,) = call(misfit_kernel, [VM] * 5, [tiles_b])(own, *r, obs_t)
        if sweep == ITERS - 1:
            (share,) = call(share_kernel, [SM] + [VM] * 5, [sds((256, 128), f32)])(
                place, own, *r, obs_t
            )
        mine = [rounded] + [by_core(rounded, 0, -k) for k in (1, 2, 3)]
        other = [to_ahead(m, "core", 1) for m in mine]
        edge, edge_b = sds((32, 128), f32), sds((32, 128), bf16)
        g0, g1, g2, g3, e0, e1, e2, e3 = call(
            bwd_kernel,
            [SM, SM, SM, SM] + [VM] * 8 + [ANY],
            [tiles, tiles_b, tiles_b, tiles_b, edge, edge_b, edge_b, edge_b],
            [jac_scratch, pltpu.VMEM((64, 128, 128), bf16), pltpu.VMEM((33, 128, 128), f32), sems],
        )(rows, cols, cnt, place, *mine, *other, jac)
        r = [to_ahead(e, "ray", k + 1) for k, e in enumerate((e1, e2, e3))]
        (near,) = call(edge_kernel, [VM] * 4, [edge])(e0, *r)
        nxt = along(near, -1)
        prv = along(near, 1)
        r = [to_ahead(g, "ray", k + 1) for k, g in enumerate((g1, g2, g3))]
        if sweep < ITERS - 1:
            state, model = call(
                wave_kernel, [VM] * 7, [sds((STATE_ROWS, 128), f32), flat_b], WAVE_BUFS + SYNTH_BUFS
            )(g0, *r, nxt, prv, state)
        else:
            (coeffs,) = call(
                last_kernel,
                [VM] * 7,
                [sds((32, 4096), f32)],
                [pltpu.VMEM((STATE_ROWS, 128), f32)] + WAVE_BUFS,
            )(g0, *r, nxt, prv, state)
    return (coeffs.T, share)


def solution(mesh):
    fine = Mesh(mesh.devices.reshape(4, 4, 4, 2), ("ray", "x", "z", "core"))
    placed = (
        P(MP, "ray"),
        P("ray", None),
        P("ray", MP, None, None, None),
        P("ray", MP, None),
        P("ray", MP, None),
        P("ray", MP),
    )
    return jax.shard_map(
        body,
        mesh=fine,
        in_specs=placed,
        out_specs=(P(MP, "ray"), P(("ray",) + MP, None)),
        check_vma=False,
    )
```

profile of v0, /device:TPU:0, one launch (start us, length us, event | category | flops | bytes accessed | tf_op | source)
XLA Modules:
  0.0 192.1 jit_solution(17077352210273607705)
XLA Ops:
  4.5 2.9 %collective-permute-start.5 = (bf16[1024,128]{1,0:T(8,128)(2,1)S(1)}, bf16[1024,128]{1,0:T(8,128)(2,1)S(1)}, u32[]{:S(2)}, u32[]{:S(2)}) collective-permute-start(bf16[1024,128]{1,0:T(8,128)(2,1)S(1)} %shard_map.79.refs_0_), channel_id=1, source_target_pairs={{0,64},{32,96},{64,0},{96,32},{1,65},{33,97},{65,1},{97,33},{2,66}... | collective-permute-start | bytes 786440 | tf_op jit(solution)/shard_map/ppermute | solution.py:318
  8.7 6.6 %collective-permute-done.recv = f32[48,128]{1,0:T(8,128)S(1)} collective-permute-done((f32[48,128]{1,0:T(8,128)S(1)}, f32[48,128]{1,0:T(8,128)S(1)}, u32[]{:S(2)}, u32[]{:S(2)}) %collective-permute-start) | collective-permute-done | bytes 24608 | tf_op jit(solution)/shard_map/ppermute | solution.py:340
  17.4 3.6 %collective-permute-done.3.f3 = bf16[128,128]{1,0:T(8,128)(2,1)S(1)} collective-permute-done((bf16[128,128]{1,0:T(8,128)(2,1)S(1)}, bf16[128,128]{1,0:T(8,128)(2,1)S(1)}, u32[]{:S(2)}, u32[]{:S(2)}) %collective-permute-start.3) | collective-permute-done | bytes 32800 | tf_op jit(solution)/shard_map/ppermute | solution.py:318
  24.9 4.0 %shard_map.80 = (f32[32,128,128]{2,1,0:T(8,128)S(1)}, bf16[32,128,128]{2,1,0:T(8,128)(2,1)S(1)}) custom-call(s32[384]{0:T(512)S(1)} %reduce.rows, s32[384]{0:T(512)S(1)} %reduce.1.cols, s32[1]{0:T(128)} %bitcast.13.cnt, s32[4]{0:T(128)S(1)} %pad_add_fusion.place, bf16[128,128]{1,0:T(8,128)(2,1)S(1)} %get-tuple-element.57.f0, ...), custom_call_target="tpu_custom_call" | custom-call | tf_op jit(solution)/shard_map/pallas_call | solution.py:382
  29.0 2.6 %collective-permute-done.7.recv = bf16[32,128,128]{2,1,0:T(8,128)(2,1)S(1)} collective-permute-done((bf16[32,128,128]{2,1,0:T(8,128)(2,1)S(1)}, bf16[32,128,128]{2,1,0:T(8,128)(2,1)S(1)}, u32[]{:S(2)}, u32[]{:S(2)}) %collective-permute-start.7) | collective-permute-done | bytes 1048608 | tf_op jit(solution)/shard_map/ppermute | solution.py:323
  33.4 4.1 %collective-permute-start.9 = (bf16[8,128,128]{2,1,0:T(8,128)(2,1)S(1)}, bf16[8,128,128]{2,1,0:T(8,128)(2,1)S(1)}, u32[]{:S(2)}, u32[]{:S(2)}) collective-permute-start(bf16[8,128,128]{2,1,0:T(8,128)(2,1)S(1)} %get-tuple-element.62), channel_id=1, source_target_pairs={{0,4},{1,17},{2,6},{3,19},{4,0},{5,21},{6,2},{7,23},{8,12},{9,25},... | collective-permute-start | bytes 786440 | tf_op jit(solution)/shard_map/ppermute | solution.py:333
  40.4 4.3 %collective-permute-done.9.r2 = bf16[8,128,128]{2,1,0:T(8,128)(2,1)S(1)} collective-permute-done((bf16[8,128,128]{2,1,0:T(8,128)(2,1)S(1)}, bf16[8,128,128]{2,1,0:T(8,128)(2,1)S(1)}, u32[]{:S(2)}, u32[]{:S(2)}) %collective-permute-start.9) | collective-permute-done | bytes 262176 | tf_op jit(solution)/shard_map/ppermute | solution.py:333
  51.2 2.5 %collective-permute-done.13.r3 = bf16[8,128,128]{2,1,0:T(8,128)(2,1)S(1)} collective-permute-done((bf16[8,128,128]{2,1,0:T(8,128)(2,1)S(1)}, bf16[8,128,128]{2,1,0:T(8,128)(2,1)S(1)}, u32[]{:S(2)}, u32[]{:S(2)}) %collective-permute-start.13) | collective-permute-done | bytes 262176 | tf_op jit(solution)/shard_map/ppermute | solution.py:333
  55.0 2.7 %collective-permute-done.11.r1 = bf16[8,128,128]{2,1,0:T(8,128)(2,1)S(1)} collective-permute-done((bf16[8,128,128]{2,1,0:T(8,128)(2,1)S(1)}, bf16[8,128,128]{2,1,0:T(8,128)(2,1)S(1)}, u32[]{:S(2)}, u32[]{:S(2)}) %collective-permute-start.11) | collective-permute-done | bytes 262176 | tf_op jit(solution)/shard_map/ppermute | solution.py:333
  65.5 3.3 %collective-permute-done.15.refs_2_ = bf16[8,128,128]{2,1,0:T(8,128)(2,1)S(1)} collective-permute-done((bf16[8,128,128]{2,1,0:T(8,128)(2,1)S(1)}, bf16[8,128,128]{2,1,0:T(8,128)(2,1)S(1)}, u32[]{:S(2)}, u32[]{:S(2)}) %collective-permute-start.15) | collective-permute-done | bytes 262176 | tf_op jit(solution)/shard_map/ppermute | solution.py:333
  70.7 4.0 %shard_map.85 = (f32[8,128,128]{2,1,0:T(8,128)S(1)}, bf16[8,128,128]{2,1,0:T(8,128)(2,1)S(1)}, bf16[8,128,128]{2,1,0:T(8,128)(2,1)S(1)}, bf16[8,128,128]{2,1,0:T...) custom-call(s32[384]{0:T(512)S(1)} %reduce.rows, ...), custom_call_target="tpu_custom_call" | custom-call | tf_op jit(solution)/shard_map/pallas_call | solution.py:403
  76.4 3.8 %collective-permute-start.22 = (bf16[8,128,128]{2,1,0:T(8,128)(2,1)S(1)}, bf16[8,128,128]{2,1,0:T(8,128)(2,1)S(1)}, u32[]{:S(2)}, u32[]{:S(2)}) collective-permute-start(bf16[8,128,128]{2,1,0:T(8,128)(2,1)S(1)} %get-tuple-element.68), channel_id=1, source_target_pairs={{0,64},{32,96},{64,0},{96,32},{1,65},{33,97},{65,1},{97,33},{2,66}... | collective-permute-start | bytes 786440 | tf_op jit(solution)/shard_map/ppermute | solution.py:323
  82.6 4.9 %collective-permute-done.24.r1 = bf16[32,128]{1,0:T(8,128)(2,1)S(1)} collective-permute-done((bf16[32,128]{1,0:T(8,128)(2,1)S(1)}, bf16[32,128]{1,0:T(8,128)(2,1)S(1)}, u32[]{:S(2)}, u32[]{:S(2)}) %collective-permute-start.24) | collective-permute-done | bytes 8224 | tf_op jit(solution)/shard_map/ppermute | solution.py:323
  87.6 4.1 %collective-permute-start.26 = (bf16[32,128]{1,0:T(8,128)(2,1)S(1)}, bf16[32,128]{1,0:T(8,128)(2,1)S(1)}, u32[]{:S(2)}, u32[]{:S(2)}) collective-permute-start(bf16[32,128]{1,0:T(8,128)(2,1)S(1)} %get-tuple-element.73), channel_id=1, source_target_pairs={{0,96},{32,0},{64,32},{96,64},{1,97},{33,1},{65,33},{97,65},{2,98}... | collective-permute-start | bytes 24584 | tf_op jit(solution)/shard_map/ppermute | solution.py:323
  93.0 5.1 %collective-permute-start.27 = (f32[32,128]{1,0:T(8,128)S(1)}, f32[32,128]{1,0:T(8,128)S(1)}, u32[]{:S(2)}, u32[]{:S(2)}) collective-permute-start(f32[32,128]{1,0:T(8,128)S(1)} %shard_map.86), channel_id=1, source_target_pairs={{0,31},{1,0},{2,1},{3,2},{4,3},{5,4},{6,5},{7,6},{8,7},{9,8},{10,9... | collective-permute-start | bytes 49160 | tf_op jit(solution)/shard_map/ppermute | solution.py:340
  102.2 3.6 %collective-permute-start.30 = (bf16[1024,128]{1,0:T(8,128)(2,1)S(1)}, bf16[1024,128]{1,0:T(8,128)(2,1)S(1)}, u32[]{:S(2)}, u32[]{:S(2)}) collective-permute-start(bf16[1024,128]{1,0:T(8,128)(2,1)S(1)} %get-tuple-element.75.p0), channel_id=1, source_target_pairs={{0,64},{32,96},{64,0},{96,32},{1,65},{33,97},{65,1},{97,33},{2,66}... | collective-permute-start | bytes 786440 | tf_op jit(solution)/shard_map/ppermute | solution.py:318
  106.9 4.0 %collective-permute-done.31.p3 = bf16[1024,128]{1,0:T(8,128)(2,1)S(1)} collective-permute-done((bf16[1024,128]{1,0:T(8,128)(2,1)S(1)}, bf16[1024,128]{1,0:T(8,128)(2,1)S(1)}, u32[]{:S(2)}, u32[]{:S(2)}) %collective-permute-start.31) | collective-permute-done | bytes 262176 | tf_op jit(solution)/shard_map/ppermute | solution.py:318
  110.8 6.8 %collective-permute-done.30.p2 = bf16[1024,128]{1,0:T(8,128)(2,1)S(1)} collective-permute-done((bf16[1024,128]{1,0:T(8,128)(2,1)S(1)}, bf16[1024,128]{1,0:T(8,128)(2,1)S(1)}, u32[]{:S(2)}, u32[]{:S(2)}) %collective-permute-start.30) | collective-permute-done | bytes 262176 | tf_op jit(solution)/shard_map/ppermute | solution.py:318
  117.6 4.0 %shard_map.88 = (f32[32,128,128]{2,1,0:T(8,128)S(1)}, bf16[32,128,128]{2,1,0:T(8,128)(2,1)S(1)}) custom-call(s32[384]{0:T(512)S(1)} %reduce.rows, s32[384]{0:T(512)S(1)} %reduce.1.cols, s32[1]{0:T(128)} %bitcast.15.cnt, s32[4]{0:T(128)S(1)} %pad_add_fusion.place, bf16[1024,128]{1,0:T(8,128)(2,1)S(1)} %get-tuple-element.75.p0, ...), custom_call_target="tpu_custom_call" | custom-call | tf_op jit(solution)/shard_map/pallas_call | solution.py:382
  121.7 2.6 %collective-permute-done.32.recv = bf16[32,128,128]{2,1,0:T(8,128)(2,1)S(1)} collective-permute-done((bf16[32,128,128]{2,1,0:T(8,128)(2,1)S(1)}, bf16[32,128,128]{2,1,0:T(8,128)(2,1)S(1)}, u32[]{:S(2)}, u32[]{:S(2)}) %collective-permute-start.32) | collective-permute-done | bytes 1048608 | tf_op jit(solution)/shard_map/ppermute | solution.py:323
  125.1 3.1 %collective-permute-start.34 = (bf16[8,128,128]{2,1,0:T(8,128)(2,1)S(1)}, bf16[8,128,128]{2,1,0:T(8,128)(2,1)S(1)}, u32[]{:S(2)}, u32[]{:S(2)}) collective-permute-start(bf16[8,128,128]{2,1,0:T(8,128)(2,1)S(1)} %get-tuple-element.80), channel_id=1, source_target_pairs={{0,4},{1,17},{2,6},{3,19},{4,0},{5,21},{6,2},{7,23},{8,12},{9,25},... | collective-permute-start | bytes 786440 | tf_op jit(solution)/shard_map/ppermute | solution.py:333
  130.1 5.4 %collective-permute-done.33.r1 = bf16[8,128,128]{2,1,0:T(8,128)(2,1)S(1)} collective-permute-done((bf16[8,128,128]{2,1,0:T(8,128)(2,1)S(1)}, bf16[8,128,128]{2,1,0:T(8,128)(2,1)S(1)}, u32[]{:S(2)}, u32[]{:S(2)}) %collective-permute-start.33) | collective-permute-done | bytes 262176 | tf_op jit(solution)/shard_map/ppermute | solution.py:333
  139.6 3.3 %collective-permute-done.38.r3 = bf16[8,128,128]{2,1,0:T(8,128)(2,1)S(1)} collective-permute-done((bf16[8,128,128]{2,1,0:T(8,128)(2,1)S(1)}, bf16[8,128,128]{2,1,0:T(8,128)(2,1)S(1)}, u32[]{:S(2)}, u32[]{:S(2)}) %collective-permute-start.38) | collective-permute-done | bytes 262176 | tf_op jit(solution)/shard_map/ppermute | solution.py:333
  145.2 2.7 %collective-permute-done.36.r1 = bf16[8,128,128]{2,1,0:T(8,128)(2,1)S(1)} collective-permute-done((bf16[8,128,128]{2,1,0:T(8,128)(2,1)S(1)}, bf16[8,128,128]{2,1,0:T(8,128)(2,1)S(1)}, u32[]{:S(2)}, u32[]{:S(2)}) %collective-permute-start.36) | collective-permute-done | bytes 262176 | tf_op jit(solution)/shard_map/ppermute | solution.py:333
  149.6 2.7 %collective-permute-start.40 = (bf16[8,128,128]{2,1,0:T(8,128)(2,1)S(1)}, bf16[8,128,128]{2,1,0:T(8,128)(2,1)S(1)}, u32[]{:S(2)}, u32[]{:S(2)}) collective-permute-start(bf16[8,128,128]{2,1,0:T(8,128)(2,1)S(1)} %shard_map.91.refs_0_), channel_id=1, source_target_pairs={{0,4},{1,17},{2,6},{3,19},{4,0},{5,21},{6,2},{7,23},{8,12},{9,25},... | collective-permute-start | bytes 786440 | tf_op jit(solution)/shard_map/ppermute | solution.py:333
  152.9 2.9 %collective-permute-done.41.refs_3_ = bf16[8,128,128]{2,1,0:T(8,128)(2,1)S(1)} collective-permute-done((bf16[8,128,128]{2,1,0:T(8,128)(2,1)S(1)}, bf16[8,128,128]{2,1,0:T(8,128)(2,1)S(1)}, u32[]{:S(2)}, u32[]{:S(2)}) %collective-permute-start.41) | collective-permute-done | bytes 262176 | tf_op jit(solution)/shard_map/ppermute | solution.py:333
  155.8 3.7 %collective-permute-done.40.refs_2_ = bf16[8,128,128]{2,1,0:T(8,128)(2,1)S(1)} collective-permute-done((bf16[8,128,128]{2,1,0:T(8,128)(2,1)S(1)}, bf16[8,128,128]{2,1,0:T(8,128)(2,1)S(1)}, u32[]{:S(2)}, u32[]{:S(2)}) %collective-permute-start.40) | collective-permute-done | bytes 262176 | tf_op jit(solution)/shard_map/ppermute | solution.py:333
  161.4 3.8 %shard_map.92 = (f32[8,128,128]{2,1,0:T(8,128)S(1)}, bf16[8,128,128]{2,1,0:T(8,128)(2,1)S(1)}, bf16[8,128,128]{2,1,0:T(8,128)(2,1)S(1)}, bf16[8,128,128]{2,1,0:T...) custom-call(s32[384]{0:T(512)S(1)} %reduce.rows, ...), custom_call_target="tpu_custom_call" | custom-call | tf_op jit(solution)/shard_map/pallas_call | solution.py:403
  167.4 3.7 %collective-permute-start.47 = (bf16[8,128,128]{2,1,0:T(8,128)(2,1)S(1)}, bf16[8,128,128]{2,1,0:T(8,128)(2,1)S(1)}, u32[]{:S(2)}, u32[]{:S(2)}) collective-permute-start(bf16[8,128,128]{2,1,0:T(8,128)(2,1)S(1)} %get-tuple-element.86), channel_id=1, source_target_pairs={{0,64},{32,96},{64,0},{96,32},{1,65},{33,97},{65,1},{97,33},{2,66}... | collective-permute-start | bytes 786440 | tf_op jit(solution)/shard_map/ppermute | solution.py:323
  173.2 4.9 %collective-permute-done.49.r1 = bf16[32,128]{1,0:T(8,128)(2,1)S(1)} collective-permute-done((bf16[32,128]{1,0:T(8,128)(2,1)S(1)}, bf16[32,128]{1,0:T(8,128)(2,1)S(1)}, u32[]{:S(2)}, u32[]{:S(2)}) %collective-permute-start.49) | collective-permute-done | bytes 8224 | tf_op jit(solution)/shard_map/ppermute | solution.py:323
  178.1 4.6 %collective-permute-start.51 = (bf16[32,128]{1,0:T(8,128)(2,1)S(1)}, bf16[32,128]{1,0:T(8,128)(2,1)S(1)}, u32[]{:S(2)}, u32[]{:S(2)}) collective-permute-start(bf16[32,128]{1,0:T(8,128)(2,1)S(1)} %get-tuple-element.91), channel_id=1, source_target_pairs={{0,96},{32,0},{64,32},{96,64},{1,97},{33,1},{65,33},{97,65},{2,98}... | collective-permute-start | bytes 24584 | tf_op jit(solution)/shard_map/ppermute | solution.py:323
  184.0 5.1 %collective-permute-start.52 = (f32[32,128]{1,0:T(8,128)S(1)}, f32[32,128]{1,0:T(8,128)S(1)}, u32[]{:S(2)}, u32[]{:S(2)}) collective-permute-start(f32[32,128]{1,0:T(8,128)S(1)} %shard_map.93), channel_id=1, source_target_pairs={{0,31},{1,0},{2,1},{3,2},{4,3},{5,4},{6,5},{7,6},{8,7},{9,8},{10,9... | collective-permute-start | bytes 49160 | tf_op jit(solution)/shard_map/ppermute | solution.py:340
  (102 shorter events, 66.3 us)
Async XLA Ops:
  2.7 22.2 %collective-permute-start.6 = (bf16[1024,128]{1,0:T(8,128)(2,1)S(1)}, bf16[1024,128]{1,0:T(8,128)(2,1)S(1)}, u32[]{:S(2)}, u32[]{:S(2)}) collective-permute-start(bf16[1024,128]{1,0:T(8,128)(2,1)S(1)} %shard_map.79.refs_0_), channel_id=1, source_target_pairs={{0,32},{32,64},{64,96},{96,0},{1,33},{33,65},{65,97},{97,1},{2,34}... | collective-permute-start | bytes 786440 | tf_op jit(solution)/shard_map/ppermute | solution.py:318
  4.5 20.4 %collective-permute-start.5 = (bf16[1024,128]{1,0:T(8,128)(2,1)S(1)}, bf16[1024,128]{1,0:T(8,128)(2,1)S(1)}, u32[]{:S(2)}, u32[]{:S(2)}) collective-permute-start(bf16[1024,128]{1,0:T(8,128)(2,1)S(1)} %shard_map.79.refs_0_), channel_id=1, source_target_pairs={{0,64},{32,96},{64,0},{96,32},{1,65},{33,97},{65,1},{97,33},{2,66}... | collective-permute-start | bytes 786440 | tf_op jit(solution)/shard_map/ppermute | solution.py:318
  7.4 17.5 %collective-permute-start.4 = (bf16[1024,128]{1,0:T(8,128)(2,1)S(1)}, bf16[1024,128]{1,0:T(8,128)(2,1)S(1)}, u32[]{:S(2)}, u32[]{:S(2)}) collective-permute-start(bf16[1024,128]{1,0:T(8,128)(2,1)S(1)} %shard_map.79.refs_0_), channel_id=1, source_target_pairs={{0,96},{32,0},{64,32},{96,64},{1,97},{33,1},{65,33},{97,65},{2,98}... | collective-permute-start | bytes 786440 | tf_op jit(solution)/shard_map/ppermute | solution.py:318
  32.4 8.1 %collective-permute-start.8 = (bf16[8,128,128]{2,1,0:T(8,128)(2,1)S(1)}, bf16[8,128,128]{2,1,0:T(8,128)(2,1)S(1)}, u32[]{:S(2)}, u32[]{:S(2)}) collective-permute-start(bf16[8,128,128]{2,1,0:T(8,128)(2,1)S(1)} %get-tuple-element.61), channel_id=1, source_target_pairs={{0,2},{1,9},{2,4},{3,11},{4,6},{5,13},{6,0},{7,15},{8,10},{9,17},{... | collective-permute-start | bytes 786440 | tf_op jit(solution)/shard_map/ppermute | solution.py:333
  33.4 11.3 %collective-permute-start.9 = (bf16[8,128,128]{2,1,0:T(8,128)(2,1)S(1)}, bf16[8,128,128]{2,1,0:T(8,128)(2,1)S(1)}, u32[]{:S(2)}, u32[]{:S(2)}) collective-permute-start(bf16[8,128,128]{2,1,0:T(8,128)(2,1)S(1)} %get-tuple-element.62), channel_id=1, source_target_pairs={{0,4},{1,17},{2,6},{3,19},{4,0},{5,21},{6,2},{7,23},{8,12},{9,25},... | collective-permute-start | bytes 786440 | tf_op jit(solution)/shard_map/ppermute | solution.py:333
  37.5 7.2 %collective-permute-start.10 = (bf16[8,128,128]{2,1,0:T(8,128)(2,1)S(1)}, bf16[8,128,128]{2,1,0:T(8,128)(2,1)S(1)}, u32[]{:S(2)}, u32[]{:S(2)}) collective-permute-start(bf16[8,128,128]{2,1,0:T(8,128)(2,1)S(1)} %get-tuple-element.63), channel_id=1, source_target_pairs={{0,6},{1,25},{2,0},{3,27},{4,2},{5,29},{6,4},{7,31},{8,14},{9,1},{... | collective-permute-start | bytes 786440 | tf_op jit(solution)/shard_map/ppermute | solution.py:333
  44.8 8.9 %collective-permute-start.13 = (bf16[8,128,128]{2,1,0:T(8,128)(2,1)S(1)}, bf16[8,128,128]{2,1,0:T(8,128)(2,1)S(1)}, u32[]{:S(2)}, u32[]{:S(2)}) collective-permute-start(bf16[8,128,128]{2,1,0:T(8,128)(2,1)S(1)} %get-tuple-element.65), channel_id=1, source_target_pairs={{0,24},{1,7},{2,26},{3,1},{4,28},{5,3},{6,30},{7,5},{8,0},{9,15},{... | collective-permute-start | bytes 786440 | tf_op jit(solution)/shard_map/ppermute | solution.py:333
  47.0 8.0 %collective-permute-start.12 = (bf16[8,128,128]{2,1,0:T(8,128)(2,1)S(1)}, bf16[8,128,128]{2,1,0:T(8,128)(2,1)S(1)}, u32[]{:S(2)}, u32[]{:S(2)}) collective-permute-start(bf16[8,128,128]{2,1,0:T(8,128)(2,1)S(1)} %get-tuple-element.65), channel_id=1, source_target_pairs={{0,16},{1,5},{2,18},{3,7},{4,20},{5,1},{6,22},{7,3},{8,24},{9,13},... | collective-permute-start | bytes 786440 | tf_op jit(solution)/shard_map/ppermute | solution.py:333
  48.0 9.7 %collective-permute-start.11 = (bf16[8,128,128]{2,1,0:T(8,128)(2,1)S(1)}, bf16[8,128,128]{2,1,0:T(8,128)(2,1)S(1)}, u32[]{:S(2)}, u32[]{:S(2)}) collective-permute-start(bf16[8,128,128]{2,1,0:T(8,128)(2,1)S(1)} %get-tuple-element.65), channel_id=1, source_target_pairs={{0,8},{1,3},{2,10},{3,5},{4,12},{5,7},{6,14},{7,1},{8,16},{9,11},{... | collective-permute-start | bytes 786440 | tf_op jit(solution)/shard_map/ppermute | solution.py:333
  57.9 7.7 %collective-permute-start.16 = (bf16[8,128,128]{2,1,0:T(8,128)(2,1)S(1)}, bf16[8,128,128]{2,1,0:T(8,128)(2,1)S(1)}, u32[]{:S(2)}, u32[]{:S(2)}) collective-permute-start(bf16[8,128,128]{2,1,0:T(8,128)(2,1)S(1)} %shard_map.84.refs_0_), channel_id=1, source_target_pairs={{0,2},{1,9},{2,4},{3,11},{4,6},{5,13},{6,0},{7,15},{8,10},{9,17},{... | collective-permute-start | bytes 786440 | tf_op jit(solution)/shard_map/ppermute | solution.py:333
  59.5 9.3 %collective-permute-start.15 = (bf16[8,128,128]{2,1,0:T(8,128)(2,1)S(1)}, bf16[8,128,128]{2,1,0:T(8,128)(2,1)S(1)}, u32[]{:S(2)}, u32[]{:S(2)}) collective-permute-start(bf16[8,128,128]{2,1,0:T(8,128)(2,1)S(1)} %shard_map.84.refs_0_), channel_id=1, source_target_pairs={{0,4},{1,17},{2,6},{3,19},{4,0},{5,21},{6,2},{7,23},{8,12},{9,25},... | collective-permute-start | bytes 786440 | tf_op jit(solution)/shard_map/ppermute | solution.py:333
  61.6 7.6 %collective-permute-start.14 = (bf16[8,128,128]{2,1,0:T(8,128)(2,1)S(1)}, bf16[8,128,128]{2,1,0:T(8,128)(2,1)S(1)}, u32[]{:S(2)}, u32[]{:S(2)}) collective-permute-start(bf16[8,128,128]{2,1,0:T(8,128)(2,1)S(1)} %shard_map.84.refs_0_), channel_id=1, source_target_pairs={{0,6},{1,25},{2,0},{3,27},{4,2},{5,29},{6,4},{7,31},{8,14},{9,1},{... | collective-permute-start | bytes 786440 | tf_op jit(solution)/shard_map/ppermute | solution.py:333
  74.8 24.8 %collective-permute-start.21 = (bf16[8,128,128]{2,1,0:T(8,128)(2,1)S(1)}, bf16[8,128,128]{2,1,0:T(8,128)(2,1)S(1)}, u32[]{:S(2)}, u32[]{:S(2)}) collective-permute-start(bf16[8,128,128]{2,1,0:T(8,128)(2,1)S(1)} %get-tuple-element.67), channel_id=1, source_target_pairs={{0,32},{32,64},{64,96},{96,0},{1,33},{33,65},{65,97},{97,1},{2,34}... | collective-permute-start | bytes 786440 | tf_op jit(solution)/shard_map/ppermute | solution.py:323
  76.4 23.1 %collective-permute-start.22 = (bf16[8,128,128]{2,1,0:T(8,128)(2,1)S(1)}, bf16[8,128,128]{2,1,0:T(8,128)(2,1)S(1)}, u32[]{:S(2)}, u32[]{:S(2)}) collective-permute-start(bf16[8,128,128]{2,1,0:T(8,128)(2,1)S(1)} %get-tuple-element.68), channel_id=1, source_target_pairs={{0,64},{32,96},{64,0},{96,32},{1,65},{33,97},{65,1},{97,33},{2,66}... | collective-permute-start | bytes 786440 | tf_op jit(solution)/shard_map/ppermute | solution.py:323
  80.2 19.4 %collective-permute-start.23 = (bf16[8,128,128]{2,1,0:T(8,128)(2,1)S(1)}, bf16[8,128,128]{2,1,0:T(8,128)(2,1)S(1)}, u32[]{:S(2)}, u32[]{:S(2)}) collective-permute-start(bf16[8,128,128]{2,1,0:T(8,128)(2,1)S(1)} %get-tuple-element.69), channel_id=1, source_target_pairs={{0,96},{32,0},{64,32},{96,64},{1,97},{33,1},{65,33},{97,65},{2,98}... | collective-permute-start | bytes 786440 | tf_op jit(solution)/shard_map/ppermute | solution.py:323
  82.2 9.4 %collective-permute-start.25 = (bf16[32,128]{1,0:T(8,128)(2,1)S(1)}, bf16[32,128]{1,0:T(8,128)(2,1)S(1)}, u32[]{:S(2)}, u32[]{:S(2)}) collective-permute-start(bf16[32,128]{1,0:T(8,128)(2,1)S(1)} %get-tuple-element.72), channel_id=1, source_target_pairs={{0,64},{32,96},{64,0},{96,32},{1,65},{33,97},{65,1},{97,33},{2,66}... | collective-permute-start | bytes 24584 | tf_op jit(solution)/shard_map/ppermute | solution.py:323
  100.6 10.2 %collective-permute-start.31 = (bf16[1024,128]{1,0:T(8,128)(2,1)S(1)}, bf16[1024,128]{1,0:T(8,128)(2,1)S(1)}, u32[]{:S(2)}, u32[]{:S(2)}) collective-permute-start(bf16[1024,128]{1,0:T(8,128)(2,1)S(1)} %get-tuple-element.75.p0), channel_id=1, source_target_pairs={{0,32},{32,64},{64,96},{96,0},{1,33},{33,65},{65,97},{97,1},{2,34}... | collective-permute-start | bytes 786440 | tf_op jit(solution)/shard_map/ppermute | solution.py:318
  102.2 15.5 %collective-permute-start.30 = (bf16[1024,128]{1,0:T(8,128)(2,1)S(1)}, bf16[1024,128]{1,0:T(8,128)(2,1)S(1)}, u32[]{:S(2)}, u32[]{:S(2)}) collective-permute-start(bf16[1024,128]{1,0:T(8,128)(2,1)S(1)} %get-tuple-element.75.p0), channel_id=1, source_target_pairs={{0,64},{32,96},{64,0},{96,32},{1,65},{33,97},{65,1},{97,33},{2,66}... | collective-permute-start | bytes 786440 | tf_op jit(solution)/shard_map/ppermute | solution.py:318
  105.7 11.9 %collective-permute-start.29 = (bf16[1024,128]{1,0:T(8,128)(2,1)S(1)}, bf16[1024,128]{1,0:T(8,128)(2,1)S(1)}, u32[]{:S(2)}, u32[]{:S(2)}) collective-permute-start(bf16[1024,128]{1,0:T(8,128)(2,1)S(1)} %get-tuple-element.75.p0), channel_id=1, source_target_pairs={{0,96},{32,0},{64,32},{96,64},{1,97},{33,1},{65,33},{97,65},{2,98}... | collective-permute-start | bytes 786440 | tf_op jit(solution)/shard_map/ppermute | solution.py:318
  125.1 10.5 %collective-permute-start.33 = (bf16[8,128,128]{2,1,0:T(8,128)(2,1)S(1)}, bf16[8,128,128]{2,1,0:T(8,128)(2,1)S(1)}, u32[]{:S(2)}, u32[]{:S(2)}) collective-permute-start(bf16[8,128,128]{2,1,0:T(8,128)(2,1)S(1)} %get-tuple-element.79), channel_id=1, source_target_pairs={{0,2},{1,9},{2,4},{3,11},{4,6},{5,13},{6,0},{7,15},{8,10},{9,17},{... | collective-permute-start | bytes 786440 | tf_op jit(solution)/shard_map/ppermute | solution.py:333
  125.1 10.4 %collective-permute-start.34 = (bf16[8,128,128]{2,1,0:T(8,128)(2,1)S(1)}, bf16[8,128,128]{2,1,0:T(8,128)(2,1)S(1)}, u32[]{:S(2)}, u32[]{:S(2)}) collective-permute-start(bf16[8,128,128]{2,1,0:T(8,128)(2,1)S(1)} %get-tuple-element.80), channel_id=1, source_target_pairs={{0,4},{1,17},{2,6},{3,19},{4,0},{5,21},{6,2},{7,23},{8,12},{9,25},... | collective-permute-start | bytes 786440 | tf_op jit(solution)/shard_map/ppermute | solution.py:333
  128.2 8.1 %collective-permute-start.35 = (bf16[8,128,128]{2,1,0:T(8,128)(2,1)S(1)}, bf16[8,128,128]{2,1,0:T(8,128)(2,1)S(1)}, u32[]{:S(2)}, u32[]{:S(2)}) collective-permute-start(bf16[8,128,128]{2,1,0:T(8,128)(2,1)S(1)} %get-tuple-element.81), channel_id=1, source_target_pairs={{0,6},{1,25},{2,0},{3,27},{4,2},{5,29},{6,4},{7,31},{8,14},{9,1},{... | collective-permute-start | bytes 786440 | tf_op jit(solution)/shard_map/ppermute | solution.py:333
  137.2 8.0 %collective-permute-start.37 = (bf16[8,128,128]{2,1,0:T(8,128)(2,1)S(1)}, bf16[8,128,128]{2,1,0:T(8,128)(2,1)S(1)}, u32[]{:S(2)}, u32[]{:S(2)}) collective-permute-start(bf16[8,128,128]{2,1,0:T(8,128)(2,1)S(1)} %get-tuple-element.83), channel_id=1, source_target_pairs={{0,16},{1,5},{2,18},{3,7},{4,20},{5,1},{6,22},{7,3},{8,24},{9,13},... | collective-permute-start | bytes 786440 | tf_op jit(solution)/shard_map/ppermute | solution.py:333
  138.3 9.6 %collective-permute-start.36 = (bf16[8,128,128]{2,1,0:T(8,128)(2,1)S(1)}, bf16[8,128,128]{2,1,0:T(8,128)(2,1)S(1)}, u32[]{:S(2)}, u32[]{:S(2)}) collective-permute-start(bf16[8,128,128]{2,1,0:T(8,128)(2,1)S(1)} %get-tuple-element.83), channel_id=1, source_target_pairs={{0,8},{1,3},{2,10},{3,5},{4,12},{5,7},{6,14},{7,1},{8,16},{9,11},{... | collective-permute-start | bytes 786440 | tf_op jit(solution)/shard_map/ppermute | solution.py:333
  148.2 7.7 %collective-permute-start.41 = (bf16[8,128,128]{2,1,0:T(8,128)(2,1)S(1)}, bf16[8,128,128]{2,1,0:T(8,128)(2,1)S(1)}, u32[]{:S(2)}, u32[]{:S(2)}) collective-permute-start(bf16[8,128,128]{2,1,0:T(8,128)(2,1)S(1)} %shard_map.91.refs_0_), channel_id=1, source_target_pairs={{0,2},{1,9},{2,4},{3,11},{4,6},{5,13},{6,0},{7,15},{8,10},{9,17},{... | collective-permute-start | bytes 786440 | tf_op jit(solution)/shard_map/ppermute | solution.py:333
  149.6 9.9 %collective-permute-start.40 = (bf16[8,128,128]{2,1,0:T(8,128)(2,1)S(1)}, bf16[8,128,128]{2,1,0:T(8,128)(2,1)S(1)}, u32[]{:S(2)}, u32[]{:S(2)}) collective-permute-start(bf16[8,128,128]{2,1,0:T(8,128)(2,1)S(1)} %shard_map.91.refs_0_), channel_id=1, source_target_pairs={{0,4},{1,17},{2,6},{3,19},{4,0},{5,21},{6,2},{7,23},{8,12},{9,25},... | collective-permute-start | bytes 786440 | tf_op jit(solution)/shard_map/ppermute | solution.py:333
  152.3 7.2 %collective-permute-start.39 = (bf16[8,128,128]{2,1,0:T(8,128)(2,1)S(1)}, bf16[8,128,128]{2,1,0:T(8,128)(2,1)S(1)}, u32[]{:S(2)}, u32[]{:S(2)}) collective-permute-start(bf16[8,128,128]{2,1,0:T(8,128)(2,1)S(1)} %shard_map.91.refs_0_), channel_id=1, source_target_pairs={{0,6},{1,25},{2,0},{3,27},{4,2},{5,29},{6,4},{7,31},{8,14},{9,1},{... | collective-permute-start | bytes 786440 | tf_op jit(solution)/shard_map/ppermute | solution.py:333
  152.9 7.1 %collective-permute-start.42 = (bf16[8,128,128]{2,1,0:T(8,128)(2,1)S(1)}, bf16[8,128,128]{2,1,0:T(8,128)(2,1)S(1)}, u32[]{:S(2)}, u32[]{:S(2)}) collective-permute-start(bf16[8,128,128]{2,1,0:T(8,128)(2,1)S(1)} %shard_map.91.refs_0_), channel_id=1, source_target_pairs={{0,1},{1,0},{2,3},{3,2},{4,5},{5,4},{6,7},{7,6},{8,9},{9,8},{10,11... | collective-permute-start | bytes 786440 | tf_op jit(solution)/shard_map/ppermute | solution.py:323
  165.2 25.3 %collective-permute-start.46 = (bf16[8,128,128]{2,1,0:T(8,128)(2,1)S(1)}, bf16[8,128,128]{2,1,0:T(8,128)(2,1)S(1)}, u32[]{:S(2)}, u32[]{:S(2)}) collective-permute-start(bf16[8,128,128]{2,1,0:T(8,128)(2,1)S(1)} %get-tuple-element.85), channel_id=1, source_target_pairs={{0,32},{32,64},{64,96},{96,0},{1,33},{33,65},{65,97},{97,1},{2,34}... | collective-permute-start | bytes 786440 | tf_op jit(solution)/shard_map/ppermute | solution.py:323
  167.4 23.1 %collective-permute-start.47 = (bf16[8,128,128]{2,1,0:T(8,128)(2,1)S(1)}, bf16[8,128,128]{2,1,0:T(8,128)(2,1)S(1)}, u32[]{:S(2)}, u32[]{:S(2)}) collective-permute-start(bf16[8,128,128]{2,1,0:T(8,128)(2,1)S(1)} %get-tuple-element.86), channel_id=1, source_target_pairs={{0,64},{32,96},{64,0},{96,32},{1,65},{33,97},{65,1},{97,33},{2,66}... | collective-permute-start | bytes 786440 | tf_op jit(solution)/shard_map/ppermute | solution.py:323
  171.2 19.4 %collective-permute-start.48 = (bf16[8,128,128]{2,1,0:T(8,128)(2,1)S(1)}, bf16[8,128,128]{2,1,0:T(8,128)(2,1)S(1)}, u32[]{:S(2)}, u32[]{:S(2)}) collective-permute-start(bf16[8,128,128]{2,1,0:T(8,128)(2,1)S(1)} %get-tuple-element.87), channel_id=1, source_target_pairs={{0,96},{32,0},{64,32},{96,64},{1,97},{33,1},{65,33},{97,65},{2,98}... | collective-permute-start | bytes 786440 | tf_op jit(solution)/shard_map/ppermute | solution.py:323
  173.2 9.4 %collective-permute-start.50 = (bf16[32,128]{1,0:T(8,128)(2,1)S(1)}, bf16[32,128]{1,0:T(8,128)(2,1)S(1)}, u32[]{:S(2)}, u32[]{:S(2)}) collective-permute-start(bf16[32,128]{1,0:T(8,128)(2,1)S(1)} %get-tuple-element.90), channel_id=1, source_target_pairs={{0,64},{32,96},{64,0},{96,32},{1,65},{33,97},{65,1},{97,33},{2,66}... | collective-permute-start | bytes 24584 | tf_op jit(solution)/shard_map/ppermute | solution.py:323
  (23 other events, 105.3 us)
where the time goes:
time: 193 us; the launch traced here: 192 us
  waiting for transfers between devices  83.3 us (43%)
  starting transfers between devices  79.6 us (41%)
  Pallas kernels  24.1 us (12%)
  local copies, waits for them, and re-layouts  2.11 us (1%)
    ppermute x18, waiting for transfers between devices, by_core(): return lax.ppermute(x, MP, pairs)  38.4 us
    ppermute x18, starting transfers between devices, by_core(): return lax.ppermute(x, MP, pairs)  30.4 us
    ppermute x22, starting transfers between devices, to_ahead(): return lax.ppermute(x, axis, [(i, (i + by) % n) for i in range(n)])  25.3 us
    ppermute x22, waiting for transfers between devices, to_ahead(): return lax.ppermute(x, axis, [(i, (i + by) % n) for i in range(n)])  20.7 us
    ppermute x9, waiting for transfers between devices, from_ahead(): return lax.ppermute(x, axis, [(i, (i - by) % n) for i in range(n)])  16.2 us
    ppermute x9, starting transfers between devices, from_ahead(): return lax.ppermute(x, axis, [(i, (i - by) % n) for i in range(n)])  13.8 us
    ppermute x5, starting transfers between devices, along(): return lax.ppermute(x, MP, [(i, (i + by) % 32) for i in range(32)])  10.1 us
    ppermute x5, waiting for transfers between devices, along(): return lax.ppermute(x, MP, [(i, (i + by) % 32) for i in range(32)])  8.14 us
  transfers between devices with their start and end apart: 54, of which 32 were waited for; matrix products, arithmetic and copies ran while one was open for 1% of the time, Pallas kernels for 1%

commit v1 on v0

--- a/solution.py
+++ b/solution.py
@@ -336,6 +336,13 @@
 MP = ("x", "z", "core")
 
 
+def three(xs, move):
+    out = []
+    for k in (1, 2, 3):
+        out.append(move(xs[k - 1], k))
+    return out
+
+
 def along(x, by):
     return lax.ppermute(x, MP, [(i, (i + by) % 32) for i in range(32)])
 
@@ -375,10 +382,12 @@
     jac_scratch = pltpu.VMEM((n_slots, TILE, TILE), bf16)
     sems = pltpu.SemaphoreType.DMA((n_slots // CHUNK,))
     for sweep in range(ITERS):
-        pieces = [model] + [from_ahead(model, "ray", k) for k in (1, 2, 3)]
+        pull = lambda a, k: from_ahead(a, "ray", k)
+        push = lambda a, k: to_ahead(a, "ray", k)
+        pieces = [model] + three([model] * 3, pull)
         fixes = []
         if sweep == 0:
-            fixes = [fix] + [from_ahead(fix, "ray", k) for k in (1, 2, 3)]
+            fixes = [fix] + three([fix] * 3, pull)
         keep, send = call(
             fwd_kernel if sweep else first_kernel,
             [SM] * 4 + [VM] * (4 + len(fixes)) + [ANY],
@@ -389,15 +398,15 @@
         own, s1, s2, s3 = call(
             split_kernel, [SM, VM, VM], [tiles, tiles_b, tiles_b, tiles_b]
         )(place, keep, got)
-        r = [by_core(s, 0, k + 1) for k, s in enumerate((s1, s2, s3))]
+        r = three((s1, s2, s3), lambda a, k: by_core(a, 0, k))
         own, sent = call(gather_kernel, [VM] * 4, [tiles, tiles_b])(own, *r)
-        r = [by_core(sent, 1, k) for k in (1, 2, 3)]
+        r = three([sent] * 3, lambda a, k: by_core(a, 1, k))
         (rounded,) = call(misfit_kernel, [VM] * 5, [tiles_b])(own, *r, obs_t)
         if sweep == ITERS - 1:
             (share,) = call(share_kernel, [SM] + [VM] * 5, [sds((256, 128), f32)])(
                 place, own, *r, obs_t
             )
-        mine = [rounded] + [by_core(rounded, 0, -k) for k in (1, 2, 3)]
+        mine = [rounded] + three([rounded] * 3, lambda a, k: by_core(a, 0, -k))
         other = [to_ahead(m, "core", 1) for m in mine]
         edge, edge_b = sds((32, 128), f32), sds((32, 128), bf16)
         g0, g1, g2, g3, e0, e1, e2, e3 = call(
@@ -406,11 +415,11 @@
             [tiles, tiles_b, tiles_b, tiles_b, edge, edge_b, edge_b, edge_b],
             [jac_scratch, pltpu.VMEM((64, 128, 128), bf16), pltpu.VMEM((33, 128, 128), f32), sems],
         )(rows, cols, cnt, place, *mine, *other, jac)
-        r = [to_ahead(e, "ray", k + 1) for k, e in enumerate((e1, e2, e3))]
+        r = three((e1, e2, e3), push)
         (near,) = call(edge_kernel, [VM] * 4, [edge])(e0, *r)
         nxt = along(near, -1)
-        prv = along(near, 1)
-        r = [to_ahead(g, "ray", k + 1) for k, g in enumerate((g1, g2, g3))]
+        prv = along(near, 1) if sweep < ITERS - 1 else near
+        r = three((g1, g2, g3), push)
         if sweep < ITERS - 1:
             state, model = call(
                 wave_kernel, [VM] * 7, [sds((STATE_ROWS, 128), f32), flat_b], WAVE_BUFS + SYNTH_BUFS

time: 193 us -> 190 us (0.984)
  starting transfers between devices: 79.6 us -> 75.8 us
    ppermute x5 -> x4, starting transfers between devices: 10.1 us -> 6.32 us  [along(): return lax.ppermute(x, MP, [(i, (i + by) % 32) for i in range(32)])]
    ppermute x5 -> x4, waiting for transfers between devices: 8.14 us -> 8.14 us  [along(): return lax.ppermute(x, MP, [(i, (i + by) % 32) for i in range(32)])]
  transfers between devices with their start and end apart: 54 -> 53, of which waited for: 32 -> 32; matrix products, arithmetic and copies ran while one was open for 1% -> 1% of each run, Pallas kernels for 1% -> 1%
where the time goes in v1:
time: 190 us; the launch traced here: 188 us
  waiting for transfers between devices  83.3 us (44%)
  starting transfers between devices  75.8 us (40%)
  Pallas kernels  24.1 us (13%)
  local copies, waits for them, and re-layouts  2.11 us (1%)
    ppermute x18, waiting for transfers between devices, by_core(): return lax.ppermute(x, MP, pairs)  38.4 us
    ppermute x18, starting transfers between devices, by_core(): return lax.ppermute(x, MP, pairs)  30.4 us
    ppermute x22, starting transfers between devices, to_ahead(): return lax.ppermute(x, axis, [(i, (i + by) % n) for i in range(n)])  25.3 us
    ppermute x22, waiting for transfers between devices, to_ahead(): return lax.ppermute(x, axis, [(i, (i + by) % n) for i in range(n)])  20.7 us
    ppermute x9, waiting for transfers between devices, from_ahead(): return lax.ppermute(x, axis, [(i, (i - by) % n) for i in range(n)])  16.2 us
    ppermute x9, starting transfers between devices, from_ahead(): return lax.ppermute(x, axis, [(i, (i - by) % n) for i in range(n)])  13.8 us
    ppermute x4, waiting for transfers between devices, along(): return lax.ppermute(x, MP, [(i, (i + by) % 32) for i in range(32)])  8.14 us
    pallas_call x2, Pallas kernels, body(): call(fwd_kernel if sweep else first_kernel, [SM] * 4 + [VM] * (4 + len(fi...  7.91 us
  transfers between devices with their start and end apart: 53, of which 32 were waited for; matrix products, arithmetic and copies ran while one was open for 1% of the time, Pallas kernels for 1%

profile of v1, /device:TPU:0, one launch (start us, length us, event | category | flops | bytes accessed | tf_op | source)
XLA Modules:
  0.0 188.2 jit_solution(16300006314463043167)
XLA Ops:
  4.5 2.9 %collective-permute-start.5 = (bf16[1024,128]{1,0:T(8,128)(2,1)S(1)}, bf16[1024,128]{1,0:T(8,128)(2,1)S(1)}, u32[]{:S(2)}, u32[]{:S(2)}) collective-permute-start(bf16[1024,128]{1,0:T(8,128)(2,1)S(1)} %shard_map.79.refs_0_), channel_id=1, source_target_pairs={{0,64},{32,96},{64,0},{96,32},{1,65},{33,97},{65,1},{97,33},{2,66}... | collective-permute-start | bytes 786440 | tf_op jit(solution)/shard_map/ppermute | solution.py:318
  8.7 6.6 %collective-permute-done.recv = f32[48,128]{1,0:T(8,128)S(1)} collective-permute-done((f32[48,128]{1,0:T(8,128)S(1)}, f32[48,128]{1,0:T(8,128)S(1)}, u32[]{:S(2)}, u32[]{:S(2)}) %collective-permute-start) | collective-permute-done | bytes 24608 | tf_op jit(solution)/shard_map/ppermute | solution.py:347
  17.4 3.6 %collective-permute-done.3.f3 = bf16[128,128]{1,0:T(8,128)(2,1)S(1)} collective-permute-done((bf16[128,128]{1,0:T(8,128)(2,1)S(1)}, bf16[128,128]{1,0:T(8,128)(2,1)S(1)}, u32[]{:S(2)}, u32[]{:S(2)}) %collective-permute-start.3) | collective-permute-done | bytes 32800 | tf_op jit(solution)/shard_map/ppermute | solution.py:318
  24.9 4.0 %shard_map.80 = (f32[32,128,128]{2,1,0:T(8,128)S(1)}, bf16[32,128,128]{2,1,0:T(8,128)(2,1)S(1)}) custom-call(s32[384]{0:T(512)S(1)} %reduce.rows, s32[384]{0:T(512)S(1)} %reduce.1.cols, s32[1]{0:T(128)} %bitcast.13.cnt, s32[4]{0:T(128)S(1)} %pad_add_fusion.place, bf16[128,128]{1,0:T(8,128)(2,1)S(1)} %get-tuple-element.57.f0, ...), custom_call_target="tpu_custom_call" | custom-call | tf_op jit(solution)/shard_map/pallas_call | solution.py:391
  29.0 2.6 %collective-permute-done.7.recv = bf16[32,128,128]{2,1,0:T(8,128)(2,1)S(1)} collective-permute-done((bf16[32,128,128]{2,1,0:T(8,128)(2,1)S(1)}, bf16[32,128,128]{2,1,0:T(8,128)(2,1)S(1)}, u32[]{:S(2)}, u32[]{:S(2)}) %collective-permute-start.7) | collective-permute-done | bytes 1048608 | tf_op jit(solution)/shard_map/ppermute | solution.py:323
  33.4 4.1 %collective-permute-start.9 = (bf16[8,128,128]{2,1,0:T(8,128)(2,1)S(1)}, bf16[8,128,128]{2,1,0:T(8,128)(2,1)S(1)}, u32[]{:S(2)}, u32[]{:S(2)}) collective-permute-start(bf16[8,128,128]{2,1,0:T(8,128)(2,1)S(1)} %get-tuple-element.62), channel_id=1, source_target_pairs={{0,4},{1,17},{2,6},{3,19},{4,0},{5,21},{6,2},{7,23},{8,12},{9,25},... | collective-permute-start | bytes 786440 | tf_op jit(solution)/shard_map/ppermute | solution.py:333
  40.4 4.3 %collective-permute-done.9.r2 = bf16[8,128,128]{2,1,0:T(8,128)(2,1)S(1)} collective-permute-done((bf16[8,128,128]{2,1,0:T(8,128)(2,1)S(1)}, bf16[8,128,128]{2,1,0:T(8,128)(2,1)S(1)}, u32[]{:S(2)}, u32[]{:S(2)}) %collective-permute-start.9) | collective-permute-done | bytes 262176 | tf_op jit(solution)/shard_map/ppermute | solution.py:333
  51.2 2.5 %collective-permute-done.13.r3 = bf16[8,128,128]{2,1,0:T(8,128)(2,1)S(1)} collective-permute-done((bf16[8,128,128]{2,1,0:T(8,128)(2,1)S(1)}, bf16[8,128,128]{2,1,0:T(8,128)(2,1)S(1)}, u32[]{:S(2)}, u32[]{:S(2)}) %collective-permute-start.13) | collective-permute-done | bytes 262176 | tf_op jit(solution)/shard_map/ppermute | solution.py:333
  55.0 2.7 %collective-permute-done.11.r1 = bf16[8,128,128]{2,1,0:T(8,128)(2,1)S(1)} collective-permute-done((bf16[8,128,128]{2,1,0:T(8,128)(2,1)S(1)}, bf16[8,128,128]{2,1,0:T(8,128)(2,1)S(1)}, u32[]{:S(2)}, u32[]{:S(2)}) %collective-permute-start.11) | collective-permute-done | bytes 262176 | tf_op jit(solution)/shard_map/ppermute | solution.py:333
  65.5 3.3 %collective-permute-done.15.refs_2_ = bf16[8,128,128]{2,1,0:T(8,128)(2,1)S(1)} collective-permute-done((bf16[8,128,128]{2,1,0:T(8,128)(2,1)S(1)}, bf16[8,128,128]{2,1,0:T(8,128)(2,1)S(1)}, u32[]{:S(2)}, u32[]{:S(2)}) %collective-permute-start.15) | collective-permute-done | bytes 262176 | tf_op jit(solution)/shard_map/ppermute | solution.py:333
  70.7 4.0 %shard_map.85 = (f32[8,128,128]{2,1,0:T(8,128)S(1)}, bf16[8,128,128]{2,1,0:T(8,128)(2,1)S(1)}, bf16[8,128,128]{2,1,0:T(8,128)(2,1)S(1)}, bf16[8,128,128]{2,1,0:T...) custom-call(s32[384]{0:T(512)S(1)} %reduce.rows, ...), custom_call_target="tpu_custom_call" | custom-call | tf_op jit(solution)/shard_map/pallas_call | solution.py:412
  76.4 3.8 %collective-permute-start.22 = (bf16[8,128,128]{2,1,0:T(8,128)(2,1)S(1)}, bf16[8,128,128]{2,1,0:T(8,128)(2,1)S(1)}, u32[]{:S(2)}, u32[]{:S(2)}) collective-permute-start(bf16[8,128,128]{2,1,0:T(8,128)(2,1)S(1)} %get-tuple-element.68), channel_id=1, source_target_pairs={{0,64},{32,96},{64,0},{96,32},{1,65},{33,97},{65,1},{97,33},{2,66}... | collective-permute-start | bytes 786440 | tf_op jit(solution)/shard_map/ppermute | solution.py:323
  82.6 4.9 %collective-permute-done.24.r1 = bf16[32,128]{1,0:T(8,128)(2,1)S(1)} collective-permute-done((bf16[32,128]{1,0:T(8,128)(2,1)S(1)}, bf16[32,128]{1,0:T(8,128)(2,1)S(1)}, u32[]{:S(2)}, u32[]{:S(2)}) %collective-permute-start.24) | collective-permute-done | bytes 8224 | tf_op jit(solution)/shard_map/ppermute | solution.py:323
  87.6 4.1 %collective-permute-start.26 = (bf16[32,128]{1,0:T(8,128)(2,1)S(1)}, bf16[32,128]{1,0:T(8,128)(2,1)S(1)}, u32[]{:S(2)}, u32[]{:S(2)}) collective-permute-start(bf16[32,128]{1,0:T(8,128)(2,1)S(1)} %get-tuple-element.73), channel_id=1, source_target_pairs={{0,96},{32,0},{64,32},{96,64},{1,97},{33,1},{65,33},{97,65},{2,98}... | collective-permute-start | bytes 24584 | tf_op jit(solution)/shard_map/ppermute | solution.py:323
  93.0 5.1 %collective-permute-start.27 = (f32[32,128]{1,0:T(8,128)S(1)}, f32[32,128]{1,0:T(8,128)S(1)}, u32[]{:S(2)}, u32[]{:S(2)}) collective-permute-start(f32[32,128]{1,0:T(8,128)S(1)} %shard_map.86), channel_id=1, source_target_pairs={{0,31},{1,0},{2,1},{3,2},{4,3},{5,4},{6,5},{7,6},{8,7},{9,8},{10,9... | collective-permute-start | bytes 49160 | tf_op jit(solution)/shard_map/ppermute | solution.py:347
  102.2 3.6 %collective-permute-start.30 = (bf16[1024,128]{1,0:T(8,128)(2,1)S(1)}, bf16[1024,128]{1,0:T(8,128)(2,1)S(1)}, u32[]{:S(2)}, u32[]{:S(2)}) collective-permute-start(bf16[1024,128]{1,0:T(8,128)(2,1)S(1)} %get-tuple-element.75.p0), channel_id=1, source_target_pairs={{0,64},{32,96},{64,0},{96,32},{1,65},{33,97},{65,1},{97,33},{2,66}... | collective-permute-start | bytes 786440 | tf_op jit(solution)/shard_map/ppermute | solution.py:318
  106.9 4.0 %collective-permute-done.31.p3 = bf16[1024,128]{1,0:T(8,128)(2,1)S(1)} collective-permute-done((bf16[1024,128]{1,0:T(8,128)(2,1)S(1)}, bf16[1024,128]{1,0:T(8,128)(2,1)S(1)}, u32[]{:S(2)}, u32[]{:S(2)}) %collective-permute-start.31) | collective-permute-done | bytes 262176 | tf_op jit(solution)/shard_map/ppermute | solution.py:318
  110.8 6.8 %collective-permute-done.30.p2 = bf16[1024,128]{1,0:T(8,128)(2,1)S(1)} collective-permute-done((bf16[1024,128]{1,0:T(8,128)(2,1)S(1)}, bf16[1024,128]{1,0:T(8,128)(2,1)S(1)}, u32[]{:S(2)}, u32[]{:S(2)}) %collective-permute-start.30) | collective-permute-done | bytes 262176 | tf_op jit(solution)/shard_map/ppermute | solution.py:318
  117.6 4.0 %shard_map.88 = (f32[32,128,128]{2,1,0:T(8,128)S(1)}, bf16[32,128,128]{2,1,0:T(8,128)(2,1)S(1)}) custom-call(s32[384]{0:T(512)S(1)} %reduce.rows, s32[384]{0:T(512)S(1)} %reduce.1.cols, s32[1]{0:T(128)} %bitcast.15.cnt, s32[4]{0:T(128)S(1)} %pad_add_fusion.place, bf16[1024,128]{1,0:T(8,128)(2,1)S(1)} %get-tuple-element.75.p0, ...), custom_call_target="tpu_custom_call" | custom-call | tf_op jit(solution)/shard_map/pallas_call | solution.py:391
  121.7 2.6 %collective-permute-done.32.recv = bf16[32,128,128]{2,1,0:T(8,128)(2,1)S(1)} collective-permute-done((bf16[32,128,128]{2,1,0:T(8,128)(2,1)S(1)}, bf16[32,128,128]{2,1,0:T(8,128)(2,1)S(1)}, u32[]{:S(2)}, u32[]{:S(2)}) %collective-permute-start.32) | collective-permute-done | bytes 1048608 | tf_op jit(solution)/shard_map/ppermute | solution.py:323
  125.1 3.1 %collective-permute-start.34 = (bf16[8,128,128]{2,1,0:T(8,128)(2,1)S(1)}, bf16[8,128,128]{2,1,0:T(8,128)(2,1)S(1)}, u32[]{:S(2)}, u32[]{:S(2)}) collective-permute-start(bf16[8,128,128]{2,1,0:T(8,128)(2,1)S(1)} %get-tuple-element.80), channel_id=1, source_target_pairs={{0,4},{1,17},{2,6},{3,19},{4,0},{5,21},{6,2},{7,23},{8,12},{9,25},... | collective-permute-start | bytes 786440 | tf_op jit(solution)/shard_map/ppermute | solution.py:333
  130.1 5.4 %collective-permute-done.33.r1 = bf16[8,128,128]{2,1,0:T(8,128)(2,1)S(1)} collective-permute-done((bf16[8,128,128]{2,1,0:T(8,128)(2,1)S(1)}, bf16[8,128,128]{2,1,0:T(8,128)(2,1)S(1)}, u32[]{:S(2)}, u32[]{:S(2)}) %collective-permute-start.33) | collective-permute-done | bytes 262176 | tf_op jit(solution)/shard_map/ppermute | solution.py:333
  139.6 3.3 %collective-permute-done.38.r3 = bf16[8,128,128]{2,1,0:T(8,128)(2,1)S(1)} collective-permute-done((bf16[8,128,128]{2,1,0:T(8,128)(2,1)S(1)}, bf16[8,128,128]{2,1,0:T(8,128)(2,1)S(1)}, u32[]{:S(2)}, u32[]{:S(2)}) %collective-permute-start.38) | collective-permute-done | bytes 262176 | tf_op jit(solution)/shard_map/ppermute | solution.py:333
  142.9 2.3 %collective-permute-done.37.r2 = bf16[8,128,128]{2,1,0:T(8,128)(2,1)S(1)} collective-permute-done((bf16[8,128,128]{2,1,0:T(8,128)(2,1)S(1)}, bf16[8,128,128]{2,1,0:T(8,128)(2,1)S(1)}, u32[]{:S(2)}, u32[]{:S(2)}) %collective-permute-start.37) | collective-permute-done | bytes 262176 | tf_op jit(solution)/shard_map/ppermute | solution.py:333
  145.2 2.7 %collective-permute-done.36.r1 = bf16[8,128,128]{2,1,0:T(8,128)(2,1)S(1)} collective-permute-done((bf16[8,128,128]{2,1,0:T(8,128)(2,1)S(1)}, bf16[8,128,128]{2,1,0:T(8,128)(2,1)S(1)}, u32[]{:S(2)}, u32[]{:S(2)}) %collective-permute-start.36) | collective-permute-done | bytes 262176 | tf_op jit(solution)/shard_map/ppermute | solution.py:333
  149.6 2.7 %collective-permute-start.40 = (bf16[8,128,128]{2,1,0:T(8,128)(2,1)S(1)}, bf16[8,128,128]{2,1,0:T(8,128)(2,1)S(1)}, u32[]{:S(2)}, u32[]{:S(2)}) collective-permute-start(bf16[8,128,128]{2,1,0:T(8,128)(2,1)S(1)} %shard_map.91.refs_0_), channel_id=1, source_target_pairs={{0,4},{1,17},{2,6},{3,19},{4,0},{5,21},{6,2},{7,23},{8,12},{9,25},... | collective-permute-start | bytes 786440 | tf_op jit(solution)/shard_map/ppermute | solution.py:333
  152.9 2.9 %collective-permute-done.41.refs_3_ = bf16[8,128,128]{2,1,0:T(8,128)(2,1)S(1)} collective-permute-done((bf16[8,128,128]{2,1,0:T(8,128)(2,1)S(1)}, bf16[8,128,128]{2,1,0:T(8,128)(2,1)S(1)}, u32[]{:S(2)}, u32[]{:S(2)}) %collective-permute-start.41) | collective-permute-done | bytes 262176 | tf_op jit(solution)/shard_map/ppermute | solution.py:333
  155.8 3.7 %collective-permute-done.40.refs_2_ = bf16[8,128,128]{2,1,0:T(8,128)(2,1)S(1)} collective-permute-done((bf16[8,128,128]{2,1,0:T(8,128)(2,1)S(1)}, bf16[8,128,128]{2,1,0:T(8,128)(2,1)S(1)}, u32[]{:S(2)}, u32[]{:S(2)}) %collective-permute-start.40) | collective-permute-done | bytes 262176 | tf_op jit(solution)/shard_map/ppermute | solution.py:333
  161.4 3.8 %shard_map.92 = (f32[8,128,128]{2,1,0:T(8,128)S(1)}, bf16[8,128,128]{2,1,0:T(8,128)(2,1)S(1)}, bf16[8,128,128]{2,1,0:T(8,128)(2,1)S(1)}, bf16[8,128,128]{2,1,0:T...) custom-call(s32[384]{0:T(512)S(1)} %reduce.rows, ...), custom_call_target="tpu_custom_call" | custom-call | tf_op jit(solution)/shard_map/pallas_call | solution.py:412
  167.4 3.7 %collective-permute-start.47 = (bf16[8,128,128]{2,1,0:T(8,128)(2,1)S(1)}, bf16[8,128,128]{2,1,0:T(8,128)(2,1)S(1)}, u32[]{:S(2)}, u32[]{:S(2)}) collective-permute-start(bf16[8,128,128]{2,1,0:T(8,128)(2,1)S(1)} %get-tuple-element.86), channel_id=1, source_target_pairs={{0,64},{32,96},{64,0},{96,32},{1,65},{33,97},{65,1},{97,33},{2,66}... | collective-permute-start | bytes 786440 | tf_op jit(solution)/shard_map/ppermute | solution.py:323
  173.2 4.9 %collective-permute-done.49.r1 = bf16[32,128]{1,0:T(8,128)(2,1)S(1)} collective-permute-done((bf16[32,128]{1,0:T(8,128)(2,1)S(1)}, bf16[32,128]{1,0:T(8,128)(2,1)S(1)}, u32[]{:S(2)}, u32[]{:S(2)}) %collective-permute-start.49) | collective-permute-done | bytes 8224 | tf_op jit(solution)/shard_map/ppermute | solution.py:323
  178.1 4.6 %collective-permute-start.51 = (bf16[32,128]{1,0:T(8,128)(2,1)S(1)}, bf16[32,128]{1,0:T(8,128)(2,1)S(1)}, u32[]{:S(2)}, u32[]{:S(2)}) collective-permute-start(bf16[32,128]{1,0:T(8,128)(2,1)S(1)} %get-tuple-element.91), channel_id=1, source_target_pairs={{0,96},{32,0},{64,32},{96,64},{1,97},{33,1},{65,33},{97,65},{2,98}... | collective-permute-start | bytes 24584 | tf_op jit(solution)/shard_map/ppermute | solution.py:323
  (100 shorter events, 65.3 us)
Async XLA Ops:
  2.7 22.2 %collective-permute-start.6 = (bf16[1024,128]{1,0:T(8,128)(2,1)S(1)}, bf16[1024,128]{1,0:T(8,128)(2,1)S(1)}, u32[]{:S(2)}, u32[]{:S(2)}) collective-permute-start(bf16[1024,128]{1,0:T(8,128)(2,1)S(1)} %shard_map.79.refs_0_), channel_id=1, source_target_pairs={{0,32},{32,64},{64,96},{96,0},{1,33},{33,65},{65,97},{97,1},{2,34}... | collective-permute-start | bytes 786440 | tf_op jit(solution)/shard_map/ppermute | solution.py:318
  4.5 20.4 %collective-permute-start.5 = (bf16[1024,128]{1,0:T(8,128)(2,1)S(1)}, bf16[1024,128]{1,0:T(8,128)(2,1)S(1)}, u32[]{:S(2)}, u32[]{:S(2)}) collective-permute-start(bf16[1024,128]{1,0:T(8,128)(2,1)S(1)} %shard_map.79.refs_0_), channel_id=1, source_target_pairs={{0,64},{32,96},{64,0},{96,32},{1,65},{33,97},{65,1},{97,33},{2,66}... | collective-permute-start | bytes 786440 | tf_op jit(solution)/shard_map/ppermute | solution.py:318
  7.4 17.5 %collective-permute-start.4 = (bf16[1024,128]{1,0:T(8,128)(2,1)S(1)}, bf16[1024,128]{1,0:T(8,128)(2,1)S(1)}, u32[]{:S(2)}, u32[]{:S(2)}) collective-permute-start(bf16[1024,128]{1,0:T(8,128)(2,1)S(1)} %shard_map.79.refs_0_), channel_id=1, source_target_pairs={{0,96},{32,0},{64,32},{96,64},{1,97},{33,1},{65,33},{97,65},{2,98}... | collective-permute-start | bytes 786440 | tf_op jit(solution)/shard_map/ppermute | solution.py:318
  32.4 8.1 %collective-permute-start.8 = (bf16[8,128,128]{2,1,0:T(8,128)(2,1)S(1)}, bf16[8,128,128]{2,1,0:T(8,128)(2,1)S(1)}, u32[]{:S(2)}, u32[]{:S(2)}) collective-permute-start(bf16[8,128,128]{2,1,0:T(8,128)(2,1)S(1)} %get-tuple-element.61), channel_id=1, source_target_pairs={{0,2},{1,9},{2,4},{3,11},{4,6},{5,13},{6,0},{7,15},{8,10},{9,17},{... | collective-permute-start | bytes 786440 | tf_op jit(solution)/shard_map/ppermute | solution.py:333
  33.4 11.3 %collective-permute-start.9 = (bf16[8,128,128]{2,1,0:T(8,128)(2,1)S(1)}, bf16[8,128,128]{2,1,0:T(8,128)(2,1)S(1)}, u32[]{:S(2)}, u32[]{:S(2)}) collective-permute-start(bf16[8,128,128]{2,1,0:T(8,128)(2,1)S(1)} %get-tuple-element.62), channel_id=1, source_target_pairs={{0,4},{1,17},{2,6},{3,19},{4,0},{5,21},{6,2},{7,23},{8,12},{9,25},... | collective-permute-start | bytes 786440 | tf_op jit(solution)/shard_map/ppermute | solution.py:333
  37.5 7.2 %collective-permute-start.10 = (bf16[8,128,128]{2,1,0:T(8,128)(2,1)S(1)}, bf16[8,128,128]{2,1,0:T(8,128)(2,1)S(1)}, u32[]{:S(2)}, u32[]{:S(2)}) collective-permute-start(bf16[8,128,128]{2,1,0:T(8,128)(2,1)S(1)} %get-tuple-element.63), channel_id=1, source_target_pairs={{0,6},{1,25},{2,0},{3,27},{4,2},{5,29},{6,4},{7,31},{8,14},{9,1},{... | collective-permute-start | bytes 786440 | tf_op jit(solution)/shard_map/ppermute | solution.py:333
  44.8 8.9 %collective-permute-start.13 = (bf16[8,128,128]{2,1,0:T(8,128)(2,1)S(1)}, bf16[8,128,128]{2,1,0:T(8,128)(2,1)S(1)}, u32[]{:S(2)}, u32[]{:S(2)}) collective-permute-start(bf16[8,128,128]{2,1,0:T(8,128)(2,1)S(1)} %get-tuple-element.65), channel_id=1, source_target_pairs={{0,24},{1,7},{2,26},{3,1},{4,28},{5,3},{6,30},{7,5},{8,0},{9,15},{... | collective-permute-start | bytes 786440 | tf_op jit(solution)/shard_map/ppermute | solution.py:333
  47.0 8.0 %collective-permute-start.12 = (bf16[8,128,128]{2,1,0:T(8,128)(2,1)S(1)}, bf16[8,128,128]{2,1,0:T(8,128)(2,1)S(1)}, u32[]{:S(2)}, u32[]{:S(2)}) collective-permute-start(bf16[8,128,128]{2,1,0:T(8,128)(2,1)S(1)} %get-tuple-element.65), channel_id=1, source_target_pairs={{0,16},{1,5},{2,18},{3,7},{4,20},{5,1},{6,22},{7,3},{8,24},{9,13},... | collective-permute-start | bytes 786440 | tf_op jit(solution)/shard_map/ppermute | solution.py:333
  48.0 9.7 %collective-permute-start.11 = (bf16[8,128,128]{2,1,0:T(8,128)(2,1)S(1)}, bf16[8,128,128]{2,1,0:T(8,128)(2,1)S(1)}, u32[]{:S(2)}, u32[]{:S(2)}) collective-permute-start(bf16[8,128,128]{2,1,0:T(8,128)(2,1)S(1)} %get-tuple-element.65), channel_id=1, source_target_pairs={{0,8},{1,3},{2,10},{3,5},{4,12},{5,7},{6,14},{7,1},{8,16},{9,11},{... | collective-permute-start | bytes 786440 | tf_op jit(solution)/shard_map/ppermute | solution.py:333
  57.9 7.7 %collective-permute-start.16 = (bf16[8,128,128]{2,1,0:T(8,128)(2,1)S(1)}, bf16[8,128,128]{2,1,0:T(8,128)(2,1)S(1)}, u32[]{:S(2)}, u32[]{:S(2)}) collective-permute-start(bf16[8,128,128]{2,1,0:T(8,128)(2,1)S(1)} %shard_map.84.refs_0_), channel_id=1, source_target_pairs={{0,2},{1,9},{2,4},{3,11},{4,6},{5,13},{6,0},{7,15},{8,10},{9,17},{... | collective-permute-start | bytes 786440 | tf_op jit(solution)/shard_map/ppermute | solution.py:333
  59.5 9.3 %collective-permute-start.15 = (bf16[8,128,128]{2,1,0:T(8,128)(2,1)S(1)}, bf16[8,128,128]{2,1,0:T(8,128)(2,1)S(1)}, u32[]{:S(2)}, u32[]{:S(2)}) collective-permute-start(bf16[8,128,128]{2,1,0:T(8,128)(2,1)S(1)} %shard_map.84.refs_0_), channel_id=1, source_target_pairs={{0,4},{1,17},{2,6},{3,19},{4,0},{5,21},{6,2},{7,23},{8,12},{9,25},... | collective-permute-start | bytes 786440 | tf_op jit(solution)/shard_map/ppermute | solution.py:333
  61.6 7.6 %collective-permute-start.14 = (bf16[8,128,128]{2,1,0:T(8,128)(2,1)S(1)}, bf16[8,128,128]{2,1,0:T(8,128)(2,1)S(1)}, u32[]{:S(2)}, u32[]{:S(2)}) collective-permute-start(bf16[8,128,128]{2,1,0:T(8,128)(2,1)S(1)} %shard_map.84.refs_0_), channel_id=1, source_target_pairs={{0,6},{1,25},{2,0},{3,27},{4,2},{5,29},{6,4},{7,31},{8,14},{9,1},{... | collective-permute-start | bytes 786440 | tf_op jit(solution)/shard_map/ppermute | solution.py:333
  74.8 24.8 %collective-permute-start.21 = (bf16[8,128,128]{2,1,0:T(8,128)(2,1)S(1)}, bf16[8,128,128]{2,1,0:T(8,128)(2,1)S(1)}, u32[]{:S(2)}, u32[]{:S(2)}) collective-permute-start(bf16[8,128,128]{2,1,0:T(8,128)(2,1)S(1)} %get-tuple-element.67), channel_id=1, source_target_pairs={{0,32},{32,64},{64,96},{96,0},{1,33},{33,65},{65,97},{97,1},{2,34}... | collective-permute-start | bytes 786440 | tf_op jit(solution)/shard_map/ppermute | solution.py:323
  76.4 23.1 %collective-permute-start.22 = (bf16[8,128,128]{2,1,0:T(8,128)(2,1)S(1)}, bf16[8,128,128]{2,1,0:T(8,128)(2,1)S(1)}, u32[]{:S(2)}, u32[]{:S(2)}) collective-permute-start(bf16[8,128,128]{2,1,0:T(8,128)(2,1)S(1)} %get-tuple-element.68), channel_id=1, source_target_pairs={{0,64},{32,96},{64,0},{96,32},{1,65},{33,97},{65,1},{97,33},{2,66}... | collective-permute-start | bytes 786440 | tf_op jit(solution)/shard_map/ppermute | solution.py:323
  80.2 19.4 %collective-permute-start.23 = (bf16[8,128,128]{2,1,0:T(8,128)(2,1)S(1)}, bf16[8,128,128]{2,1,0:T(8,128)(2,1)S(1)}, u32[]{:S(2)}, u32[]{:S(2)}) collective-permute-start(bf16[8,128,128]{2,1,0:T(8,128)(2,1)S(1)} %get-tuple-element.69), channel_id=1, source_target_pairs={{0,96},{32,0},{64,32},{96,64},{1,97},{33,1},{65,33},{97,65},{2,98}... | collective-permute-start | bytes 786440 | tf_op jit(solution)/shard_map/ppermute | solution.py:323
  82.2 9.4 %collective-permute-start.25 = (bf16[32,128]{1,0:T(8,128)(2,1)S(1)}, bf16[32,128]{1,0:T(8,128)(2,1)S(1)}, u32[]{:S(2)}, u32[]{:S(2)}) collective-permute-start(bf16[32,128]{1,0:T(8,128)(2,1)S(1)} %get-tuple-element.72), channel_id=1, source_target_pairs={{0,64},{32,96},{64,0},{96,32},{1,65},{33,97},{65,1},{97,33},{2,66}... | collective-permute-start | bytes 24584 | tf_op jit(solution)/shard_map/ppermute | solution.py:323
  100.6 10.2 %collective-permute-start.31 = (bf16[1024,128]{1,0:T(8,128)(2,1)S(1)}, bf16[1024,128]{1,0:T(8,128)(2,1)S(1)}, u32[]{:S(2)}, u32[]{:S(2)}) collective-permute-start(bf16[1024,128]{1,0:T(8,128)(2,1)S(1)} %get-tuple-element.75.p0), channel_id=1, source_target_pairs={{0,32},{32,64},{64,96},{96,0},{1,33},{33,65},{65,97},{97,1},{2,34}... | collective-permute-start | bytes 786440 | tf_op jit(solution)/shard_map/ppermute | solution.py:318
  102.2 15.5 %collective-permute-start.30 = (bf16[1024,128]{1,0:T(8,128)(2,1)S(1)}, bf16[1024,128]{1,0:T(8,128)(2,1)S(1)}, u32[]{:S(2)}, u32[]{:S(2)}) collective-permute-start(bf16[1024,128]{1,0:T(8,128)(2,1)S(1)} %get-tuple-element.75.p0), channel_id=1, source_target_pairs={{0,64},{32,96},{64,0},{96,32},{1,65},{33,97},{65,1},{97,33},{2,66}... | collective-permute-start | bytes 786440 | tf_op jit(solution)/shard_map/ppermute | solution.py:318
  105.7 11.9 %collective-permute-start.29 = (bf16[1024,128]{1,0:T(8,128)(2,1)S(1)}, bf16[1024,128]{1,0:T(8,128)(2,1)S(1)}, u32[]{:S(2)}, u32[]{:S(2)}) collective-permute-start(bf16[1024,128]{1,0:T(8,128)(2,1)S(1)} %get-tuple-element.75.p0), channel_id=1, source_target_pairs={{0,96},{32,0},{64,32},{96,64},{1,97},{33,1},{65,33},{97,65},{2,98}... | collective-permute-start | bytes 786440 | tf_op jit(solution)/shard_map/ppermute | solution.py:318
  125.1 10.5 %collective-permute-start.33 = (bf16[8,128,128]{2,1,0:T(8,128)(2,1)S(1)}, bf16[8,128,128]{2,1,0:T(8,128)(2,1)S(1)}, u32[]{:S(2)}, u32[]{:S(2)}) collective-permute-start(bf16[8,128,128]{2,1,0:T(8,128)(2,1)S(1)} %get-tuple-element.79), channel_id=1, source_target_pairs={{0,2},{1,9},{2,4},{3,11},{4,6},{5,13},{6,0},{7,15},{8,10},{9,17},{... | collective-permute-start | bytes 786440 | tf_op jit(solution)/shard_map/ppermute | solution.py:333
  125.1 10.4 %collective-permute-start.34 = (bf16[8,128,128]{2,1,0:T(8,128)(2,1)S(1)}, bf16[8,128,128]{2,1,0:T(8,128)(2,1)S(1)}, u32[]{:S(2)}, u32[]{:S(2)}) collective-permute-start(bf16[8,128,128]{2,1,0:T(8,128)(2,1)S(1)} %get-tuple-element.80), channel_id=1, source_target_pairs={{0,4},{1,17},{2,6},{3,19},{4,0},{5,21},{6,2},{7,23},{8,12},{9,25},... | collective-permute-start | bytes 786440 | tf_op jit(solution)/shard_map/ppermute | solution.py:333
  128.2 8.1 %collective-permute-start.35 = (bf16[8,128,128]{2,1,0:T(8,128)(2,1)S(1)}, bf16[8,128,128]{2,1,0:T(8,128)(2,1)S(1)}, u32[]{:S(2)}, u32[]{:S(2)}) collective-permute-start(bf16[8,128,128]{2,1,0:T(8,128)(2,1)S(1)} %get-tuple-element.81), channel_id=1, source_target_pairs={{0,6},{1,25},{2,0},{3,27},{4,2},{5,29},{6,4},{7,31},{8,14},{9,1},{... | collective-permute-start | bytes 786440 | tf_op jit(solution)/shard_map/ppermute | solution.py:333
  137.2 8.0 %collective-permute-start.37 = (bf16[8,128,128]{2,1,0:T(8,128)(2,1)S(1)}, bf16[8,128,128]{2,1,0:T(8,128)(2,1)S(1)}, u32[]{:S(2)}, u32[]{:S(2)}) collective-permute-start(bf16[8,128,128]{2,1,0:T(8,128)(2,1)S(1)} %get-tuple-element.83), channel_id=1, source_target_pairs={{0,16},{1,5},{2,18},{3,7},{4,20},{5,1},{6,22},{7,3},{8,24},{9,13},... | collective-permute-start | bytes 786440 | tf_op jit(solution)/shard_map/ppermute | solution.py:333
  138.3 9.6 %collective-permute-start.36 = (bf16[8,128,128]{2,1,0:T(8,128)(2,1)S(1)}, bf16[8,128,128]{2,1,0:T(8,128)(2,1)S(1)}, u32[]{:S(2)}, u32[]{:S(2)}) collective-permute-start(bf16[8,128,128]{2,1,0:T(8,128)(2,1)S(1)} %get-tuple-element.83), channel_id=1, source_target_pairs={{0,8},{1,3},{2,10},{3,5},{4,12},{5,7},{6,14},{7,1},{8,16},{9,11},{... | collective-permute-start | bytes 786440 | tf_op jit(solution)/shard_map/ppermute | solution.py:333
  148.2 7.7 %collective-permute-start.41 = (bf16[8,128,128]{2,1,0:T(8,128)(2,1)S(1)}, bf16[8,128,128]{2,1,0:T(8,128)(2,1)S(1)}, u32[]{:S(2)}, u32[]{:S(2)}) collective-permute-start(bf16[8,128,128]{2,1,0:T(8,128)(2,1)S(1)} %shard_map.91.refs_0_), channel_id=1, source_target_pairs={{0,2},{1,9},{2,4},{3,11},{4,6},{5,13},{6,0},{7,15},{8,10},{9,17},{... | collective-permute-start | bytes 786440 | tf_op jit(solution)/shard_map/ppermute | solution.py:333
  149.6 9.9 %collective-permute-start.40 = (bf16[8,128,128]{2,1,0:T(8,128)(2,1)S(1)}, bf16[8,128,128]{2,1,0:T(8,128)(2,1)S(1)}, u32[]{:S(2)}, u32[]{:S(2)}) collective-permute-start(bf16[8,128,128]{2,1,0:T(8,128)(2,1)S(1)} %shard_map.91.refs_0_), channel_id=1, source_target_pairs={{0,4},{1,17},{2,6},{3,19},{4,0},{5,21},{6,2},{7,23},{8,12},{9,25},... | collective-permute-start | bytes 786440 | tf_op jit(solution)/shard_map/ppermute | solution.py:333
  152.3 7.2 %collective-permute-start.39 = (bf16[8,128,128]{2,1,0:T(8,128)(2,1)S(1)}, bf16[8,128,128]{2,1,0:T(8,128)(2,1)S(1)}, u32[]{:S(2)}, u32[]{:S(2)}) collective-permute-start(bf16[8,128,128]{2,1,0:T(8,128)(2,1)S(1)} %shard_map.91.refs_0_), channel_id=1, source_target_pairs={{0,6},{1,25},{2,0},{3,27},{4,2},{5,29},{6,4},{7,31},{8,14},{9,1},{... | collective-permute-start | bytes 786440 | tf_op jit(solution)/shard_map/ppermute | solution.py:333
  152.9 7.1 %collective-permute-start.42 = (bf16[8,128,128]{2,1,0:T(8,128)(2,1)S(1)}, bf16[8,128,128]{2,1,0:T(8,128)(2,1)S(1)}, u32[]{:S(2)}, u32[]{:S(2)}) collective-permute-start(bf16[8,128,128]{2,1,0:T(8,128)(2,1)S(1)} %shard_map.91.refs_0_), channel_id=1, source_target_pairs={{0,1},{1,0},{2,3},{3,2},{4,5},{5,4},{6,7},{7,6},{8,9},{9,8},{10,11... | collective-permute-start | bytes 786440 | tf_op jit(solution)/shard_map/ppermute | solution.py:323
  165.2 21.4 %collective-permute-start.46 = (bf16[8,128,128]{2,1,0:T(8,128)(2,1)S(1)}, bf16[8,128,128]{2,1,0:T(8,128)(2,1)S(1)}, u32[]{:S(2)}, u32[]{:S(2)}) collective-permute-start(bf16[8,128,128]{2,1,0:T(8,128)(2,1)S(1)} %get-tuple-element.85), channel_id=1, source_target_pairs={{0,32},{32,64},{64,96},{96,0},{1,33},{33,65},{65,97},{97,1},{2,34}... | collective-permute-start | bytes 786440 | tf_op jit(solution)/shard_map/ppermute | solution.py:323
  167.4 19.3 %collective-permute-start.47 = (bf16[8,128,128]{2,1,0:T(8,128)(2,1)S(1)}, bf16[8,128,128]{2,1,0:T(8,128)(2,1)S(1)}, u32[]{:S(2)}, u32[]{:S(2)}) collective-permute-start(bf16[8,128,128]{2,1,0:T(8,128)(2,1)S(1)} %get-tuple-element.86), channel_id=1, source_target_pairs={{0,64},{32,96},{64,0},{96,32},{1,65},{33,97},{65,1},{97,33},{2,66}... | collective-permute-start | bytes 786440 | tf_op jit(solution)/shard_map/ppermute | solution.py:323
  171.2 15.5 %collective-permute-start.48 = (bf16[8,128,128]{2,1,0:T(8,128)(2,1)S(1)}, bf16[8,128,128]{2,1,0:T(8,128)(2,1)S(1)}, u32[]{:S(2)}, u32[]{:S(2)}) collective-permute-start(bf16[8,128,128]{2,1,0:T(8,128)(2,1)S(1)} %get-tuple-element.87), channel_id=1, source_target_pairs={{0,96},{32,0},{64,32},{96,64},{1,97},{33,1},{65,33},{97,65},{2,98}... | collective-permute-start | bytes 786440 | tf_op jit(solution)/shard_map/ppermute | solution.py:323
  173.2 9.4 %collective-permute-start.50 = (bf16[32,128]{1,0:T(8,128)(2,1)S(1)}, bf16[32,128]{1,0:T(8,128)(2,1)S(1)}, u32[]{:S(2)}, u32[]{:S(2)}) collective-permute-start(bf16[32,128]{1,0:T(8,128)(2,1)S(1)} %get-tuple-element.90), channel_id=1, source_target_pairs={{0,64},{32,96},{64,0},{96,32},{1,65},{33,97},{65,1},{97,33},{2,66}... | collective-permute-start | bytes 24584 | tf_op jit(solution)/shard_map/ppermute | solution.py:323
  (22 other events, 95.0 us)

commit v2 on v1

--- a/solution.py
+++ b/solution.py
@@ -148,11 +148,9 @@
 
 
 def fwd_kernel(
-    rows, cols, cnt, place, p0, p1, p2, p3, jac, keep, send, jbuf, model, acc, sems, fixes=None
+    rows, cols, cnt, place, p0, p1, p2, p3, jac, acc, t0, t1, t2, t3, jbuf, model, sems, fixes=None
 ):
-    live = cnt[0]
-    core = place[2]
-    groups, arrive = tile_copies(jac, jbuf, sems, live)
+    groups, arrive = tile_copies(jac, jbuf, sems, cnt[0])
     acc[...] = jnp.zeros(acc.shape, f32)
     for c in range(CELL_TILES):
         q, t = c // 8, c % 8
@@ -165,24 +163,27 @@
         arrive(g)
         for v in range(GROUP):
             s = g * GROUP + v
-            r = jnp.where(s < live, rows[s], ROW_BLOCKS)
-            acc[r] += jnp.dot(jbuf[s], model[cols[s]], preferred_element_type=f32)
+            acc[rows[s]] += jnp.dot(jbuf[s], model[cols[s]], preferred_element_type=f32)
         return carry
 
     lax.fori_loop(0, groups, group, 0)
-    for xz in range(16):
-        for h in range(2):
-            keep[2 * xz + h] = acc[4 * xz + 2 * core + h]
-            send[2 * xz + h] = acc[4 * xz + 2 * (1 - core) + h].astype(bf16)
-
-
-def split_kernel(place, keep, recv, own, s1, s2, s3):
-    first, _, step, other = axes(place, place[2])
-    for k, out in enumerate((own, s1, s2, s3)):
+    first, _, step, other = axes(place, 1 - place[2])
+    for k, out in enumerate((t0, t1, t2, t3)):
+        for e in range(4):
+            for h in range(2):
+                b = ROW_BLOCKS // 2 + 2 * (step * ((first + k) % 4) + other * e) + h
+                out[2 * e + h] = acc[b].astype(bf16)
+
+
+def split_kernel(k):
+    def kernel(place, acc, recv, out):
+        first, _, step, other = axes(place, place[2])
         for e in range(4):
             for h in range(2):
                 b = 2 * (step * ((first + k) % 4) + other * e) + h
-                out[2 * e + h] = (keep[b] + recv[b].astype(f32)).astype(out.dtype)
+                out[2 * e + h] = (acc[b] + recv[2 * e + h].astype(f32)).astype(out.dtype)
+
+    return kernel
 
 
 def gather_kernel(own, r1, r2, r3, total, sent):
@@ -231,8 +232,7 @@
         arrive(g)
         for v in range(GROUP):
             s = g * GROUP + v
-            c = jnp.where(s < live, cols[s], CELL_TILES)
-            acc[c] += jnp.dot(mis[rows[s]], jbuf[s], preferred_element_type=f32)
+            acc[cols[s]] += jnp.dot(mis[rows[s]], jbuf[s], preferred_element_type=f32)
         return carry
 
     lax.fori_loop(0, groups, group, 0)
@@ -353,8 +353,12 @@
     cols = tile_cols[0, 0]
     cnt = tile_count[0]
     n_slots = jac.shape[0]
+    live = jnp.arange(n_slots, dtype=jnp.int32) < cnt[0]
     x, z, core, ray = (lax.axis_index(a) for a in ("x", "z", "core", "ray"))
     place = jnp.stack([x, z, core, ray]).astype(jnp.int32)
+    fwd_rows = rows // 4 * 2 + rows % 2 + ROW_BLOCKS // 2 * (rows // 2 % 2 != core)
+    fwd_rows = jnp.where(live, fwd_rows, ROW_BLOCKS)
+    bwd_cols = jnp.where(live, cols, CELL_TILES)
     tiles = sds((8, 128, 128), f32)
     tiles_b = sds((8, 128, 128), bf16)
     flat_b = sds((1024, 128), bf16)
@@ -388,17 +392,20 @@
         fixes = []
         if sweep == 0:
             fixes = [fix] + three([fix] * 3, pull)
-        keep, send = call(
+        acc, *sends = call(
             fwd_kernel if sweep else first_kernel,
             [SM] * 4 + [VM] * (4 + len(fixes)) + [ANY],
-            [sds((32, 128, 128), f32), sds((32, 128, 128), bf16)],
-            [jac_scratch, pltpu.VMEM((32, 128, 128), bf16), pltpu.VMEM((65, 128, 128), f32), sems],
-        )(rows, cols, cnt, place, *fixes, *pieces, jac)
-        got = to_ahead(send, "core", 1)
-        own, s1, s2, s3 = call(
-            split_kernel, [SM, VM, VM], [tiles, tiles_b, tiles_b, tiles_b]
-        )(place, keep, got)
-        r = three((s1, s2, s3), lambda a, k: by_core(a, 0, k))
+            [sds((ROW_BLOCKS + 1, 128, 128), f32)] + [tiles_b] * 4,
+            [jac_scratch, pltpu.VMEM((32, 128, 128), bf16), sems],
+        )(fwd_rows, cols, cnt, place, *fixes, *pieces, jac)
+        parts = [None] * 4
+        for k in (2, 1, 3, 0):
+            got = to_ahead(sends[k], "core", 1)
+            (parts[k],) = call(
+                split_kernel(k), [SM, VM, VM], [tiles_b if k else tiles]
+            )(place, acc, got)
+        own = parts[0]
+        r = three(parts[1:], lambda a, k: by_core(a, 0, k))
         own, sent = call(gather_kernel, [VM] * 4, [tiles, tiles_b])(own, *r)
         r = three([sent] * 3, lambda a, k: by_core(a, 1, k))
         (rounded,) = call(misfit_kernel, [VM] * 5, [tiles_b])(own, *r, obs_t)
@@ -414,7 +421,7 @@
             [SM, SM, SM, SM] + [VM] * 8 + [ANY],
             [tiles, tiles_b, tiles_b, tiles_b, edge, edge_b, edge_b, edge_b],
             [jac_scratch, pltpu.VMEM((64, 128, 128), bf16), pltpu.VMEM((33, 128, 128), f32), sems],
-        )(rows, cols, cnt, place, *mine, *other, jac)
+        )(rows, bwd_cols, cnt, place, *mine, *other, jac)
         r = three((e1, e2, e3), push)
         (near,) = call(edge_kernel, [VM] * 4, [edge])(e0, *r)
         nxt = along(near, -1)

time: 190 us -> 191 us (level)
  starting transfers between devices: 75.8 us -> 63.8 us
  waiting for transfers between devices: 83.3 us -> 93 us
  Pallas kernels: 24.1 us -> 27.7 us
    ppermute x18, waiting for transfers between devices: 38.4 us -> 44.5 us  [by_core(): return lax.ppermute(x, MP, pairs)]
    ppermute x18, starting transfers between devices: 30.4 us -> 25.6 us  [by_core(): return lax.ppermute(x, MP, pairs)]
    ppermute x22 -> x28, starting transfers between devices: 25.3 us -> 21.4 us  [to_ahead(): return lax.ppermute(x, axis, [(i, (i + by) % n) for i in range(n)])]
    ppermute x4, starting transfers between devices: 6.32 us -> 2.52 us  [along(): return lax.ppermute(x, MP, [(i, (i + by) % 32) for i in range(32)])]
    pallas_call x2 -> x8, Pallas kernels: 1.45 us -> 4.78 us  [body(): call(split_kernel(k), [SM, VM, VM], [tiles_b if k else tiles])]
    ppermute x22 -> x28, waiting for transfers between devices: 20.7 us -> 23.6 us  [to_ahead(): return lax.ppermute(x, axis, [(i, (i + by) % n) for i in range(n)])]
  transfers between devices with their start and end apart: 53 -> 59, of which waited for: 32 -> 36; matrix products, arithmetic and copies ran while one was open for 1% -> 1% of each run, Pallas kernels for 1% -> 4%
where the time goes in v2:
time: 191 us; the launch traced here: 190 us
  waiting for transfers between devices  93 us (49%)
  starting transfers between devices  63.8 us (33%)
  Pallas kernels  27.7 us (15%)
  local copies, waits for them, and re-layouts  2.11 us (1%)
    ppermute x18, waiting for transfers between devices, by_core(): return lax.ppermute(x, MP, pairs)  44.5 us
    ppermute x18, starting transfers between devices, by_core(): return lax.ppermute(x, MP, pairs)  25.6 us
    ppermute x28, waiting for transfers between devices, to_ahead(): return lax.ppermute(x, axis, [(i, (i + by) % n) for i in range(n)])  23.6 us
    ppermute x28, starting transfers between devices, to_ahead(): return lax.ppermute(x, axis, [(i, (i + by) % n) for i in range(n)])  21.4 us
    ppermute x9, waiting for transfers between devices, from_ahead(): return lax.ppermute(x, axis, [(i, (i - by) % n) for i in range(n)])  17.6 us
    ppermute x9, starting transfers between devices, from_ahead(): return lax.ppermute(x, axis, [(i, (i - by) % n) for i in range(n)])  14.4 us
    pallas_call x2, Pallas kernels, body(): call(fwd_kernel if sweep else first_kernel, [SM] * 4 + [VM] * (4 + len(fi...  8.34 us
    pallas_call x2, Pallas kernels, body(): call(bwd_kernel, [SM, SM, SM, SM] + [VM] * 8 + [ANY], [tiles, tiles_b, ti...  7.67 us
  transfers between devices with their start and end apart: 59, of which 36 were waited for; matrix products, arithmetic and copies ran while one was open for 1% of the time, Pallas kernels for 4%

profile of v2, /device:TPU:0, one launch (start us, length us, event | category | flops | bytes accessed | tf_op | source)
XLA Modules:
  0.0 189.7 jit_solution(12899608644004621833)
XLA Ops:
  2.7 3.2 %collective-permute-start.4 = (bf16[1024,128]{1,0:T(8,128)(2,1)S(1)}, bf16[1024,128]{1,0:T(8,128)(2,1)S(1)}, u32[]{:S(2)}, u32[]{:S(2)}) collective-permute-start(bf16[1024,128]{1,0:T(8,128)(2,1)S(1)} %shard_map.79.refs_0_), channel_id=1, source_target_pairs={{0,96},{32,0},{64,32},{96,64},{1,97},{33,1},{65,33},{97,65},{2,98}... | collective-permute-start | bytes 786440 | tf_op jit(solution)/shard_map/ppermute | solution.py:318
  10.0 3.1 %collective-permute-start.1 = (bf16[128,128]{1,0:T(8,128)(2,1)S(1)}, bf16[128,128]{1,0:T(8,128)(2,1)S(1)}, u32[]{:S(2)}, u32[]{:S(2)}) collective-permute-start(bf16[128,128]{1,0:T(8,128)(2,1)S(1)} %get-tuple-element.55.f0), channel_id=1, source_target_pairs={{0,96},{32,0},{64,32},{96,64},{1,97},{33,1},{65,33},{97,65},{2,98}... | collective-permute-start | bytes 98312 | tf_op jit(solution)/shard_map/ppermute | solution.py:318
  13.9 4.6 %collective-permute-done.1.f1 = bf16[128,128]{1,0:T(8,128)(2,1)S(1)} collective-permute-done((bf16[128,128]{1,0:T(8,128)(2,1)S(1)}, bf16[128,128]{1,0:T(8,128)(2,1)S(1)}, u32[]{:S(2)}, u32[]{:S(2)}) %collective-permute-start.1) | collective-permute-done | bytes 32800 | tf_op jit(solution)/shard_map/ppermute | solution.py:318
  24.3 4.1 %shard_map.80 = (f32[65,128,128]{2,1,0:T(8,128)S(1)}, bf16[8,128,128]{2,1,0:T(8,128)(2,1)S(1)}, bf16[8,128,128]{2,1,0:T(8,128)(2,1)S(1)}, bf16[8,128,128]{2,1,0:T(8,128)(2,1)S(1)}, bf16[8,128,128]{2,1,0:T(8,128)(2,1)S(1)}) custom-call(s32[384]{0:T(512)S(1)} %fusion.4.rows, s32[384]{0:T(512)S(1)} %reduce.1.cols, s32[1]{0:T(128)} %bitcast.16.cnt, ...), custom_call_target="tpu_custom_call" | custom-call | tf_op jit(solution)/shard_map/pallas_call | solution.py:395
  31.1 4.5 %collective-permute-start.13 = (bf16[8,128,128]{2,1,0:T(8,128)(2,1)S(1)}, bf16[8,128,128]{2,1,0:T(8,128)(2,1)S(1)}, u32[]{:S(2)}, u32[]{:S(2)}) collective-permute-start(bf16[8,128,128]{2,1,0:T(8,128)(2,1)S(1)} %shard_map.84), channel_id=1, source_target_pairs={{0,6},{1,25},{2,0},{3,27},{4,2},{5,29},{6,4},{7,31},{8,14},{9,1},{... | collective-permute-start | bytes 786440 | tf_op jit(solution)/shard_map/ppermute | solution.py:333
  39.8 2.6 %collective-permute-done.13.r3 = bf16[8,128,128]{2,1,0:T(8,128)(2,1)S(1)} collective-permute-done((bf16[8,128,128]{2,1,0:T(8,128)(2,1)S(1)}, bf16[8,128,128]{2,1,0:T(8,128)(2,1)S(1)}, u32[]{:S(2)}, u32[]{:S(2)}) %collective-permute-start.13) | collective-permute-done | bytes 262176 | tf_op jit(solution)/shard_map/ppermute | solution.py:333
  44.3 2.7 %collective-permute-done.9.r1 = bf16[8,128,128]{2,1,0:T(8,128)(2,1)S(1)} collective-permute-done((bf16[8,128,128]{2,1,0:T(8,128)(2,1)S(1)}, bf16[8,128,128]{2,1,0:T(8,128)(2,1)S(1)}, u32[]{:S(2)}, u32[]{:S(2)}) %collective-permute-start.9) | collective-permute-done | bytes 262176 | tf_op jit(solution)/shard_map/ppermute | solution.py:333
  54.8 2.8 %collective-permute-done.15.r2 = bf16[8,128,128]{2,1,0:T(8,128)(2,1)S(1)} collective-permute-done((bf16[8,128,128]{2,1,0:T(8,128)(2,1)S(1)}, bf16[8,128,128]{2,1,0:T(8,128)(2,1)S(1)}, u32[]{:S(2)}, u32[]{:S(2)}) %collective-permute-start.15) | collective-permute-done | bytes 262176 | tf_op jit(solution)/shard_map/ppermute | solution.py:333
  61.0 4.3 %collective-permute-done.17.refs_1_ = bf16[8,128,128]{2,1,0:T(8,128)(2,1)S(1)} collective-permute-done((bf16[8,128,128]{2,1,0:T(8,128)(2,1)S(1)}, bf16[8,128,128]{2,1,0:T(8,128)(2,1)S(1)}, u32[]{:S(2)}, u32[]{:S(2)}) %collective-permute-start.17) | collective-permute-done | bytes 262176 | tf_op jit(solution)/shard_map/ppermute | solution.py:333
  67.4 2.7 %collective-permute-done.19.refs_3_ = bf16[8,128,128]{2,1,0:T(8,128)(2,1)S(1)} collective-permute-done((bf16[8,128,128]{2,1,0:T(8,128)(2,1)S(1)}, bf16[8,128,128]{2,1,0:T(8,128)(2,1)S(1)}, u32[]{:S(2)}, u32[]{:S(2)}) %collective-permute-start.19) | collective-permute-done | bytes 262176 | tf_op jit(solution)/shard_map/ppermute | solution.py:333
  71.6 3.8 %shard_map.88 = (f32[8,128,128]{2,1,0:T(8,128)S(1)}, bf16[8,128,128]{2,1,0:T(8,128)(2,1)S(1)}, bf16[8,128,128]{2,1,0:T(8,128)(2,1)S(1)}, bf16[8,128,128]{2,1,0:T...) custom-call(s32[384]{0:T(512)S(1)} %reduce.rows, ...), custom_call_target="tpu_custom_call" | custom-call | tf_op jit(solution)/shard_map/pallas_call | solution.py:419
  76.9 4.1 %collective-permute-start.25 = (bf16[8,128,128]{2,1,0:T(8,128)(2,1)S(1)}, bf16[8,128,128]{2,1,0:T(8,128)(2,1)S(1)}, u32[]{:S(2)}, u32[]{:S(2)}) collective-permute-start(bf16[8,128,128]{2,1,0:T(8,128)(2,1)S(1)} %get-tuple-element.65), channel_id=1, source_target_pairs={{0,64},{32,96},{64,0},{96,32},{1,65},{33,97},{65,1},{97,33},{2,66}... | collective-permute-start | bytes 786440 | tf_op jit(solution)/shard_map/ppermute | solution.py:323
  83.0 5.2 %collective-permute-done.27.r1 = bf16[32,128]{1,0:T(8,128)(2,1)S(1)} collective-permute-done((bf16[32,128]{1,0:T(8,128)(2,1)S(1)}, bf16[32,128]{1,0:T(8,128)(2,1)S(1)}, u32[]{:S(2)}, u32[]{:S(2)}) %collective-permute-start.27) | collective-permute-done | bytes 8224 | tf_op jit(solution)/shard_map/ppermute | solution.py:323
  88.2 4.2 %collective-permute-start.29 = (bf16[32,128]{1,0:T(8,128)(2,1)S(1)}, bf16[32,128]{1,0:T(8,128)(2,1)S(1)}, u32[]{:S(2)}, u32[]{:S(2)}) collective-permute-start(bf16[32,128]{1,0:T(8,128)(2,1)S(1)} %get-tuple-element.70), channel_id=1, source_target_pairs={{0,96},{32,0},{64,32},{96,64},{1,97},{33,1},{65,33},{97,65},{2,98}... | collective-permute-start | bytes 24584 | tf_op jit(solution)/shard_map/ppermute | solution.py:323
  93.8 2.4 %collective-permute-start.30 = (f32[32,128]{1,0:T(8,128)S(1)}, f32[32,128]{1,0:T(8,128)S(1)}, u32[]{:S(2)}, u32[]{:S(2)}) collective-permute-start(f32[32,128]{1,0:T(8,128)S(1)} %shard_map.89), channel_id=1, source_target_pairs={{0,31},{1,0},{2,1},{3,2},{4,3},{5,4},{6,5},{7,6},{8,7},{9,8},{10,9... | collective-permute-start | bytes 49160 | tf_op jit(solution)/shard_map/ppermute | solution.py:347
  97.7 5.0 %collective-permute-done.31.prv = f32[32,128]{1,0:T(8,128)S(1)} collective-permute-done((f32[32,128]{1,0:T(8,128)S(1)}, f32[32,128]{1,0:T(8,128)S(1)}, u32[]{:S(2)}, u32[]{:S(2)}) %collective-permute-start.31) | collective-permute-done | bytes 16416 | tf_op jit(solution)/shard_map/ppermute | solution.py:347
  103.8 3.3 %collective-permute-start.32 = (bf16[1024,128]{1,0:T(8,128)(2,1)S(1)}, bf16[1024,128]{1,0:T(8,128)(2,1)S(1)}, u32[]{:S(2)}, u32[]{:S(2)}) collective-permute-start(bf16[1024,128]{1,0:T(8,128)(2,1)S(1)} %get-tuple-element.72.p0), channel_id=1, source_target_pairs={{0,96},{32,0},{64,32},{96,64},{1,97},{33,1},{65,33},{97,65},{2,98}... | collective-permute-start | bytes 786440 | tf_op jit(solution)/shard_map/ppermute | solution.py:318
  108.1 5.7 %collective-permute-done.32.p1 = bf16[1024,128]{1,0:T(8,128)(2,1)S(1)} collective-permute-done((bf16[1024,128]{1,0:T(8,128)(2,1)S(1)}, bf16[1024,128]{1,0:T(8,128)(2,1)S(1)}, u32[]{:S(2)}, u32[]{:S(2)}) %collective-permute-start.32) | collective-permute-done | bytes 262176 | tf_op jit(solution)/shard_map/ppermute | solution.py:318
  115.1 2.4 %collective-permute-done.34.p3 = bf16[1024,128]{1,0:T(8,128)(2,1)S(1)} collective-permute-done((bf16[1024,128]{1,0:T(8,128)(2,1)S(1)}, bf16[1024,128]{1,0:T(8,128)(2,1)S(1)}, u32[]{:S(2)}, u32[]{:S(2)}) %collective-permute-start.34) | collective-permute-done | bytes 262176 | tf_op jit(solution)/shard_map/ppermute | solution.py:318
  117.6 4.2 %shard_map.91 = (f32[65,128,128]{2,1,0:T(8,128)S(1)}, bf16[8,128,128]{2,1,0:T(8,128)(2,1)S(1)}, bf16[8,128,128]{2,1,0:T(8,128)(2,1)S(1)}, bf16[8,128,128]{2,1,0:T(8,128)(2,1)S(1)}, bf16[8,128,128]{2,1,0:T(8,128)(2,1)S(1)}) custom-call(s32[384]{0:T(512)S(1)} %fusion.4.rows, s32[384]{0:T(512)S(1)} %reduce.1.cols, s32[1]{0:T(128)} %bitcast.18.cnt, ...), custom_call_target="tpu_custom_call" | custom-call | tf_op jit(solution)/shard_map/pallas_call | solution.py:395
  124.0 2.9 %collective-permute-start.41 = (bf16[8,128,128]{2,1,0:T(8,128)(2,1)S(1)}, bf16[8,128,128]{2,1,0:T(8,128)(2,1)S(1)}, u32[]{:S(2)}, u32[]{:S(2)}) collective-permute-start(bf16[8,128,128]{2,1,0:T(8,128)(2,1)S(1)} %shard_map.95), channel_id=1, source_target_pairs={{0,6},{1,25},{2,0},{3,27},{4,2},{5,29},{6,4},{7,31},{8,14},{9,1},{... | collective-permute-start | bytes 786440 | tf_op jit(solution)/shard_map/ppermute | solution.py:333
  129.8 3.9 %collective-permute-done.41.r3 = bf16[8,128,128]{2,1,0:T(8,128)(2,1)S(1)} collective-permute-done((bf16[8,128,128]{2,1,0:T(8,128)(2,1)S(1)}, bf16[8,128,128]{2,1,0:T(8,128)(2,1)S(1)}, u32[]{:S(2)}, u32[]{:S(2)}) %collective-permute-start.41) | collective-permute-done | bytes 262176 | tf_op jit(solution)/shard_map/ppermute | solution.py:333
  135.6 2.7 %collective-permute-done.37.r1 = bf16[8,128,128]{2,1,0:T(8,128)(2,1)S(1)} collective-permute-done((bf16[8,128,128]{2,1,0:T(8,128)(2,1)S(1)}, bf16[8,128,128]{2,1,0:T(8,128)(2,1)S(1)}, u32[]{:S(2)}, u32[]{:S(2)}) %collective-permute-start.37) | collective-permute-done | bytes 262176 | tf_op jit(solution)/shard_map/ppermute | solution.py:333
  138.4 2.4 %collective-permute-start.42 = (bf16[8,128,128]{2,1,0:T(8,128)(2,1)S(1)}, bf16[8,128,128]{2,1,0:T(8,128)(2,1)S(1)}, u32[]{:S(2)}, u32[]{:S(2)}) collective-permute-start(bf16[8,128,128]{2,1,0:T(8,128)(2,1)S(1)} %get-tuple-element.79), channel_id=1, source_target_pairs={{0,8},{1,3},{2,10},{3,5},{4,12},{5,7},{6,14},{7,1},{8,16},{9,11},{... | collective-permute-start | bytes 786440 | tf_op jit(solution)/shard_map/ppermute | solution.py:333
  143.6 2.5 %collective-permute-done.42.r1 = bf16[8,128,128]{2,1,0:T(8,128)(2,1)S(1)} collective-permute-done((bf16[8,128,128]{2,1,0:T(8,128)(2,1)S(1)}, bf16[8,128,128]{2,1,0:T(8,128)(2,1)S(1)}, u32[]{:S(2)}, u32[]{:S(2)}) %collective-permute-start.42) | collective-permute-done | bytes 262176 | tf_op jit(solution)/shard_map/ppermute | solution.py:333
  146.1 3.4 %collective-permute-done.43.r2 = bf16[8,128,128]{2,1,0:T(8,128)(2,1)S(1)} collective-permute-done((bf16[8,128,128]{2,1,0:T(8,128)(2,1)S(1)}, bf16[8,128,128]{2,1,0:T(8,128)(2,1)S(1)}, u32[]{:S(2)}, u32[]{:S(2)}) %collective-permute-start.43) | collective-permute-done | bytes 262176 | tf_op jit(solution)/shard_map/ppermute | solution.py:333
  152.0 4.3 %collective-permute-done.45.refs_1_ = bf16[8,128,128]{2,1,0:T(8,128)(2,1)S(1)} collective-permute-done((bf16[8,128,128]{2,1,0:T(8,128)(2,1)S(1)}, bf16[8,128,128]{2,1,0:T(8,128)(2,1)S(1)}, u32[]{:S(2)}, u32[]{:S(2)}) %collective-permute-start.45) | collective-permute-done | bytes 262176 | tf_op jit(solution)/shard_map/ppermute | solution.py:333
  158.6 2.7 %collective-permute-done.47.refs_3_ = bf16[8,128,128]{2,1,0:T(8,128)(2,1)S(1)} collective-permute-done((bf16[8,128,128]{2,1,0:T(8,128)(2,1)S(1)}, bf16[8,128,128]{2,1,0:T(8,128)(2,1)S(1)}, u32[]{:S(2)}, u32[]{:S(2)}) %collective-permute-start.47) | collective-permute-done | bytes 262176 | tf_op jit(solution)/shard_map/ppermute | solution.py:333
  162.8 3.8 %shard_map.98 = (f32[8,128,128]{2,1,0:T(8,128)S(1)}, bf16[8,128,128]{2,1,0:T(8,128)(2,1)S(1)}, bf16[8,128,128]{2,1,0:T(8,128)(2,1)S(1)}, bf16[8,128,128]{2,1,0:T...) custom-call(s32[384]{0:T(512)S(1)} %reduce.rows, ...), custom_call_target="tpu_custom_call" | custom-call | tf_op jit(solution)/shard_map/pallas_call | solution.py:419
  166.8 4.1 %collective-permute-start.53 = (bf16[8,128,128]{2,1,0:T(8,128)(2,1)S(1)}, bf16[8,128,128]{2,1,0:T(8,128)(2,1)S(1)}, u32[]{:S(2)}, u32[]{:S(2)}) collective-permute-start(bf16[8,128,128]{2,1,0:T(8,128)(2,1)S(1)} %get-tuple-element.82), channel_id=1, source_target_pairs={{0,64},{32,96},{64,0},{96,32},{1,65},{33,97},{65,1},{97,33},{2,66}... | collective-permute-start | bytes 786440 | tf_op jit(solution)/shard_map/ppermute | solution.py:323
  173.7 9.3 %collective-permute-done.55.r1 = bf16[32,128]{1,0:T(8,128)(2,1)S(1)} collective-permute-done((bf16[32,128]{1,0:T(8,128)(2,1)S(1)}, bf16[32,128]{1,0:T(8,128)(2,1)S(1)}, u32[]{:S(2)}, u32[]{:S(2)}) %collective-permute-start.55) | collective-permute-done | bytes 8224 | tf_op jit(solution)/shard_map/ppermute | solution.py:323
  182.9 3.6 %collective-permute-done.57.r3 = bf16[32,128]{1,0:T(8,128)(2,1)S(1)} collective-permute-done((bf16[32,128]{1,0:T(8,128)(2,1)S(1)}, bf16[32,128]{1,0:T(8,128)(2,1)S(1)}, u32[]{:S(2)}, u32[]{:S(2)}) %collective-permute-start.57) | collective-permute-done | bytes 8224 | tf_op jit(solution)/shard_map/ppermute | solution.py:323
  (120 shorter events, 68.3 us)
Async XLA Ops:
  2.7 21.6 %collective-permute-start.4 = (bf16[1024,128]{1,0:T(8,128)(2,1)S(1)}, bf16[1024,128]{1,0:T(8,128)(2,1)S(1)}, u32[]{:S(2)}, u32[]{:S(2)}) collective-permute-start(bf16[1024,128]{1,0:T(8,128)(2,1)S(1)} %shard_map.79.refs_0_), channel_id=1, source_target_pairs={{0,96},{32,0},{64,32},{96,64},{1,97},{33,1},{65,33},{97,65},{2,98}... | collective-permute-start | bytes 786440 | tf_op jit(solution)/shard_map/ppermute | solution.py:318
  5.9 18.4 %collective-permute-start.5 = (bf16[1024,128]{1,0:T(8,128)(2,1)S(1)}, bf16[1024,128]{1,0:T(8,128)(2,1)S(1)}, u32[]{:S(2)}, u32[]{:S(2)}) collective-permute-start(bf16[1024,128]{1,0:T(8,128)(2,1)S(1)} %shard_map.79.refs_0_), channel_id=1, source_target_pairs={{0,64},{32,96},{64,0},{96,32},{1,65},{33,97},{65,1},{97,33},{2,66}... | collective-permute-start | bytes 786440 | tf_op jit(solution)/shard_map/ppermute | solution.py:318
  6.6 17.8 %collective-permute-start.6 = (bf16[1024,128]{1,0:T(8,128)(2,1)S(1)}, bf16[1024,128]{1,0:T(8,128)(2,1)S(1)}, u32[]{:S(2)}, u32[]{:S(2)}) collective-permute-start(bf16[1024,128]{1,0:T(8,128)(2,1)S(1)} %shard_map.79.refs_0_), channel_id=1, source_target_pairs={{0,32},{32,64},{64,96},{96,0},{1,33},{33,65},{65,97},{97,1},{2,34}... | collective-permute-start | bytes 786440 | tf_op jit(solution)/shard_map/ppermute | solution.py:318
  10.0 8.4 %collective-permute-start.1 = (bf16[128,128]{1,0:T(8,128)(2,1)S(1)}, bf16[128,128]{1,0:T(8,128)(2,1)S(1)}, u32[]{:S(2)}, u32[]{:S(2)}) collective-permute-start(bf16[128,128]{1,0:T(8,128)(2,1)S(1)} %get-tuple-element.55.f0), channel_id=1, source_target_pairs={{0,96},{32,0},{64,32},{96,64},{1,97},{33,1},{65,33},{97,65},{2,98}... | collective-permute-start | bytes 98312 | tf_op jit(solution)/shard_map/ppermute | solution.py:318
  13.2 9.0 %collective-permute-start.2 = (bf16[128,128]{1,0:T(8,128)(2,1)S(1)}, bf16[128,128]{1,0:T(8,128)(2,1)S(1)}, u32[]{:S(2)}, u32[]{:S(2)}) collective-permute-start(bf16[128,128]{1,0:T(8,128)(2,1)S(1)} %get-tuple-element.55.f0), channel_id=1, source_target_pairs={{0,64},{32,96},{64,0},{96,32},{1,65},{33,97},{65,1},{97,33},{2,66}... | collective-permute-start | bytes 98312 | tf_op jit(solution)/shard_map/ppermute | solution.py:318
  29.9 9.3 %collective-permute-start.7 = (bf16[8,128,128]{2,1,0:T(8,128)(2,1)S(1)}, bf16[8,128,128]{2,1,0:T(8,128)(2,1)S(1)}, u32[]{:S(2)}, u32[]{:S(2)}) collective-permute-start(bf16[8,128,128]{2,1,0:T(8,128)(2,1)S(1)} %get-tuple-element.57), channel_id=1, source_target_pairs={{0,1},{1,0},{2,3},{3,2},{4,5},{5,4},{6,7},{7,6},{8,9},{9,8},{10,11... | collective-permute-start | bytes 786440 | tf_op jit(solution)/shard_map/ppermute | solution.py:323
  31.1 11.3 %collective-permute-start.13 = (bf16[8,128,128]{2,1,0:T(8,128)(2,1)S(1)}, bf16[8,128,128]{2,1,0:T(8,128)(2,1)S(1)}, u32[]{:S(2)}, u32[]{:S(2)}) collective-permute-start(bf16[8,128,128]{2,1,0:T(8,128)(2,1)S(1)} %shard_map.84), channel_id=1, source_target_pairs={{0,6},{1,25},{2,0},{3,27},{4,2},{5,29},{6,4},{7,31},{8,14},{9,1},{... | collective-permute-start | bytes 786440 | tf_op jit(solution)/shard_map/ppermute | solution.py:333
  36.3 8.1 %collective-permute-start.11 = (bf16[8,128,128]{2,1,0:T(8,128)(2,1)S(1)}, bf16[8,128,128]{2,1,0:T(8,128)(2,1)S(1)}, u32[]{:S(2)}, u32[]{:S(2)}) collective-permute-start(bf16[8,128,128]{2,1,0:T(8,128)(2,1)S(1)} %shard_map.83), channel_id=1, source_target_pairs={{0,4},{1,17},{2,6},{3,19},{4,0},{5,21},{6,2},{7,23},{8,12},{9,25},... | collective-permute-start | bytes 786440 | tf_op jit(solution)/shard_map/ppermute | solution.py:333
  37.7 9.3 %collective-permute-start.9 = (bf16[8,128,128]{2,1,0:T(8,128)(2,1)S(1)}, bf16[8,128,128]{2,1,0:T(8,128)(2,1)S(1)}, u32[]{:S(2)}, u32[]{:S(2)}) collective-permute-start(bf16[8,128,128]{2,1,0:T(8,128)(2,1)S(1)} %shard_map.82), channel_id=1, source_target_pairs={{0,2},{1,9},{2,4},{3,11},{4,6},{5,13},{6,0},{7,15},{8,10},{9,17},{... | collective-permute-start | bytes 786440 | tf_op jit(solution)/shard_map/ppermute | solution.py:333
  48.1 9.6 %collective-permute-start.15 = (bf16[8,128,128]{2,1,0:T(8,128)(2,1)S(1)}, bf16[8,128,128]{2,1,0:T(8,128)(2,1)S(1)}, u32[]{:S(2)}, u32[]{:S(2)}) collective-permute-start(bf16[8,128,128]{2,1,0:T(8,128)(2,1)S(1)} %get-tuple-element.62), channel_id=1, source_target_pairs={{0,16},{1,5},{2,18},{3,7},{4,20},{5,1},{6,22},{7,3},{8,24},{9,13},... | collective-permute-start | bytes 786440 | tf_op jit(solution)/shard_map/ppermute | solution.py:333
  50.4 8.3 %collective-permute-start.16 = (bf16[8,128,128]{2,1,0:T(8,128)(2,1)S(1)}, bf16[8,128,128]{2,1,0:T(8,128)(2,1)S(1)}, u32[]{:S(2)}, u32[]{:S(2)}) collective-permute-start(bf16[8,128,128]{2,1,0:T(8,128)(2,1)S(1)} %get-tuple-element.62), channel_id=1, source_target_pairs={{0,24},{1,7},{2,26},{3,1},{4,28},{5,3},{6,30},{7,5},{8,0},{9,15},{... | collective-permute-start | bytes 786440 | tf_op jit(solution)/shard_map/ppermute | solution.py:333
  59.4 8.0 %collective-permute-start.18 = (bf16[8,128,128]{2,1,0:T(8,128)(2,1)S(1)}, bf16[8,128,128]{2,1,0:T(8,128)(2,1)S(1)}, u32[]{:S(2)}, u32[]{:S(2)}) collective-permute-start(bf16[8,128,128]{2,1,0:T(8,128)(2,1)S(1)} %shard_map.87.refs_0_), channel_id=1, source_target_pairs={{0,4},{1,17},{2,6},{3,19},{4,0},{5,21},{6,2},{7,23},{8,12},{9,25},... | collective-permute-start | bytes 786440 | tf_op jit(solution)/shard_map/ppermute | solution.py:333
  60.1 10.0 %collective-permute-start.19 = (bf16[8,128,128]{2,1,0:T(8,128)(2,1)S(1)}, bf16[8,128,128]{2,1,0:T(8,128)(2,1)S(1)}, u32[]{:S(2)}, u32[]{:S(2)}) collective-permute-start(bf16[8,128,128]{2,1,0:T(8,128)(2,1)S(1)} %shard_map.87.refs_0_), channel_id=1, source_target_pairs={{0,2},{1,9},{2,4},{3,11},{4,6},{5,13},{6,0},{7,15},{8,10},{9,17},{... | collective-permute-start | bytes 786440 | tf_op jit(solution)/shard_map/ppermute | solution.py:333
  61.0 9.1 %collective-permute-start.20 = (bf16[8,128,128]{2,1,0:T(8,128)(2,1)S(1)}, bf16[8,128,128]{2,1,0:T(8,128)(2,1)S(1)}, u32[]{:S(2)}, u32[]{:S(2)}) collective-permute-start(bf16[8,128,128]{2,1,0:T(8,128)(2,1)S(1)} %shard_map.87.refs_0_), channel_id=1, source_target_pairs={{0,1},{1,0},{2,3},{3,2},{4,5},{5,4},{6,7},{7,6},{8,9},{9,8},{10,11... | collective-permute-start | bytes 786440 | tf_op jit(solution)/shard_map/ppermute | solution.py:323
  75.4 27.3 %collective-permute-start.24 = (bf16[8,128,128]{2,1,0:T(8,128)(2,1)S(1)}, bf16[8,128,128]{2,1,0:T(8,128)(2,1)S(1)}, u32[]{:S(2)}, u32[]{:S(2)}) collective-permute-start(bf16[8,128,128]{2,1,0:T(8,128)(2,1)S(1)} %get-tuple-element.64), channel_id=1, source_target_pairs={{0,32},{32,64},{64,96},{96,0},{1,33},{33,65},{65,97},{97,1},{2,34}... | collective-permute-start | bytes 786440 | tf_op jit(solution)/shard_map/ppermute | solution.py:323
  76.9 25.9 %collective-permute-start.25 = (bf16[8,128,128]{2,1,0:T(8,128)(2,1)S(1)}, bf16[8,128,128]{2,1,0:T(8,128)(2,1)S(1)}, u32[]{:S(2)}, u32[]{:S(2)}) collective-permute-start(bf16[8,128,128]{2,1,0:T(8,128)(2,1)S(1)} %get-tuple-element.65), channel_id=1, source_target_pairs={{0,64},{32,96},{64,0},{96,32},{1,65},{33,97},{65,1},{97,33},{2,66}... | collective-permute-start | bytes 786440 | tf_op jit(solution)/shard_map/ppermute | solution.py:323
  81.0 21.8 %collective-permute-start.26 = (bf16[8,128,128]{2,1,0:T(8,128)(2,1)S(1)}, bf16[8,128,128]{2,1,0:T(8,128)(2,1)S(1)}, u32[]{:S(2)}, u32[]{:S(2)}) collective-permute-start(bf16[8,128,128]{2,1,0:T(8,128)(2,1)S(1)} %get-tuple-element.66), channel_id=1, source_target_pairs={{0,96},{32,0},{64,32},{96,64},{1,97},{33,1},{65,33},{97,65},{2,98}... | collective-permute-start | bytes 786440 | tf_op jit(solution)/shard_map/ppermute | solution.py:323
  83.0 9.4 %collective-permute-start.28 = (bf16[32,128]{1,0:T(8,128)(2,1)S(1)}, bf16[32,128]{1,0:T(8,128)(2,1)S(1)}, u32[]{:S(2)}, u32[]{:S(2)}) collective-permute-start(bf16[32,128]{1,0:T(8,128)(2,1)S(1)} %get-tuple-element.69), channel_id=1, source_target_pairs={{0,64},{32,96},{64,0},{96,32},{1,65},{33,97},{65,1},{97,33},{2,66}... | collective-permute-start | bytes 24584 | tf_op jit(solution)/shard_map/ppermute | solution.py:323
  103.8 10.0 %collective-permute-start.32 = (bf16[1024,128]{1,0:T(8,128)(2,1)S(1)}, bf16[1024,128]{1,0:T(8,128)(2,1)S(1)}, u32[]{:S(2)}, u32[]{:S(2)}) collective-permute-start(bf16[1024,128]{1,0:T(8,128)(2,1)S(1)} %get-tuple-element.72.p0), channel_id=1, source_target_pairs={{0,96},{32,0},{64,32},{96,64},{1,97},{33,1},{65,33},{97,65},{2,98}... | collective-permute-start | bytes 786440 | tf_op jit(solution)/shard_map/ppermute | solution.py:318
  107.2 10.4 %collective-permute-start.34 = (bf16[1024,128]{1,0:T(8,128)(2,1)S(1)}, bf16[1024,128]{1,0:T(8,128)(2,1)S(1)}, u32[]{:S(2)}, u32[]{:S(2)}) collective-permute-start(bf16[1024,128]{1,0:T(8,128)(2,1)S(1)} %get-tuple-element.72.p0), channel_id=1, source_target_pairs={{0,32},{32,64},{64,96},{96,0},{1,33},{33,65},{65,97},{97,1},{2,34}... | collective-permute-start | bytes 786440 | tf_op jit(solution)/shard_map/ppermute | solution.py:318
  124.0 9.6 %collective-permute-start.41 = (bf16[8,128,128]{2,1,0:T(8,128)(2,1)S(1)}, bf16[8,128,128]{2,1,0:T(8,128)(2,1)S(1)}, u32[]{:S(2)}, u32[]{:S(2)}) collective-permute-start(bf16[8,128,128]{2,1,0:T(8,128)(2,1)S(1)} %shard_map.95), channel_id=1, source_target_pairs={{0,6},{1,25},{2,0},{3,27},{4,2},{5,29},{6,4},{7,31},{8,14},{9,1},{... | collective-permute-start | bytes 786440 | tf_op jit(solution)/shard_map/ppermute | solution.py:333
  127.5 8.1 %collective-permute-start.39 = (bf16[8,128,128]{2,1,0:T(8,128)(2,1)S(1)}, bf16[8,128,128]{2,1,0:T(8,128)(2,1)S(1)}, u32[]{:S(2)}, u32[]{:S(2)}) collective-permute-start(bf16[8,128,128]{2,1,0:T(8,128)(2,1)S(1)} %shard_map.94), channel_id=1, source_target_pairs={{0,4},{1,17},{2,6},{3,19},{4,0},{5,21},{6,2},{7,23},{8,12},{9,25},... | collective-permute-start | bytes 786440 | tf_op jit(solution)/shard_map/ppermute | solution.py:333
  128.2 10.1 %collective-permute-start.37 = (bf16[8,128,128]{2,1,0:T(8,128)(2,1)S(1)}, bf16[8,128,128]{2,1,0:T(8,128)(2,1)S(1)}, u32[]{:S(2)}, u32[]{:S(2)}) collective-permute-start(bf16[8,128,128]{2,1,0:T(8,128)(2,1)S(1)} %shard_map.93), channel_id=1, source_target_pairs={{0,2},{1,9},{2,4},{3,11},{4,6},{5,13},{6,0},{7,15},{8,10},{9,17},{... | collective-permute-start | bytes 786440 | tf_op jit(solution)/shard_map/ppermute | solution.py:333
  140.8 8.7 %collective-permute-start.43 = (bf16[8,128,128]{2,1,0:T(8,128)(2,1)S(1)}, bf16[8,128,128]{2,1,0:T(8,128)(2,1)S(1)}, u32[]{:S(2)}, u32[]{:S(2)}) collective-permute-start(bf16[8,128,128]{2,1,0:T(8,128)(2,1)S(1)} %get-tuple-element.79), channel_id=1, source_target_pairs={{0,16},{1,5},{2,18},{3,7},{4,20},{5,1},{6,22},{7,3},{8,24},{9,13},... | collective-permute-start | bytes 786440 | tf_op jit(solution)/shard_map/ppermute | solution.py:333
  150.6 8.0 %collective-permute-start.46 = (bf16[8,128,128]{2,1,0:T(8,128)(2,1)S(1)}, bf16[8,128,128]{2,1,0:T(8,128)(2,1)S(1)}, u32[]{:S(2)}, u32[]{:S(2)}) collective-permute-start(bf16[8,128,128]{2,1,0:T(8,128)(2,1)S(1)} %shard_map.97.refs_0_), channel_id=1, source_target_pairs={{0,4},{1,17},{2,6},{3,19},{4,0},{5,21},{6,2},{7,23},{8,12},{9,25},... | collective-permute-start | bytes 786440 | tf_op jit(solution)/shard_map/ppermute | solution.py:333
  150.6 10.7 %collective-permute-start.47 = (bf16[8,128,128]{2,1,0:T(8,128)(2,1)S(1)}, bf16[8,128,128]{2,1,0:T(8,128)(2,1)S(1)}, u32[]{:S(2)}, u32[]{:S(2)}) collective-permute-start(bf16[8,128,128]{2,1,0:T(8,128)(2,1)S(1)} %shard_map.97.refs_0_), channel_id=1, source_target_pairs={{0,2},{1,9},{2,4},{3,11},{4,6},{5,13},{6,0},{7,15},{8,10},{9,17},{... | collective-permute-start | bytes 786440 | tf_op jit(solution)/shard_map/ppermute | solution.py:333
  152.0 9.3 %collective-permute-start.48 = (bf16[8,128,128]{2,1,0:T(8,128)(2,1)S(1)}, bf16[8,128,128]{2,1,0:T(8,128)(2,1)S(1)}, u32[]{:S(2)}, u32[]{:S(2)}) collective-permute-start(bf16[8,128,128]{2,1,0:T(8,128)(2,1)S(1)} %shard_map.97.refs_0_), channel_id=1, source_target_pairs={{0,1},{1,0},{2,3},{3,2},{4,5},{5,4},{6,7},{7,6},{8,9},{9,8},{10,11... | collective-permute-start | bytes 786440 | tf_op jit(solution)/shard_map/ppermute | solution.py:323
  166.7 21.4 %collective-permute-start.52 = (bf16[8,128,128]{2,1,0:T(8,128)(2,1)S(1)}, bf16[8,128,128]{2,1,0:T(8,128)(2,1)S(1)}, u32[]{:S(2)}, u32[]{:S(2)}) collective-permute-start(bf16[8,128,128]{2,1,0:T(8,128)(2,1)S(1)} %get-tuple-element.81), channel_id=1, source_target_pairs={{0,32},{32,64},{64,96},{96,0},{1,33},{33,65},{65,97},{97,1},{2,34}... | collective-permute-start | bytes 786440 | tf_op jit(solution)/shard_map/ppermute | solution.py:323
  166.8 21.3 %collective-permute-start.53 = (bf16[8,128,128]{2,1,0:T(8,128)(2,1)S(1)}, bf16[8,128,128]{2,1,0:T(8,128)(2,1)S(1)}, u32[]{:S(2)}, u32[]{:S(2)}) collective-permute-start(bf16[8,128,128]{2,1,0:T(8,128)(2,1)S(1)} %get-tuple-element.82), channel_id=1, source_target_pairs={{0,64},{32,96},{64,0},{96,32},{1,65},{33,97},{65,1},{97,33},{2,66}... | collective-permute-start | bytes 786440 | tf_op jit(solution)/shard_map/ppermute | solution.py:323
  170.9 17.2 %collective-permute-start.54 = (bf16[8,128,128]{2,1,0:T(8,128)(2,1)S(1)}, bf16[8,128,128]{2,1,0:T(8,128)(2,1)S(1)}, u32[]{:S(2)}, u32[]{:S(2)}) collective-permute-start(bf16[8,128,128]{2,1,0:T(8,128)(2,1)S(1)} %get-tuple-element.83), channel_id=1, source_target_pairs={{0,96},{32,0},{64,32},{96,64},{1,97},{33,1},{65,33},{97,65},{2,98}... | collective-permute-start | bytes 786440 | tf_op jit(solution)/shard_map/ppermute | solution.py:323
  172.2 10.7 %collective-permute-start.55 = (bf16[32,128]{1,0:T(8,128)(2,1)S(1)}, bf16[32,128]{1,0:T(8,128)(2,1)S(1)}, u32[]{:S(2)}, u32[]{:S(2)}) collective-permute-start(bf16[32,128]{1,0:T(8,128)(2,1)S(1)} %get-tuple-element.85), channel_id=1, source_target_pairs={{0,32},{32,64},{64,96},{96,0},{1,33},{33,65},{65,97},{97,1},{2,34}... | collective-permute-start | bytes 24584 | tf_op jit(solution)/shard_map/ppermute | solution.py:323
  172.9 10.0 %collective-permute-start.56 = (bf16[32,128]{1,0:T(8,128)(2,1)S(1)}, bf16[32,128]{1,0:T(8,128)(2,1)S(1)}, u32[]{:S(2)}, u32[]{:S(2)}) collective-permute-start(bf16[32,128]{1,0:T(8,128)(2,1)S(1)} %get-tuple-element.86), channel_id=1, source_target_pairs={{0,64},{32,96},{64,0},{96,32},{1,65},{33,97},{65,1},{97,33},{2,66}... | collective-permute-start | bytes 24584 | tf_op jit(solution)/shard_map/ppermute | solution.py:323
  (28 other events, 138.9 us)

commit v3 on v1

--- a/solution.py
+++ b/solution.py
@@ -11,7 +11,7 @@
 LEVELS = 5
 ITERS = 2
 TILE = 128
-GROUP = 48
+GROUP = 64
 CHUNK = 16
 ROW_BLOCKS = 64
 CELL_TILES = 32
@@ -75,9 +75,10 @@
         tails[8 * g : 8 * g + 8, :] = last
 
 
-def axes(place, core):
-    first = jnp.where(core == 0, place[1], place[0])
-    second = jnp.where(core == 0, place[0], place[1])
+def axes(core):
+    x, z = lax.axis_index("x"), lax.axis_index("z")
+    first = jnp.where(core == 0, z, x)
+    second = jnp.where(core == 0, x, z)
     step = jnp.where(core == 0, 1, 4)
     return first, second, step, 5 - step
 
@@ -143,15 +144,16 @@
     fix[...] = model[0:128, :]
 
 
-def first_kernel(rows, cols, cnt, place, f0, f1, f2, f3, *refs):
-    fwd_kernel(rows, cols, cnt, place, *refs, fixes=(f0, f1, f2, f3))
+def first_kernel(table, f0, f1, f2, f3, *refs):
+    fwd_kernel(table, *refs, fixes=(f0, f1, f2, f3))
 
 
 def fwd_kernel(
-    rows, cols, cnt, place, p0, p1, p2, p3, jac, keep, send, jbuf, model, acc, sems, fixes=None
+    table, p0, p1, p2, p3, jac, keep, send, jbuf, model, acc, sems, fixes=None
 ):
-    live = cnt[0]
-    core = place[2]
+    slots = jac.shape[0]
+    live = table[2 * slots]
+    core = lax.axis_index("core")
     groups, arrive = tile_copies(jac, jbuf, sems, live)
     acc[...] = jnp.zeros(acc.shape, f32)
     for c in range(CELL_TILES):
@@ -165,8 +167,8 @@
         arrive(g)
         for v in range(GROUP):
             s = g * GROUP + v
-            r = jnp.where(s < live, rows[s], ROW_BLOCKS)
-            acc[r] += jnp.dot(jbuf[s], model[cols[s]], preferred_element_type=f32)
+            r = jnp.where(s < live, table[s], ROW_BLOCKS)
+            acc[r] += jnp.dot(jbuf[s], model[table[slots + s]], preferred_element_type=f32)
         return carry
 
     lax.fori_loop(0, groups, group, 0)
@@ -176,8 +178,8 @@
             send[2 * xz + h] = acc[4 * xz + 2 * (1 - core) + h].astype(bf16)
 
 
-def split_kernel(place, keep, recv, own, s1, s2, s3):
-    first, _, step, other = axes(place, place[2])
+def split_kernel(keep, recv, own, s1, s2, s3):
+    first, _, step, other = axes(lax.axis_index("core"))
     for k, out in enumerate((own, s1, s2, s3)):
         for e in range(4):
             for h in range(2):
@@ -196,8 +198,8 @@
     return own[i] + r1[i].astype(f32) + r2[i].astype(f32) + r3[i].astype(f32) - obs[i]
 
 
-def obs_kernel(place, obs, out):
-    back = (128 - 32 * place[3]) % 128
+def obs_kernel(obs, out):
+    back = (128 - 32 * lax.axis_index("ray")) % 128
     for i in range(8):
         out[i] = pltpu.roll(obs[i // 2, 128 * (i % 2) : 128 * (i % 2) + 128, :], back, 1)
 
@@ -207,20 +209,21 @@
         rounded[i] = misfit_tile(own, r1, r2, r3, obs, i).T.astype(bf16)
 
 
-def share_kernel(place, own, r1, r2, r3, obs, share):
+def share_kernel(own, r1, r2, r3, obs, share):
     for h in range(2):
-        tile = misfit_tile(own, r1, r2, r3, obs, 2 * axes(place, place[2])[1] + h)
-        share[128 * h : 128 * h + 128, :] = pltpu.roll(tile, 32 * place[3], 1)
-
-
-def bwd_kernel(rows, cols, cnt, place, *refs):
+        tile = misfit_tile(own, r1, r2, r3, obs, 2 * axes(lax.axis_index("core"))[1] + h)
+        share[128 * h : 128 * h + 128, :] = pltpu.roll(tile, 32 * lax.axis_index("ray"), 1)
+
+
+def bwd_kernel(table, *refs):
     jac, g0, g1, g2, g3, e0, e1, e2, e3, jbuf, mis, acc, sems = refs[8:]
-    live = cnt[0]
-    core = place[2]
+    slots = jac.shape[0]
+    live = table[2 * slots]
+    core = lax.axis_index("core")
     groups, arrive = tile_copies(jac, jbuf, sems, live)
     acc[...] = jnp.zeros(acc.shape, f32)
     for pieces, c in ((refs[0:4], core), (refs[4:8], 1 - core)):
-        first, _, step, other = axes(place, c)
+        first, _, step, other = axes(c)
         for k in range(4):
             b = 4 * step * ((first + k) % 4) + 2 * c
             for e in range(4):
@@ -231,8 +234,8 @@
         arrive(g)
         for v in range(GROUP):
             s = g * GROUP + v
-            c = jnp.where(s < live, cols[s], CELL_TILES)
-            acc[c] += jnp.dot(mis[rows[s]], jbuf[s], preferred_element_type=f32)
+            c = jnp.where(s < live, table[slots + s], CELL_TILES)
+            acc[c] += jnp.dot(mis[table[s]], jbuf[s], preferred_element_type=f32)
         return carry
 
     lax.fori_loop(0, groups, group, 0)
@@ -353,8 +356,8 @@
     cols = tile_cols[0, 0]
     cnt = tile_count[0]
     n_slots = jac.shape[0]
-    x, z, core, ray = (lax.axis_index(a) for a in ("x", "z", "core", "ray"))
-    place = jnp.stack([x, z, core, ray]).astype(jnp.int32)
+    table = jnp.concatenate([rows, cols, cnt])
+    x, z, core = (lax.axis_index(a) for a in ("x", "z", "core"))
     tiles = sds((8, 128, 128), f32)
     tiles_b = sds((8, 128, 128), bf16)
     flat_b = sds((1024, 128), bf16)
@@ -369,7 +372,7 @@
         lambda a: lax.dynamic_slice(a, (x, 0, 1, 0, 0), (1, 4, 1, 256, 128)).reshape(4, 256, 128),
         obs_all,
     )
-    (obs_t,) = call(obs_kernel, [SM, VM], [tiles])(place, obs_rows)
+    (obs_t,) = call(obs_kernel, [VM], [tiles])(obs_rows)
     recv = along(tails, 1)
     (model,) = call(early_kernel, [VM], [flat_b], SYNTH_BUFS)(state)
     state, fix = call(
@@ -390,31 +393,31 @@
             fixes = [fix] + three([fix] * 3, pull)
         keep, send = call(
             fwd_kernel if sweep else first_kernel,
-            [SM] * 4 + [VM] * (4 + len(fixes)) + [ANY],
+            [SM] + [VM] * (4 + len(fixes)) + [ANY],
             [sds((32, 128, 128), f32), sds((32, 128, 128), bf16)],
             [jac_scratch, pltpu.VMEM((32, 128, 128), bf16), pltpu.VMEM((65, 128, 128), f32), sems],
-        )(rows, cols, cnt, place, *fixes, *pieces, jac)
+        )(table, *fixes, *pieces, jac)
         got = to_ahead(send, "core", 1)
         own, s1, s2, s3 = call(
-            split_kernel, [SM, VM, VM], [tiles, tiles_b, tiles_b, tiles_b]
-        )(place, keep, got)
+            split_kernel, [VM, VM], [tiles, tiles_b, tiles_b, tiles_b]
+        )(keep, got)
         r = three((s1, s2, s3), lambda a, k: by_core(a, 0, k))
         own, sent = call(gather_kernel, [VM] * 4, [tiles, tiles_b])(own, *r)
         r = three([sent] * 3, lambda a, k: by_core(a, 1, k))
         (rounded,) = call(misfit_kernel, [VM] * 5, [tiles_b])(own, *r, obs_t)
         if sweep == ITERS - 1:
-            (share,) = call(share_kernel, [SM] + [VM] * 5, [sds((256, 128), f32)])(
-                place, own, *r, obs_t
+            (share,) = call(share_kernel, [VM] * 5, [sds((256, 128), f32)])(
+                own, *r, obs_t
             )
         mine = [rounded] + three([rounded] * 3, lambda a, k: by_core(a, 0, -k))
         other = [to_ahead(m, "core", 1) for m in mine]
         edge, edge_b = sds((32, 128), f32), sds((32, 128), bf16)
         g0, g1, g2, g3, e0, e1, e2, e3 = call(
             bwd_kernel,
-            [SM, SM, SM, SM] + [VM] * 8 + [ANY],
+            [SM] + [VM] * 8 + [ANY],
             [tiles, tiles_b, tiles_b, tiles_b, edge, edge_b, edge_b, edge_b],
             [jac_scratch, pltpu.VMEM((64, 128, 128), bf16), pltpu.VMEM((33, 128, 128), f32), sems],
-        )(rows, cols, cnt, place, *mine, *other, jac)
+        )(table, *mine, *other, jac)
         r = three((e1, e2, e3), push)
         (near,) = call(edge_kernel, [VM] * 4, [edge])(e0, *r)
         nxt = along(near, -1)

time: 190 us -> 191 us (level)
  waiting for transfers between devices: 83.3 us -> 92.5 us
  starting transfers between devices: 75.8 us -> 70.8 us
  Pallas kernels: 24.1 us -> 21.6 us
    ppermute x22, waiting for transfers between devices: 20.7 us -> 27.7 us  [to_ahead(): return lax.ppermute(x, axis, [(i, (i + by) % n) for i in range(n)])]
    ppermute x22, starting transfers between devices: 25.3 us -> 21.1 us  [to_ahead(): return lax.ppermute(x, axis, [(i, (i + by) % n) for i in range(n)])]
    pallas_call x8, Pallas kernels: 19.3 us -> 16.8 us  [the longest x2 8.39 us: body(): call(fwd_kernel if sweep else first_kernel, [SM] + [VM] * (4 + len(fixes)...]
  transfers between devices with their start and end apart: 53 -> 53, of which waited for: 32 -> 33; matrix products, arithmetic and copies ran while one was open for 1% -> 1% of each run, Pallas kernels for 1% -> 1%
where the time goes in v3:
time: 191 us; the launch traced here: 190 us
  waiting for transfers between devices  92.5 us (48%)
  starting transfers between devices  70.8 us (37%)
  Pallas kernels  21.6 us (11%)
  local copies, waits for them, and re-layouts  2.11 us (1%)
    ppermute x18, waiting for transfers between devices, by_core(): return lax.ppermute(x, MP, pairs)  39.5 us
    ppermute x18, starting transfers between devices, by_core(): return lax.ppermute(x, MP, pairs)  30.9 us
    ppermute x22, waiting for transfers between devices, to_ahead(): return lax.ppermute(x, axis, [(i, (i + by) % n) for i in range(n)])  27.7 us
    ppermute x22, starting transfers between devices, to_ahead(): return lax.ppermute(x, axis, [(i, (i + by) % n) for i in range(n)])  21.1 us
    ppermute x9, waiting for transfers between devices, from_ahead(): return lax.ppermute(x, axis, [(i, (i - by) % n) for i in range(n)])  16.6 us
    ppermute x9, starting transfers between devices, from_ahead(): return lax.ppermute(x, axis, [(i, (i - by) % n) for i in range(n)])  13.1 us
    ppermute x4, waiting for transfers between devices, along(): return lax.ppermute(x, MP, [(i, (i + by) % 32) for i in range(32)])  8.69 us
    pallas_call x2, Pallas kernels, body(): call(fwd_kernel if sweep else first_kernel, [SM] + [VM] * (4 + len(fixes)...  8.39 us
  transfers between devices with their start and end apart: 53, of which 33 were waited for; matrix products, arithmetic and copies ran while one was open for 1% of the time, Pallas kernels for 1%

profile of v3, /device:TPU:0, one launch (start us, length us, event | category | flops | bytes accessed | tf_op | source)
XLA Modules:
  0.0 189.9 jit_solution(5277316759069294788)
XLA Ops:
  4.5 2.9 %collective-permute-start.5 = (bf16[1024,128]{1,0:T(8,128)(2,1)S(1)}, bf16[1024,128]{1,0:T(8,128)(2,1)S(1)}, u32[]{:S(2)}, u32[]{:S(2)}) collective-permute-start(bf16[1024,128]{1,0:T(8,128)(2,1)S(1)} %shard_map.79.refs_0_), channel_id=1, source_target_pairs={{0,64},{32,96},{64,0},{96,32},{1,65},{33,97},{65,1},{97,33},{2,66}... | collective-permute-start | bytes 786440 | tf_op jit(solution)/shard_map/ppermute | solution.py:321
  8.7 6.6 %collective-permute-done.recv = f32[48,128]{1,0:T(8,128)S(1)} collective-permute-done((f32[48,128]{1,0:T(8,128)S(1)}, f32[48,128]{1,0:T(8,128)S(1)}, u32[]{:S(2)}, u32[]{:S(2)}) %collective-permute-start) | collective-permute-done | bytes 24608 | tf_op jit(solution)/shard_map/ppermute | solution.py:350
  21.4 2.7 %collective-permute-done.2.f2 = bf16[128,128]{1,0:T(8,128)(2,1)S(1)} collective-permute-done((bf16[128,128]{1,0:T(8,128)(2,1)S(1)}, bf16[128,128]{1,0:T(8,128)(2,1)S(1)}, u32[]{:S(2)}, u32[]{:S(2)}) %collective-permute-start.2) | collective-permute-done | bytes 32800 | tf_op jit(solution)/shard_map/ppermute | solution.py:321
  24.9 4.2 %shard_map.80 = (f32[32,128,128]{2,1,0:T(8,128)S(1)}, bf16[32,128,128]{2,1,0:T(8,128)(2,1)S(1)}) custom-call(s32[769]{0:T(1024)S(1)} %pad_add_fusion.table, bf16[128,128]{1,0:T(8,128)(2,1)S(1)} %get-tuple-element.57.f0, bf16[128,128]{1,0:T(8,128)(2,1)S(1)} %collective-permute-done.1.f1, bf16[128,128]{1,0:T(8,128)(2,1)S(1)} %collective-permute-done.2.f2, ...), custom_call_target="tpu_custom_call" | custom-call | tf_op jit(solution)/shard_map/pallas_call | solution.py:394
  29.2 2.6 %collective-permute-done.7.recv = bf16[32,128,128]{2,1,0:T(8,128)(2,1)S(1)} collective-permute-done((bf16[32,128,128]{2,1,0:T(8,128)(2,1)S(1)}, bf16[32,128,128]{2,1,0:T(8,128)(2,1)S(1)}, u32[]{:S(2)}, u32[]{:S(2)}) %collective-permute-start.7) | collective-permute-done | bytes 1048608 | tf_op jit(solution)/shard_map/ppermute | solution.py:326
  34.0 3.5 %collective-permute-start.9 = (bf16[8,128,128]{2,1,0:T(8,128)(2,1)S(1)}, bf16[8,128,128]{2,1,0:T(8,128)(2,1)S(1)}, u32[]{:S(2)}, u32[]{:S(2)}) collective-permute-start(bf16[8,128,128]{2,1,0:T(8,128)(2,1)S(1)} %get-tuple-element.62), channel_id=1, source_target_pairs={{0,4},{1,17},{2,6},{3,19},{4,0},{5,21},{6,2},{7,23},{8,12},{9,25},... | collective-permute-start | bytes 786440 | tf_op jit(solution)/shard_map/ppermute | solution.py:336
  40.3 4.3 %collective-permute-done.9.r2 = bf16[8,128,128]{2,1,0:T(8,128)(2,1)S(1)} collective-permute-done((bf16[8,128,128]{2,1,0:T(8,128)(2,1)S(1)}, bf16[8,128,128]{2,1,0:T(8,128)(2,1)S(1)}, u32[]{:S(2)}, u32[]{:S(2)}) %collective-permute-start.9) | collective-permute-done | bytes 262176 | tf_op jit(solution)/shard_map/ppermute | solution.py:336
  44.7 2.4 %collective-permute-start.13 = (bf16[8,128,128]{2,1,0:T(8,128)(2,1)S(1)}, bf16[8,128,128]{2,1,0:T(8,128)(2,1)S(1)}, u32[]{:S(2)}, u32[]{:S(2)}) collective-permute-start(bf16[8,128,128]{2,1,0:T(8,128)(2,1)S(1)} %get-tuple-element.65), channel_id=1, source_target_pairs={{0,24},{1,7},{2,26},{3,1},{4,28},{5,3},{6,30},{7,5},{8,0},{9,15},{... | collective-permute-start | bytes 786440 | tf_op jit(solution)/shard_map/ppermute | solution.py:336
  50.5 3.4 %collective-permute-done.13.r3 = bf16[8,128,128]{2,1,0:T(8,128)(2,1)S(1)} collective-permute-done((bf16[8,128,128]{2,1,0:T(8,128)(2,1)S(1)}, bf16[8,128,128]{2,1,0:T(8,128)(2,1)S(1)}, u32[]{:S(2)}, u32[]{:S(2)}) %collective-permute-start.13) | collective-permute-done | bytes 262176 | tf_op jit(solution)/shard_map/ppermute | solution.py:336
  55.1 2.7 %collective-permute-done.11.r1 = bf16[8,128,128]{2,1,0:T(8,128)(2,1)S(1)} collective-permute-done((bf16[8,128,128]{2,1,0:T(8,128)(2,1)S(1)}, bf16[8,128,128]{2,1,0:T(8,128)(2,1)S(1)}, u32[]{:S(2)}, u32[]{:S(2)}) %collective-permute-start.11) | collective-permute-done | bytes 262176 | tf_op jit(solution)/shard_map/ppermute | solution.py:336
  65.7 3.7 %collective-permute-done.15.refs_2_ = bf16[8,128,128]{2,1,0:T(8,128)(2,1)S(1)} collective-permute-done((bf16[8,128,128]{2,1,0:T(8,128)(2,1)S(1)}, bf16[8,128,128]{2,1,0:T(8,128)(2,1)S(1)}, u32[]{:S(2)}, u32[]{:S(2)}) %collective-permute-start.15) | collective-permute-done | bytes 262176 | tf_op jit(solution)/shard_map/ppermute | solution.py:336
  71.3 3.5 %shard_map.85 = (f32[8,128,128]{2,1,0:T(8,128)S(1)}, bf16[8,128,128]{2,1,0:T(8,128)(2,1)S(1)}, bf16[8,128,128]{2,1,0:T(8,128)(2,1)S(1)}, bf16[8,128,128]{2,1,0:T...) custom-call(s32[769]{0:T(1024)S(1)} %pad_add_fusion.table, ...), custom_call_target="tpu_custom_call" | custom-call | tf_op jit(solution)/shard_map/pallas_call | solution.py:415
  76.5 3.5 %collective-permute-start.22 = (bf16[8,128,128]{2,1,0:T(8,128)(2,1)S(1)}, bf16[8,128,128]{2,1,0:T(8,128)(2,1)S(1)}, u32[]{:S(2)}, u32[]{:S(2)}) collective-permute-start(bf16[8,128,128]{2,1,0:T(8,128)(2,1)S(1)} %get-tuple-element.68), channel_id=1, source_target_pairs={{0,64},{32,96},{64,0},{96,32},{1,65},{33,97},{65,1},{97,33},{2,66}... | collective-permute-start | bytes 786440 | tf_op jit(solution)/shard_map/ppermute | solution.py:326
  82.4 6.3 %collective-permute-done.24.r1 = bf16[32,128]{1,0:T(8,128)(2,1)S(1)} collective-permute-done((bf16[32,128]{1,0:T(8,128)(2,1)S(1)}, bf16[32,128]{1,0:T(8,128)(2,1)S(1)}, u32[]{:S(2)}, u32[]{:S(2)}) %collective-permute-start.24) | collective-permute-done | bytes 8224 | tf_op jit(solution)/shard_map/ppermute | solution.py:326
  88.7 3.3 %collective-permute-start.26 = (bf16[32,128]{1,0:T(8,128)(2,1)S(1)}, bf16[32,128]{1,0:T(8,128)(2,1)S(1)}, u32[]{:S(2)}, u32[]{:S(2)}) collective-permute-start(bf16[32,128]{1,0:T(8,128)(2,1)S(1)} %get-tuple-element.73), channel_id=1, source_target_pairs={{0,96},{32,0},{64,32},{96,64},{1,97},{33,1},{65,33},{97,65},{2,98}... | collective-permute-start | bytes 24584 | tf_op jit(solution)/shard_map/ppermute | solution.py:326
  94.2 4.2 %collective-permute-start.27 = (f32[32,128]{1,0:T(8,128)S(1)}, f32[32,128]{1,0:T(8,128)S(1)}, u32[]{:S(2)}, u32[]{:S(2)}) collective-permute-start(f32[32,128]{1,0:T(8,128)S(1)} %shard_map.86), channel_id=1, source_target_pairs={{0,31},{1,0},{2,1},{3,2},{4,3},{5,4},{6,5},{7,6},{8,7},{9,8},{10,9... | collective-permute-start | bytes 49160 | tf_op jit(solution)/shard_map/ppermute | solution.py:350
  102.5 3.5 %collective-permute-start.30 = (bf16[1024,128]{1,0:T(8,128)(2,1)S(1)}, bf16[1024,128]{1,0:T(8,128)(2,1)S(1)}, u32[]{:S(2)}, u32[]{:S(2)}) collective-permute-start(bf16[1024,128]{1,0:T(8,128)(2,1)S(1)} %get-tuple-element.75.p0), channel_id=1, source_target_pairs={{0,64},{32,96},{64,0},{96,32},{1,65},{33,97},{65,1},{97,33},{2,66}... | collective-permute-start | bytes 786440 | tf_op jit(solution)/shard_map/ppermute | solution.py:321
  106.0 4.8 %collective-permute-done.31.p3 = bf16[1024,128]{1,0:T(8,128)(2,1)S(1)} collective-permute-done((bf16[1024,128]{1,0:T(8,128)(2,1)S(1)}, bf16[1024,128]{1,0:T(8,128)(2,1)S(1)}, u32[]{:S(2)}, u32[]{:S(2)}) %collective-permute-start.31) | collective-permute-done | bytes 262176 | tf_op jit(solution)/shard_map/ppermute | solution.py:321
  110.8 6.8 %collective-permute-done.30.p2 = bf16[1024,128]{1,0:T(8,128)(2,1)S(1)} collective-permute-done((bf16[1024,128]{1,0:T(8,128)(2,1)S(1)}, bf16[1024,128]{1,0:T(8,128)(2,1)S(1)}, u32[]{:S(2)}, u32[]{:S(2)}) %collective-permute-start.30) | collective-permute-done | bytes 262176 | tf_op jit(solution)/shard_map/ppermute | solution.py:321
  117.6 4.2 %shard_map.88 = (f32[32,128,128]{2,1,0:T(8,128)S(1)}, bf16[32,128,128]{2,1,0:T(8,128)(2,1)S(1)}) custom-call(s32[769]{0:T(1024)S(1)} %pad_add_fusion.table, bf16[1024,128]{1,0:T(8,128)(2,1)S(1)} %get-tuple-element.75.p0, bf16[1024,128]{1,0:T(8,128)(2,1)S(1)} %collective-permute-done.29.p1, bf16[1024,128]{1,0:T(8,128)(2,1)S(1)} %collective-permute-done.30.p2, ...), custom_call_target="tpu_custom_call" | custom-call | tf_op jit(solution)/shard_map/pallas_call | solution.py:394
  125.4 3.3 %collective-permute-start.34 = (bf16[8,128,128]{2,1,0:T(8,128)(2,1)S(1)}, bf16[8,128,128]{2,1,0:T(8,128)(2,1)S(1)}, u32[]{:S(2)}, u32[]{:S(2)}) collective-permute-start(bf16[8,128,128]{2,1,0:T(8,128)(2,1)S(1)} %get-tuple-element.80), channel_id=1, source_target_pairs={{0,4},{1,17},{2,6},{3,19},{4,0},{5,21},{6,2},{7,23},{8,12},{9,25},... | collective-permute-start | bytes 786440 | tf_op jit(solution)/shard_map/ppermute | solution.py:336
  132.6 3.3 %collective-permute-done.34.r2 = bf16[8,128,128]{2,1,0:T(8,128)(2,1)S(1)} collective-permute-done((bf16[8,128,128]{2,1,0:T(8,128)(2,1)S(1)}, bf16[8,128,128]{2,1,0:T(8,128)(2,1)S(1)}, u32[]{:S(2)}, u32[]{:S(2)}) %collective-permute-start.34) | collective-permute-done | bytes 262176 | tf_op jit(solution)/shard_map/ppermute | solution.py:336
  139.6 3.2 %collective-permute-done.38.r3 = bf16[8,128,128]{2,1,0:T(8,128)(2,1)S(1)} collective-permute-done((bf16[8,128,128]{2,1,0:T(8,128)(2,1)S(1)}, bf16[8,128,128]{2,1,0:T(8,128)(2,1)S(1)}, u32[]{:S(2)}, u32[]{:S(2)}) %collective-permute-start.38) | collective-permute-done | bytes 262176 | tf_op jit(solution)/shard_map/ppermute | solution.py:336
  142.8 2.9 %collective-permute-done.37.r2 = bf16[8,128,128]{2,1,0:T(8,128)(2,1)S(1)} collective-permute-done((bf16[8,128,128]{2,1,0:T(8,128)(2,1)S(1)}, bf16[8,128,128]{2,1,0:T(8,128)(2,1)S(1)}, u32[]{:S(2)}, u32[]{:S(2)}) %collective-permute-start.37) | collective-permute-done | bytes 262176 | tf_op jit(solution)/shard_map/ppermute | solution.py:336
  145.8 2.7 %collective-permute-done.36.r1 = bf16[8,128,128]{2,1,0:T(8,128)(2,1)S(1)} collective-permute-done((bf16[8,128,128]{2,1,0:T(8,128)(2,1)S(1)}, bf16[8,128,128]{2,1,0:T(8,128)(2,1)S(1)}, u32[]{:S(2)}, u32[]{:S(2)}) %collective-permute-start.36) | collective-permute-done | bytes 262176 | tf_op jit(solution)/shard_map/ppermute | solution.py:336
  149.5 3.3 %collective-permute-start.40 = (bf16[8,128,128]{2,1,0:T(8,128)(2,1)S(1)}, bf16[8,128,128]{2,1,0:T(8,128)(2,1)S(1)}, u32[]{:S(2)}, u32[]{:S(2)}) collective-permute-start(bf16[8,128,128]{2,1,0:T(8,128)(2,1)S(1)} %shard_map.91.refs_0_), channel_id=1, source_target_pairs={{0,4},{1,17},{2,6},{3,19},{4,0},{5,21},{6,2},{7,23},{8,12},{9,25},... | collective-permute-start | bytes 786440 | tf_op jit(solution)/shard_map/ppermute | solution.py:336
  153.1 3.2 %collective-permute-done.41.refs_3_ = bf16[8,128,128]{2,1,0:T(8,128)(2,1)S(1)} collective-permute-done((bf16[8,128,128]{2,1,0:T(8,128)(2,1)S(1)}, bf16[8,128,128]{2,1,0:T(8,128)(2,1)S(1)}, u32[]{:S(2)}, u32[]{:S(2)}) %collective-permute-start.41) | collective-permute-done | bytes 262176 | tf_op jit(solution)/shard_map/ppermute | solution.py:336
  156.4 3.7 %collective-permute-done.40.refs_2_ = bf16[8,128,128]{2,1,0:T(8,128)(2,1)S(1)} collective-permute-done((bf16[8,128,128]{2,1,0:T(8,128)(2,1)S(1)}, bf16[8,128,128]{2,1,0:T(8,128)(2,1)S(1)}, u32[]{:S(2)}, u32[]{:S(2)}) %collective-permute-start.40) | collective-permute-done | bytes 262176 | tf_op jit(solution)/shard_map/ppermute | solution.py:336
  161.9 3.5 %shard_map.92 = (f32[8,128,128]{2,1,0:T(8,128)S(1)}, bf16[8,128,128]{2,1,0:T(8,128)(2,1)S(1)}, bf16[8,128,128]{2,1,0:T(8,128)(2,1)S(1)}, bf16[8,128,128]{2,1,0:T...) custom-call(s32[769]{0:T(1024)S(1)} %pad_add_fusion.table, ...), custom_call_target="tpu_custom_call" | custom-call | tf_op jit(solution)/shard_map/pallas_call | solution.py:415
  167.5 3.9 %collective-permute-start.47 = (bf16[8,128,128]{2,1,0:T(8,128)(2,1)S(1)}, bf16[8,128,128]{2,1,0:T(8,128)(2,1)S(1)}, u32[]{:S(2)}, u32[]{:S(2)}) collective-permute-start(bf16[8,128,128]{2,1,0:T(8,128)(2,1)S(1)} %get-tuple-element.86), channel_id=1, source_target_pairs={{0,64},{32,96},{64,0},{96,32},{1,65},{33,97},{65,1},{97,33},{2,66}... | collective-permute-start | bytes 786440 | tf_op jit(solution)/shard_map/ppermute | solution.py:326
  173.4 9.3 %collective-permute-done.49.r1 = bf16[32,128]{1,0:T(8,128)(2,1)S(1)} collective-permute-done((bf16[32,128]{1,0:T(8,128)(2,1)S(1)}, bf16[32,128]{1,0:T(8,128)(2,1)S(1)}, u32[]{:S(2)}, u32[]{:S(2)}) %collective-permute-start.49) | collective-permute-done | bytes 8224 | tf_op jit(solution)/shard_map/ppermute | solution.py:326
  183.3 3.0 %collective-permute-done.51.r3 = bf16[32,128]{1,0:T(8,128)(2,1)S(1)} collective-permute-done((bf16[32,128]{1,0:T(8,128)(2,1)S(1)}, bf16[32,128]{1,0:T(8,128)(2,1)S(1)}, u32[]{:S(2)}, u32[]{:S(2)}) %collective-permute-start.51) | collective-permute-done | bytes 8224 | tf_op jit(solution)/shard_map/ppermute | solution.py:326
  (100 shorter events, 65.1 us)
Async XLA Ops:
  2.7 22.2 %collective-permute-start.6 = (bf16[1024,128]{1,0:T(8,128)(2,1)S(1)}, bf16[1024,128]{1,0:T(8,128)(2,1)S(1)}, u32[]{:S(2)}, u32[]{:S(2)}) collective-permute-start(bf16[1024,128]{1,0:T(8,128)(2,1)S(1)} %shard_map.79.refs_0_), channel_id=1, source_target_pairs={{0,32},{32,64},{64,96},{96,0},{1,33},{33,65},{65,97},{97,1},{2,34}... | collective-permute-start | bytes 786440 | tf_op jit(solution)/shard_map/ppermute | solution.py:321
  4.5 20.4 %collective-permute-start.5 = (bf16[1024,128]{1,0:T(8,128)(2,1)S(1)}, bf16[1024,128]{1,0:T(8,128)(2,1)S(1)}, u32[]{:S(2)}, u32[]{:S(2)}) collective-permute-start(bf16[1024,128]{1,0:T(8,128)(2,1)S(1)} %shard_map.79.refs_0_), channel_id=1, source_target_pairs={{0,64},{32,96},{64,0},{96,32},{1,65},{33,97},{65,1},{97,33},{2,66}... | collective-permute-start | bytes 786440 | tf_op jit(solution)/shard_map/ppermute | solution.py:321
  7.4 17.5 %collective-permute-start.4 = (bf16[1024,128]{1,0:T(8,128)(2,1)S(1)}, bf16[1024,128]{1,0:T(8,128)(2,1)S(1)}, u32[]{:S(2)}, u32[]{:S(2)}) collective-permute-start(bf16[1024,128]{1,0:T(8,128)(2,1)S(1)} %shard_map.79.refs_0_), channel_id=1, source_target_pairs={{0,96},{32,0},{64,32},{96,64},{1,97},{33,1},{65,33},{97,65},{2,98}... | collective-permute-start | bytes 786440 | tf_op jit(solution)/shard_map/ppermute | solution.py:321
  32.0 8.3 %collective-permute-start.8 = (bf16[8,128,128]{2,1,0:T(8,128)(2,1)S(1)}, bf16[8,128,128]{2,1,0:T(8,128)(2,1)S(1)}, u32[]{:S(2)}, u32[]{:S(2)}) collective-permute-start(bf16[8,128,128]{2,1,0:T(8,128)(2,1)S(1)} %get-tuple-element.61), channel_id=1, source_target_pairs={{0,2},{1,9},{2,4},{3,11},{4,6},{5,13},{6,0},{7,15},{8,10},{9,17},{... | collective-permute-start | bytes 786440 | tf_op jit(solution)/shard_map/ppermute | solution.py:336
  34.0 10.6 %collective-permute-start.9 = (bf16[8,128,128]{2,1,0:T(8,128)(2,1)S(1)}, bf16[8,128,128]{2,1,0:T(8,128)(2,1)S(1)}, u32[]{:S(2)}, u32[]{:S(2)}) collective-permute-start(bf16[8,128,128]{2,1,0:T(8,128)(2,1)S(1)} %get-tuple-element.62), channel_id=1, source_target_pairs={{0,4},{1,17},{2,6},{3,19},{4,0},{5,21},{6,2},{7,23},{8,12},{9,25},... | collective-permute-start | bytes 786440 | tf_op jit(solution)/shard_map/ppermute | solution.py:336
  44.7 9.2 %collective-permute-start.13 = (bf16[8,128,128]{2,1,0:T(8,128)(2,1)S(1)}, bf16[8,128,128]{2,1,0:T(8,128)(2,1)S(1)}, u32[]{:S(2)}, u32[]{:S(2)}) collective-permute-start(bf16[8,128,128]{2,1,0:T(8,128)(2,1)S(1)} %get-tuple-element.65), channel_id=1, source_target_pairs={{0,24},{1,7},{2,26},{3,1},{4,28},{5,3},{6,30},{7,5},{8,0},{9,15},{... | collective-permute-start | bytes 786440 | tf_op jit(solution)/shard_map/ppermute | solution.py:336
  47.1 8.0 %collective-permute-start.12 = (bf16[8,128,128]{2,1,0:T(8,128)(2,1)S(1)}, bf16[8,128,128]{2,1,0:T(8,128)(2,1)S(1)}, u32[]{:S(2)}, u32[]{:S(2)}) collective-permute-start(bf16[8,128,128]{2,1,0:T(8,128)(2,1)S(1)} %get-tuple-element.65), channel_id=1, source_target_pairs={{0,16},{1,5},{2,18},{3,7},{4,20},{5,1},{6,22},{7,3},{8,24},{9,13},... | collective-permute-start | bytes 786440 | tf_op jit(solution)/shard_map/ppermute | solution.py:336
  48.3 9.5 %collective-permute-start.11 = (bf16[8,128,128]{2,1,0:T(8,128)(2,1)S(1)}, bf16[8,128,128]{2,1,0:T(8,128)(2,1)S(1)}, u32[]{:S(2)}, u32[]{:S(2)}) collective-permute-start(bf16[8,128,128]{2,1,0:T(8,128)(2,1)S(1)} %get-tuple-element.65), channel_id=1, source_target_pairs={{0,8},{1,3},{2,10},{3,5},{4,12},{5,7},{6,14},{7,1},{8,16},{9,11},{... | collective-permute-start | bytes 786440 | tf_op jit(solution)/shard_map/ppermute | solution.py:336
  58.0 7.7 %collective-permute-start.16 = (bf16[8,128,128]{2,1,0:T(8,128)(2,1)S(1)}, bf16[8,128,128]{2,1,0:T(8,128)(2,1)S(1)}, u32[]{:S(2)}, u32[]{:S(2)}) collective-permute-start(bf16[8,128,128]{2,1,0:T(8,128)(2,1)S(1)} %shard_map.84.refs_0_), channel_id=1, source_target_pairs={{0,2},{1,9},{2,4},{3,11},{4,6},{5,13},{6,0},{7,15},{8,10},{9,17},{... | collective-permute-start | bytes 786440 | tf_op jit(solution)/shard_map/ppermute | solution.py:336
  60.2 9.2 %collective-permute-start.15 = (bf16[8,128,128]{2,1,0:T(8,128)(2,1)S(1)}, bf16[8,128,128]{2,1,0:T(8,128)(2,1)S(1)}, u32[]{:S(2)}, u32[]{:S(2)}) collective-permute-start(bf16[8,128,128]{2,1,0:T(8,128)(2,1)S(1)} %shard_map.84.refs_0_), channel_id=1, source_target_pairs={{0,4},{1,17},{2,6},{3,19},{4,0},{5,21},{6,2},{7,23},{8,12},{9,25},... | collective-permute-start | bytes 786440 | tf_op jit(solution)/shard_map/ppermute | solution.py:336
  74.8 25.0 %collective-permute-start.21 = (bf16[8,128,128]{2,1,0:T(8,128)(2,1)S(1)}, bf16[8,128,128]{2,1,0:T(8,128)(2,1)S(1)}, u32[]{:S(2)}, u32[]{:S(2)}) collective-permute-start(bf16[8,128,128]{2,1,0:T(8,128)(2,1)S(1)} %get-tuple-element.67), channel_id=1, source_target_pairs={{0,32},{32,64},{64,96},{96,0},{1,33},{33,65},{65,97},{97,1},{2,34}... | collective-permute-start | bytes 786440 | tf_op jit(solution)/shard_map/ppermute | solution.py:326
  76.5 23.3 %collective-permute-start.22 = (bf16[8,128,128]{2,1,0:T(8,128)(2,1)S(1)}, bf16[8,128,128]{2,1,0:T(8,128)(2,1)S(1)}, u32[]{:S(2)}, u32[]{:S(2)}) collective-permute-start(bf16[8,128,128]{2,1,0:T(8,128)(2,1)S(1)} %get-tuple-element.68), channel_id=1, source_target_pairs={{0,64},{32,96},{64,0},{96,32},{1,65},{33,97},{65,1},{97,33},{2,66}... | collective-permute-start | bytes 786440 | tf_op jit(solution)/shard_map/ppermute | solution.py:326
  80.0 19.9 %collective-permute-start.23 = (bf16[8,128,128]{2,1,0:T(8,128)(2,1)S(1)}, bf16[8,128,128]{2,1,0:T(8,128)(2,1)S(1)}, u32[]{:S(2)}, u32[]{:S(2)}) collective-permute-start(bf16[8,128,128]{2,1,0:T(8,128)(2,1)S(1)} %get-tuple-element.69), channel_id=1, source_target_pairs={{0,96},{32,0},{64,32},{96,64},{1,97},{33,1},{65,33},{97,65},{2,98}... | collective-permute-start | bytes 786440 | tf_op jit(solution)/shard_map/ppermute | solution.py:326
  80.9 7.7 %collective-permute-start.24 = (bf16[32,128]{1,0:T(8,128)(2,1)S(1)}, bf16[32,128]{1,0:T(8,128)(2,1)S(1)}, u32[]{:S(2)}, u32[]{:S(2)}) collective-permute-start(bf16[32,128]{1,0:T(8,128)(2,1)S(1)} %get-tuple-element.71), channel_id=1, source_target_pairs={{0,32},{32,64},{64,96},{96,0},{1,33},{33,65},{65,97},{97,1},{2,34}... | collective-permute-start | bytes 24584 | tf_op jit(solution)/shard_map/ppermute | solution.py:326
  82.0 9.9 %collective-permute-start.25 = (bf16[32,128]{1,0:T(8,128)(2,1)S(1)}, bf16[32,128]{1,0:T(8,128)(2,1)S(1)}, u32[]{:S(2)}, u32[]{:S(2)}) collective-permute-start(bf16[32,128]{1,0:T(8,128)(2,1)S(1)} %get-tuple-element.72), channel_id=1, source_target_pairs={{0,64},{32,96},{64,0},{96,32},{1,65},{33,97},{65,1},{97,33},{2,66}... | collective-permute-start | bytes 24584 | tf_op jit(solution)/shard_map/ppermute | solution.py:326
  100.9 9.9 %collective-permute-start.31 = (bf16[1024,128]{1,0:T(8,128)(2,1)S(1)}, bf16[1024,128]{1,0:T(8,128)(2,1)S(1)}, u32[]{:S(2)}, u32[]{:S(2)}) collective-permute-start(bf16[1024,128]{1,0:T(8,128)(2,1)S(1)} %get-tuple-element.75.p0), channel_id=1, source_target_pairs={{0,32},{32,64},{64,96},{96,0},{1,33},{33,65},{65,97},{97,1},{2,34}... | collective-permute-start | bytes 786440 | tf_op jit(solution)/shard_map/ppermute | solution.py:321
  102.5 15.1 %collective-permute-start.30 = (bf16[1024,128]{1,0:T(8,128)(2,1)S(1)}, bf16[1024,128]{1,0:T(8,128)(2,1)S(1)}, u32[]{:S(2)}, u32[]{:S(2)}) collective-permute-start(bf16[1024,128]{1,0:T(8,128)(2,1)S(1)} %get-tuple-element.75.p0), channel_id=1, source_target_pairs={{0,64},{32,96},{64,0},{96,32},{1,65},{33,97},{65,1},{97,33},{2,66}... | collective-permute-start | bytes 786440 | tf_op jit(solution)/shard_map/ppermute | solution.py:321
  106.0 11.6 %collective-permute-start.29 = (bf16[1024,128]{1,0:T(8,128)(2,1)S(1)}, bf16[1024,128]{1,0:T(8,128)(2,1)S(1)}, u32[]{:S(2)}, u32[]{:S(2)}) collective-permute-start(bf16[1024,128]{1,0:T(8,128)(2,1)S(1)} %get-tuple-element.75.p0), channel_id=1, source_target_pairs={{0,96},{32,0},{64,32},{96,64},{1,97},{33,1},{65,33},{97,65},{2,98}... | collective-permute-start | bytes 786440 | tf_op jit(solution)/shard_map/ppermute | solution.py:321
  124.9 7.7 %collective-permute-start.33 = (bf16[8,128,128]{2,1,0:T(8,128)(2,1)S(1)}, bf16[8,128,128]{2,1,0:T(8,128)(2,1)S(1)}, u32[]{:S(2)}, u32[]{:S(2)}) collective-permute-start(bf16[8,128,128]{2,1,0:T(8,128)(2,1)S(1)} %get-tuple-element.79), channel_id=1, source_target_pairs={{0,2},{1,9},{2,4},{3,11},{4,6},{5,13},{6,0},{7,15},{8,10},{9,17},{... | collective-permute-start | bytes 786440 | tf_op jit(solution)/shard_map/ppermute | solution.py:336
  125.4 10.5 %collective-permute-start.34 = (bf16[8,128,128]{2,1,0:T(8,128)(2,1)S(1)}, bf16[8,128,128]{2,1,0:T(8,128)(2,1)S(1)}, u32[]{:S(2)}, u32[]{:S(2)}) collective-permute-start(bf16[8,128,128]{2,1,0:T(8,128)(2,1)S(1)} %get-tuple-element.80), channel_id=1, source_target_pairs={{0,4},{1,17},{2,6},{3,19},{4,0},{5,21},{6,2},{7,23},{8,12},{9,25},... | collective-permute-start | bytes 786440 | tf_op jit(solution)/shard_map/ppermute | solution.py:336
  128.7 7.5 %collective-permute-start.35 = (bf16[8,128,128]{2,1,0:T(8,128)(2,1)S(1)}, bf16[8,128,128]{2,1,0:T(8,128)(2,1)S(1)}, u32[]{:S(2)}, u32[]{:S(2)}) collective-permute-start(bf16[8,128,128]{2,1,0:T(8,128)(2,1)S(1)} %get-tuple-element.81), channel_id=1, source_target_pairs={{0,6},{1,25},{2,0},{3,27},{4,2},{5,29},{6,4},{7,31},{8,14},{9,1},{... | collective-permute-start | bytes 786440 | tf_op jit(solution)/shard_map/ppermute | solution.py:336
  137.8 8.0 %collective-permute-start.37 = (bf16[8,128,128]{2,1,0:T(8,128)(2,1)S(1)}, bf16[8,128,128]{2,1,0:T(8,128)(2,1)S(1)}, u32[]{:S(2)}, u32[]{:S(2)}) collective-permute-start(bf16[8,128,128]{2,1,0:T(8,128)(2,1)S(1)} %get-tuple-element.83), channel_id=1, source_target_pairs={{0,16},{1,5},{2,18},{3,7},{4,20},{5,1},{6,22},{7,3},{8,24},{9,13},... | collective-permute-start | bytes 786440 | tf_op jit(solution)/shard_map/ppermute | solution.py:336
  138.3 10.2 %collective-permute-start.36 = (bf16[8,128,128]{2,1,0:T(8,128)(2,1)S(1)}, bf16[8,128,128]{2,1,0:T(8,128)(2,1)S(1)}, u32[]{:S(2)}, u32[]{:S(2)}) collective-permute-start(bf16[8,128,128]{2,1,0:T(8,128)(2,1)S(1)} %get-tuple-element.83), channel_id=1, source_target_pairs={{0,8},{1,3},{2,10},{3,5},{4,12},{5,7},{6,14},{7,1},{8,16},{9,11},{... | collective-permute-start | bytes 786440 | tf_op jit(solution)/shard_map/ppermute | solution.py:336
  148.7 7.7 %collective-permute-start.41 = (bf16[8,128,128]{2,1,0:T(8,128)(2,1)S(1)}, bf16[8,128,128]{2,1,0:T(8,128)(2,1)S(1)}, u32[]{:S(2)}, u32[]{:S(2)}) collective-permute-start(bf16[8,128,128]{2,1,0:T(8,128)(2,1)S(1)} %shard_map.91.refs_0_), channel_id=1, source_target_pairs={{0,2},{1,9},{2,4},{3,11},{4,6},{5,13},{6,0},{7,15},{8,10},{9,17},{... | collective-permute-start | bytes 786440 | tf_op jit(solution)/shard_map/ppermute | solution.py:336
  149.5 10.5 %collective-permute-start.40 = (bf16[8,128,128]{2,1,0:T(8,128)(2,1)S(1)}, bf16[8,128,128]{2,1,0:T(8,128)(2,1)S(1)}, u32[]{:S(2)}, u32[]{:S(2)}) collective-permute-start(bf16[8,128,128]{2,1,0:T(8,128)(2,1)S(1)} %shard_map.91.refs_0_), channel_id=1, source_target_pairs={{0,4},{1,17},{2,6},{3,19},{4,0},{5,21},{6,2},{7,23},{8,12},{9,25},... | collective-permute-start | bytes 786440 | tf_op jit(solution)/shard_map/ppermute | solution.py:336
  152.9 7.2 %collective-permute-start.39 = (bf16[8,128,128]{2,1,0:T(8,128)(2,1)S(1)}, bf16[8,128,128]{2,1,0:T(8,128)(2,1)S(1)}, u32[]{:S(2)}, u32[]{:S(2)}) collective-permute-start(bf16[8,128,128]{2,1,0:T(8,128)(2,1)S(1)} %shard_map.91.refs_0_), channel_id=1, source_target_pairs={{0,6},{1,25},{2,0},{3,27},{4,2},{5,29},{6,4},{7,31},{8,14},{9,1},{... | collective-permute-start | bytes 786440 | tf_op jit(solution)/shard_map/ppermute | solution.py:336
  153.1 7.4 %collective-permute-start.42 = (bf16[8,128,128]{2,1,0:T(8,128)(2,1)S(1)}, bf16[8,128,128]{2,1,0:T(8,128)(2,1)S(1)}, u32[]{:S(2)}, u32[]{:S(2)}) collective-permute-start(bf16[8,128,128]{2,1,0:T(8,128)(2,1)S(1)} %shard_map.91.refs_0_), channel_id=1, source_target_pairs={{0,1},{1,0},{2,3},{3,2},{4,5},{5,4},{6,7},{7,6},{8,9},{9,8},{10,11... | collective-permute-start | bytes 786440 | tf_op jit(solution)/shard_map/ppermute | solution.py:326
  165.5 22.8 %collective-permute-start.46 = (bf16[8,128,128]{2,1,0:T(8,128)(2,1)S(1)}, bf16[8,128,128]{2,1,0:T(8,128)(2,1)S(1)}, u32[]{:S(2)}, u32[]{:S(2)}) collective-permute-start(bf16[8,128,128]{2,1,0:T(8,128)(2,1)S(1)} %get-tuple-element.85), channel_id=1, source_target_pairs={{0,32},{32,64},{64,96},{96,0},{1,33},{33,65},{65,97},{97,1},{2,34}... | collective-permute-start | bytes 786440 | tf_op jit(solution)/shard_map/ppermute | solution.py:326
  167.5 20.8 %collective-permute-start.47 = (bf16[8,128,128]{2,1,0:T(8,128)(2,1)S(1)}, bf16[8,128,128]{2,1,0:T(8,128)(2,1)S(1)}, u32[]{:S(2)}, u32[]{:S(2)}) collective-permute-start(bf16[8,128,128]{2,1,0:T(8,128)(2,1)S(1)} %get-tuple-element.86), channel_id=1, source_target_pairs={{0,64},{32,96},{64,0},{96,32},{1,65},{33,97},{65,1},{97,33},{2,66}... | collective-permute-start | bytes 786440 | tf_op jit(solution)/shard_map/ppermute | solution.py:326
  171.3 17.0 %collective-permute-start.48 = (bf16[8,128,128]{2,1,0:T(8,128)(2,1)S(1)}, bf16[8,128,128]{2,1,0:T(8,128)(2,1)S(1)}, u32[]{:S(2)}, u32[]{:S(2)}) collective-permute-start(bf16[8,128,128]{2,1,0:T(8,128)(2,1)S(1)} %get-tuple-element.87), channel_id=1, source_target_pairs={{0,96},{32,0},{64,32},{96,64},{1,97},{33,1},{65,33},{97,65},{2,98}... | collective-permute-start | bytes 786440 | tf_op jit(solution)/shard_map/ppermute | solution.py:326
  171.4 11.3 %collective-permute-start.49 = (bf16[32,128]{1,0:T(8,128)(2,1)S(1)}, bf16[32,128]{1,0:T(8,128)(2,1)S(1)}, u32[]{:S(2)}, u32[]{:S(2)}) collective-permute-start(bf16[32,128]{1,0:T(8,128)(2,1)S(1)} %get-tuple-element.89), channel_id=1, source_target_pairs={{0,32},{32,64},{64,96},{96,0},{1,33},{33,65},{65,97},{97,1},{2,34}... | collective-permute-start | bytes 24584 | tf_op jit(solution)/shard_map/ppermute | solution.py:326
  173.4 9.9 %collective-permute-start.50 = (bf16[32,128]{1,0:T(8,128)(2,1)S(1)}, bf16[32,128]{1,0:T(8,128)(2,1)S(1)}, u32[]{:S(2)}, u32[]{:S(2)}) collective-permute-start(bf16[32,128]{1,0:T(8,128)(2,1)S(1)} %get-tuple-element.90), channel_id=1, source_target_pairs={{0,64},{32,96},{64,0},{96,32},{1,65},{33,97},{65,1},{97,33},{2,66}... | collective-permute-start | bytes 24584 | tf_op jit(solution)/shard_map/ppermute | solution.py:326
  (22 other events, 92.5 us)

commit v4 on v3

--- a/solution.py
+++ b/solution.py
@@ -11,7 +11,8 @@
 LEVELS = 5
 ITERS = 2
 TILE = 128
-GROUP = 64
+FWD_GROUP = 48
+BWD_GROUP = 64
 CHUNK = 16
 ROW_BLOCKS = 64
 CELL_TILES = 32
@@ -83,13 +84,13 @@
     return first, second, step, 5 - step
 
 
-def tile_copies(jac, jbuf, sems, live):
+def tile_copies(jac, jbuf, sems, live, size):
     def copy(i):
         part = pl.ds(i * CHUNK, CHUNK)
         return pltpu.make_async_copy(jac.at[part], jbuf.at[part], sems.at[i])
 
-    groups = (live + GROUP - 1) // GROUP
-    per = GROUP // CHUNK
+    groups = (live + size - 1) // size
+    per = size // CHUNK
 
     for i in range(jac.shape[0] // CHUNK):
         @pl.when(i < groups * per)
@@ -144,17 +145,16 @@
     fix[...] = model[0:128, :]
 
 
-def first_kernel(table, f0, f1, f2, f3, *refs):
-    fwd_kernel(table, *refs, fixes=(f0, f1, f2, f3))
+def first_kernel(rows, cols, cnt, f0, f1, f2, f3, *refs):
+    fwd_kernel(rows, cols, cnt, *refs, fixes=(f0, f1, f2, f3))
 
 
 def fwd_kernel(
-    table, p0, p1, p2, p3, jac, keep, send, jbuf, model, acc, sems, fixes=None
+    rows, cols, cnt, p0, p1, p2, p3, jac, keep, send, jbuf, model, acc, sems, fixes=None
 ):
-    slots = jac.shape[0]
-    live = table[2 * slots]
+    live = cnt[0]
     core = lax.axis_index("core")
-    groups, arrive = tile_copies(jac, jbuf, sems, live)
+    groups, arrive = tile_copies(jac, jbuf, sems, live, FWD_GROUP)
     acc[...] = jnp.zeros(acc.shape, f32)
     for c in range(CELL_TILES):
         q, t = c // 8, c % 8
@@ -165,10 +165,10 @@
 
     def group(g, carry):
         arrive(g)
-        for v in range(GROUP):
-            s = g * GROUP + v
-            r = jnp.where(s < live, table[s], ROW_BLOCKS)
-            acc[r] += jnp.dot(jbuf[s], model[table[slots + s]], preferred_element_type=f32)
+        for v in range(FWD_GROUP):
+            s = g * FWD_GROUP + v
+            r = jnp.where(s < live, rows[s], ROW_BLOCKS)
+            acc[r] += jnp.dot(jbuf[s], model[cols[s]], preferred_element_type=f32)
         return carry
 
     lax.fori_loop(0, groups, group, 0)
@@ -216,11 +216,11 @@
 
 
 def bwd_kernel(table, *refs):
-    jac, g0, g1, g2, g3, e0, e1, e2, e3, jbuf, mis, acc, sems = refs[8:]
+    jac, g0, g1, g2, g3, edge, jbuf, mis, acc, sems = refs[8:]
     slots = jac.shape[0]
     live = table[2 * slots]
     core = lax.axis_index("core")
-    groups, arrive = tile_copies(jac, jbuf, sems, live)
+    groups, arrive = tile_copies(jac, jbuf, sems, live, BWD_GROUP)
     acc[...] = jnp.zeros(acc.shape, f32)
     for pieces, c in ((refs[0:4], core), (refs[4:8], 1 - core)):
         first, _, step, other = axes(c)
@@ -232,33 +232,35 @@
 
     def group(g, carry):
         arrive(g)
-        for v in range(GROUP):
-            s = g * GROUP + v
+        for v in range(BWD_GROUP):
+            s = g * BWD_GROUP + v
             c = jnp.where(s < live, table[slots + s], CELL_TILES)
             acc[c] += jnp.dot(mis[table[s]], jbuf[s], preferred_element_type=f32)
         return carry
 
     lax.fori_loop(0, groups, group, 0)
-    for k, out in enumerate((e0, e1, e2, e3)):
-        part = slice(32 * k, 32 * k + 32)
-        edge = jnp.where(lanes((32, 128)) < 64, acc[0, part, :], acc[CELL_TILES - 1, part, :])
-        out[...] = edge.astype(out.dtype)
+    edge[...] = jnp.where(lanes((128, 128)) < 64, acc[0], acc[CELL_TILES - 1]).astype(bf16)
     for k, out in enumerate((g0, g1, g2, g3)):
         for t in range(8):
             for q in range(4):
                 out[t, 32 * q : 32 * q + 32, :] = acc[8 * q + t, 32 * k : 32 * k + 32, :].astype(out.dtype)
 
 
-def edge_kernel(own, r1, r2, r3, edge):
-    edge[...] = own[...] + r1[...].astype(f32) + r2[...].astype(f32) + r3[...].astype(f32)
-
-
-def wave_update(own, r1, r2, r3, nxt, prv, state_in, state, ext, levels):
+def edge_kernel(nxt, prv, *out):
+    both = jnp.where(lanes((128, 128)) < 64, nxt[...], prv[...])
+    for k in range(4):
+        out[k][...] = both[32 * k : 32 * k + 32, :]
+
+
+def wave_update(own, r1, r2, r3, e0, e1, e2, e3, state_in, state, ext, levels):
     for i in range(8):
         s = own[i] + r1[i].astype(f32) + r2[i].astype(f32) + r3[i].astype(f32)
         ext[64 + 128 * i : 192 + 128 * i, :] = s.T
     ln = lanes((64, 128))
-    near = jnp.concatenate([prv[...], jnp.zeros((64, 128), f32), nxt[...]], axis=0).T
+    edge = e0[...].astype(f32)
+    for e in (e1, e2, e3):
+        edge += e[...].astype(f32)
+    near = jnp.concatenate([edge, jnp.zeros((64, 128), f32), edge], axis=0).T
     ext[0:64, :] = jnp.where(ln < 32, near[64:, :], pltpu.roll(ext[1024:1088, :], 32, 1))
     ext[1088:1152, :] = jnp.where(ln >= 96, near[:64, :], pltpu.roll(ext[64:128, :], 96, 1))
     ext[1152:1160, :] = jnp.zeros((8, 128), f32)
@@ -300,14 +302,16 @@
 
 
 def wave_kernel(
-    own, r1, r2, r3, nxt, prv, state_in, state, model, ext, l0, l1, l2, l3, *bufs
+    own, r1, r2, r3, e0, e1, e2, e3, state_in, state, model, ext, l0, l1, l2, l3, *bufs
 ):
-    wave_update(own, r1, r2, r3, nxt, prv, state_in, state, ext, (l0, l1, l2, l3))
+    wave_update(own, r1, r2, r3, e0, e1, e2, e3, state_in, state, ext, (l0, l1, l2, l3))
     synth_from(state, bufs, model)
 
 
-def last_kernel(own, r1, r2, r3, nxt, prv, state_in, out, state, ext, l0, l1, l2, l3):
-    wave_update(own, r1, r2, r3, nxt, prv, state_in, state, ext, (l0, l1, l2, l3))
+def last_kernel(
+    own, r1, r2, r3, e0, e1, e2, e3, state_in, out, state, ext, l0, l1, l2, l3
+):
+    wave_update(own, r1, r2, r3, e0, e1, e2, e3, state_in, state, ext, (l0, l1, l2, l3))
     for g in range(6):
         n = SEG_ROWS[g]
         base = SEG_OFF[g]
@@ -393,10 +397,10 @@
             fixes = [fix] + three([fix] * 3, pull)
         keep, send = call(
             fwd_kernel if sweep else first_kernel,
-            [SM] + [VM] * (4 + len(fixes)) + [ANY],
+            [SM] * 3 + [VM] * (4 + len(fixes)) + [ANY],
             [sds((32, 128, 128), f32), sds((32, 128, 128), bf16)],
             [jac_scratch, pltpu.VMEM((32, 128, 128), bf16), pltpu.VMEM((65, 128, 128), f32), sems],
-        )(table, *fixes, *pieces, jac)
+        )(rows, cols, cnt, *fixes, *pieces, jac)
         got = to_ahead(send, "core", 1)
         own, s1, s2, s3 = call(
             split_kernel, [VM, VM], [tiles, tiles_b, tiles_b, tiles_b]
@@ -411,29 +415,28 @@
             )
         mine = [rounded] + three([rounded] * 3, lambda a, k: by_core(a, 0, -k))
         other = [to_ahead(m, "core", 1) for m in mine]
-        edge, edge_b = sds((32, 128), f32), sds((32, 128), bf16)
-        g0, g1, g2, g3, e0, e1, e2, e3 = call(
+        g0, g1, g2, g3, edge = call(
             bwd_kernel,
             [SM] + [VM] * 8 + [ANY],
-            [tiles, tiles_b, tiles_b, tiles_b, edge, edge_b, edge_b, edge_b],
+            [tiles, tiles_b, tiles_b, tiles_b, sds((128, 128), bf16)],
             [jac_scratch, pltpu.VMEM((64, 128, 128), bf16), pltpu.VMEM((33, 128, 128), f32), sems],
         )(table, *mine, *other, jac)
-        r = three((e1, e2, e3), push)
-        (near,) = call(edge_kernel, [VM] * 4, [edge])(e0, *r)
-        nxt = along(near, -1)
-        prv = along(near, 1) if sweep < ITERS - 1 else near
         r = three((g1, g2, g3), push)
+        nxt = along(edge, -1)
+        prv = along(edge, 1) if sweep < ITERS - 1 else edge
+        e0, *es = call(edge_kernel, [VM] * 2, [sds((32, 128), bf16)] * 4)(nxt, prv)
+        es = [e0] + three(es, push)
         if sweep < ITERS - 1:
             state, model = call(
-                wave_kernel, [VM] * 7, [sds((STATE_ROWS, 128), f32), flat_b], WAVE_BUFS + SYNTH_BUFS
-            )(g0, *r, nxt, prv, state)
+                wave_kernel, [VM] * 9, [sds((STATE_ROWS, 128), f32), flat_b], WAVE_BUFS + SYNTH_BUFS
+            )(g0, *r, *es, state)
         else:
             (coeffs,) = call(
                 last_kernel,
-                [VM] * 7,
+                [VM] * 9,
                 [sds((32, 4096), f32)],
                 [pltpu.VMEM((STATE_ROWS, 128), f32)] + WAVE_BUFS,
-            )(g0, *r, nxt, prv, state)
+            )(g0, *r, *es, state)
     return (coeffs.T, share)
 
 

time: 191 us -> 185 us (0.969)
  starting transfers between devices: 70.8 us -> 66.1 us
  waiting for transfers between devices: 92.5 us -> 90.2 us
    ppermute x4, waiting for transfers between devices: 8.69 us -> 14.8 us  [along(): return lax.ppermute(x, MP, [(i, (i + by) % 32) for i in range(32)])]
    ppermute x9, waiting for transfers between devices: 16.6 us -> 10.7 us  [from_ahead(): return lax.ppermute(x, axis, [(i, (i - by) % n) for i in range(n)])]
    ppermute x22, waiting for transfers between devices: 27.7 us -> 21.9 us  [to_ahead(): return lax.ppermute(x, axis, [(i, (i + by) % n) for i in range(n)])]
    ppermute x22, starting transfers between devices: 21.1 us -> 17 us  [to_ahead(): return lax.ppermute(x, axis, [(i, (i + by) % n) for i in range(n)])]
    ppermute x18, waiting for transfers between devices: 39.5 us -> 42.7 us  [by_core(): return lax.ppermute(x, MP, pairs)]
  transfers between devices with their start and end apart: 53 -> 53, of which waited for: 33 -> 32; matrix products, arithmetic and copies ran while one was open for 1% -> 1% of each run, Pallas kernels for 1% -> 1%
where the time goes in v4:
time: 185 us; the launch traced here: 182 us
  waiting for transfers between devices  90.2 us (49%)
  starting transfers between devices  66.1 us (36%)
  Pallas kernels  21.1 us (11%)
  local copies, waits for them, and re-layouts  2.11 us (1%)
    ppermute x18, waiting for transfers between devices, by_core(): return lax.ppermute(x, MP, pairs)  42.7 us
    ppermute x18, starting transfers between devices, by_core(): return lax.ppermute(x, MP, pairs)  31.2 us
    ppermute x22, waiting for transfers between devices, to_ahead(): return lax.ppermute(x, axis, [(i, (i + by) % n) for i in range(n)])  21.9 us
    ppermute x22, starting transfers between devices, to_ahead(): return lax.ppermute(x, axis, [(i, (i + by) % n) for i in range(n)])  17 us
    ppermute x4, waiting for transfers between devices, along(): return lax.ppermute(x, MP, [(i, (i + by) % 32) for i in range(32)])  14.8 us
    ppermute x9, starting transfers between devices, from_ahead(): return lax.ppermute(x, axis, [(i, (i - by) % n) for i in range(n)])  13.3 us
    ppermute x9, waiting for transfers between devices, from_ahead(): return lax.ppermute(x, axis, [(i, (i - by) % n) for i in range(n)])  10.7 us
    pallas_call x2, Pallas kernels, body(): call(fwd_kernel if sweep else first_kernel, [SM] * 3 + [VM] * (4 + len(fi...  7.87 us
  transfers between devices with their start and end apart: 53, of which 32 were waited for; matrix products, arithmetic and copies ran while one was open for 1% of the time, Pallas kernels for 1%

profile of v4, /device:TPU:0, one launch (start us, length us, event | category | flops | bytes accessed | tf_op | source)
XLA Modules:
  0.0 182.4 jit_solution(6363453021328116953)
XLA Ops:
  2.7 3.2 %collective-permute-start.4 = (bf16[1024,128]{1,0:T(8,128)(2,1)S(1)}, bf16[1024,128]{1,0:T(8,128)(2,1)S(1)}, u32[]{:S(2)}, u32[]{:S(2)}) collective-permute-start(bf16[1024,128]{1,0:T(8,128)(2,1)S(1)} %shard_map.79.refs_0_), channel_id=1, source_target_pairs={{0,96},{32,0},{64,32},{96,64},{1,97},{33,1},{65,33},{97,65},{2,98}... | collective-permute-start | bytes 786440 | tf_op jit(solution)/shard_map/ppermute | solution.py:325
  7.5 6.6 %collective-permute-done.recv = f32[48,128]{1,0:T(8,128)S(1)} collective-permute-done((f32[48,128]{1,0:T(8,128)S(1)}, f32[48,128]{1,0:T(8,128)S(1)}, u32[]{:S(2)}, u32[]{:S(2)}) %collective-permute-start) | collective-permute-done | bytes 24608 | tf_op jit(solution)/shard_map/ppermute | solution.py:354
  23.9 3.9 %shard_map.80 = (f32[32,128,128]{2,1,0:T(8,128)S(1)}, bf16[32,128,128]{2,1,0:T(8,128)(2,1)S(1)}) custom-call(s32[384]{0:T(512)S(1)} %reduce.rows, s32[384]{0:T(512)S(1)} %reduce.1.cols, s32[1]{0:T(128)} %bitcast.10.cnt, bf16[128,128]{1,0:T(8,128)(2,1)S(1)} %get-tuple-element.59.f0, bf16[128,128]{1,0:T(8,128)(2,1)S(1)} %collective-permute-done.1.f1, ...), custom_call_target="tpu_custom_call" | custom-call | tf_op jit(solution)/shard_map/pallas_call | solution.py:398
  28.0 2.6 %collective-permute-done.7.recv = bf16[32,128,128]{2,1,0:T(8,128)(2,1)S(1)} collective-permute-done((bf16[32,128,128]{2,1,0:T(8,128)(2,1)S(1)}, bf16[32,128,128]{2,1,0:T(8,128)(2,1)S(1)}, u32[]{:S(2)}, u32[]{:S(2)}) %collective-permute-start.7) | collective-permute-done | bytes 1048608 | tf_op jit(solution)/shard_map/ppermute | solution.py:330
  30.8 4.9 %collective-permute-start.10 = (bf16[8,128,128]{2,1,0:T(8,128)(2,1)S(1)}, bf16[8,128,128]{2,1,0:T(8,128)(2,1)S(1)}, u32[]{:S(2)}, u32[]{:S(2)}) collective-permute-start(bf16[8,128,128]{2,1,0:T(8,128)(2,1)S(1)} %get-tuple-element.65), channel_id=1, source_target_pairs={{0,6},{1,25},{2,0},{3,27},{4,2},{5,29},{6,4},{7,31},{8,14},{9,1},{... | collective-permute-start | bytes 786440 | tf_op jit(solution)/shard_map/ppermute | solution.py:340
  39.6 6.5 %collective-permute-done.8.r1 = bf16[8,128,128]{2,1,0:T(8,128)(2,1)S(1)} collective-permute-done((bf16[8,128,128]{2,1,0:T(8,128)(2,1)S(1)}, bf16[8,128,128]{2,1,0:T(8,128)(2,1)S(1)}, u32[]{:S(2)}, u32[]{:S(2)}) %collective-permute-start.8) | collective-permute-done | bytes 262176 | tf_op jit(solution)/shard_map/ppermute | solution.py:340
  47.1 2.7 %collective-permute-start.12 = (bf16[8,128,128]{2,1,0:T(8,128)(2,1)S(1)}, bf16[8,128,128]{2,1,0:T(8,128)(2,1)S(1)}, u32[]{:S(2)}, u32[]{:S(2)}) collective-permute-start(bf16[8,128,128]{2,1,0:T(8,128)(2,1)S(1)} %get-tuple-element.67), channel_id=1, source_target_pairs={{0,16},{1,5},{2,18},{3,7},{4,20},{5,1},{6,22},{7,3},{8,24},{9,13},... | collective-permute-start | bytes 786440 | tf_op jit(solution)/shard_map/ppermute | solution.py:340
  53.9 3.1 %collective-permute-done.12.r2 = bf16[8,128,128]{2,1,0:T(8,128)(2,1)S(1)} collective-permute-done((bf16[8,128,128]{2,1,0:T(8,128)(2,1)S(1)}, bf16[8,128,128]{2,1,0:T(8,128)(2,1)S(1)}, u32[]{:S(2)}, u32[]{:S(2)}) %collective-permute-start.12) | collective-permute-done | bytes 262176 | tf_op jit(solution)/shard_map/ppermute | solution.py:340
  59.8 4.3 %collective-permute-done.14.refs_1_ = bf16[8,128,128]{2,1,0:T(8,128)(2,1)S(1)} collective-permute-done((bf16[8,128,128]{2,1,0:T(8,128)(2,1)S(1)}, bf16[8,128,128]{2,1,0:T(8,128)(2,1)S(1)}, u32[]{:S(2)}, u32[]{:S(2)}) %collective-permute-start.14) | collective-permute-done | bytes 262176 | tf_op jit(solution)/shard_map/ppermute | solution.py:340
  66.5 2.7 %collective-permute-done.16.refs_3_ = bf16[8,128,128]{2,1,0:T(8,128)(2,1)S(1)} collective-permute-done((bf16[8,128,128]{2,1,0:T(8,128)(2,1)S(1)}, bf16[8,128,128]{2,1,0:T(8,128)(2,1)S(1)}, u32[]{:S(2)}, u32[]{:S(2)}) %collective-permute-start.16) | collective-permute-done | bytes 262176 | tf_op jit(solution)/shard_map/ppermute | solution.py:340
  70.8 3.5 %shard_map.85 = (f32[8,128,128]{2,1,0:T(8,128)S(1)}, bf16[8,128,128]{2,1,0:T(8,128)(2,1)S(1)}, bf16[8,128,128]{2,1,0:T(8,128)(2,1)S(1)}, bf16[8,128,128]{2,1,0:T(8,128)(2,1)S(1)}, bf16[128,128]{1,0:T(8,128)(2,1)S(1)}) custom-call(s32[769]{0:T(1024)S(1)} %pad_add_fusion.table, bf16[8,128,128]{2,1,0:T(8,128)(2,1)S(1)} %shard_map.84.refs_0_, ...), custom_call_target="tpu_custom_call" | custom-call | tf_op jit(solution)/shard_map/pallas_call | solution.py:418
  75.5 4.7 %collective-permute-start.22 = (bf16[8,128,128]{2,1,0:T(8,128)(2,1)S(1)}, bf16[8,128,128]{2,1,0:T(8,128)(2,1)S(1)}, u32[]{:S(2)}, u32[]{:S(2)}) collective-permute-start(bf16[8,128,128]{2,1,0:T(8,128)(2,1)S(1)} %get-tuple-element.70), channel_id=1, source_target_pairs={{0,64},{32,96},{64,0},{96,32},{1,65},{33,97},{65,1},{97,33},{2,66}... | collective-permute-start | bytes 786440 | tf_op jit(solution)/shard_map/ppermute | solution.py:330
  81.1 2.6 %collective-permute-start.24 = (bf16[128,128]{1,0:T(8,128)(2,1)S(1)}, bf16[128,128]{1,0:T(8,128)(2,1)S(1)}, u32[]{:S(2)}, u32[]{:S(2)}) collective-permute-start(bf16[128,128]{1,0:T(8,128)(2,1)S(1)} %get-tuple-element.72), channel_id=1, source_target_pairs={{0,31},{1,0},{2,1},{3,2},{4,3},{5,4},{6,5},{7,6},{8,7},{9,8},{10,9... | collective-permute-start | bytes 98312 | tf_op jit(solution)/shard_map/ppermute | solution.py:354
  85.3 5.1 %collective-permute-done.25.prv = bf16[128,128]{1,0:T(8,128)(2,1)S(1)} collective-permute-done((bf16[128,128]{1,0:T(8,128)(2,1)S(1)}, bf16[128,128]{1,0:T(8,128)(2,1)S(1)}, u32[]{:S(2)}, u32[]{:S(2)}) %collective-permute-start.25) | collective-permute-done | bytes 32800 | tf_op jit(solution)/shard_map/ppermute | solution.py:354
  92.5 2.8 %collective-permute-done.26.e1 = bf16[32,128]{1,0:T(8,128)(2,1)S(1)} collective-permute-done((bf16[32,128]{1,0:T(8,128)(2,1)S(1)}, bf16[32,128]{1,0:T(8,128)(2,1)S(1)}, u32[]{:S(2)}, u32[]{:S(2)}) %collective-permute-start.26) | collective-permute-done | bytes 8224 | tf_op jit(solution)/shard_map/ppermute | solution.py:330
  102.8 3.8 %collective-permute-done.29.p1 = bf16[1024,128]{1,0:T(8,128)(2,1)S(1)} collective-permute-done((bf16[1024,128]{1,0:T(8,128)(2,1)S(1)}, bf16[1024,128]{1,0:T(8,128)(2,1)S(1)}, u32[]{:S(2)}, u32[]{:S(2)}) %collective-permute-start.29) | collective-permute-done | bytes 262176 | tf_op jit(solution)/shard_map/ppermute | solution.py:325
  106.6 2.8 %collective-permute-done.30.p2 = bf16[1024,128]{1,0:T(8,128)(2,1)S(1)} collective-permute-done((bf16[1024,128]{1,0:T(8,128)(2,1)S(1)}, bf16[1024,128]{1,0:T(8,128)(2,1)S(1)}, u32[]{:S(2)}, u32[]{:S(2)}) %collective-permute-start.30) | collective-permute-done | bytes 262176 | tf_op jit(solution)/shard_map/ppermute | solution.py:325
  109.4 2.7 %collective-permute-done.31.p3 = bf16[1024,128]{1,0:T(8,128)(2,1)S(1)} collective-permute-done((bf16[1024,128]{1,0:T(8,128)(2,1)S(1)}, bf16[1024,128]{1,0:T(8,128)(2,1)S(1)}, u32[]{:S(2)}, u32[]{:S(2)}) %collective-permute-start.31) | collective-permute-done | bytes 262176 | tf_op jit(solution)/shard_map/ppermute | solution.py:325
  112.1 3.9 %shard_map.88 = (f32[32,128,128]{2,1,0:T(8,128)S(1)}, bf16[32,128,128]{2,1,0:T(8,128)(2,1)S(1)}) custom-call(s32[384]{0:T(512)S(1)} %reduce.rows, s32[384]{0:T(512)S(1)} %reduce.1.cols, s32[1]{0:T(128)} %bitcast.11.cnt, bf16[1024,128]{1,0:T(8,128)(2,1)S(1)} %get-tuple-element.78.p0, bf16[1024,128]{1,0:T(8,128)(2,1)S(1)} %collective-permute-done.29.p1, ...), custom_call_target="tpu_custom_call" | custom-call | tf_op jit(solution)/shard_map/pallas_call | solution.py:398
  116.1 2.6 %collective-permute-done.32.recv = bf16[32,128,128]{2,1,0:T(8,128)(2,1)S(1)} collective-permute-done((bf16[32,128,128]{2,1,0:T(8,128)(2,1)S(1)}, bf16[32,128,128]{2,1,0:T(8,128)(2,1)S(1)}, u32[]{:S(2)}, u32[]{:S(2)}) %collective-permute-start.32) | collective-permute-done | bytes 1048608 | tf_op jit(solution)/shard_map/ppermute | solution.py:330
  119.0 3.8 %collective-permute-start.34 = (bf16[8,128,128]{2,1,0:T(8,128)(2,1)S(1)}, bf16[8,128,128]{2,1,0:T(8,128)(2,1)S(1)}, u32[]{:S(2)}, u32[]{:S(2)}) collective-permute-start(bf16[8,128,128]{2,1,0:T(8,128)(2,1)S(1)} %get-tuple-element.83), channel_id=1, source_target_pairs={{0,4},{1,17},{2,6},{3,19},{4,0},{5,21},{6,2},{7,23},{8,12},{9,25},... | collective-permute-start | bytes 786440 | tf_op jit(solution)/shard_map/ppermute | solution.py:340
  122.8 3.8 %collective-permute-done.33.r1 = bf16[8,128,128]{2,1,0:T(8,128)(2,1)S(1)} collective-permute-done((bf16[8,128,128]{2,1,0:T(8,128)(2,1)S(1)}, bf16[8,128,128]{2,1,0:T(8,128)(2,1)S(1)}, u32[]{:S(2)}, u32[]{:S(2)}) %collective-permute-start.33) | collective-permute-done | bytes 262176 | tf_op jit(solution)/shard_map/ppermute | solution.py:340
  126.6 3.3 %collective-permute-done.34.r2 = bf16[8,128,128]{2,1,0:T(8,128)(2,1)S(1)} collective-permute-done((bf16[8,128,128]{2,1,0:T(8,128)(2,1)S(1)}, bf16[8,128,128]{2,1,0:T(8,128)(2,1)S(1)}, u32[]{:S(2)}, u32[]{:S(2)}) %collective-permute-start.34) | collective-permute-done | bytes 262176 | tf_op jit(solution)/shard_map/ppermute | solution.py:340
  130.4 3.2 %collective-permute-start.36 = (bf16[8,128,128]{2,1,0:T(8,128)(2,1)S(1)}, bf16[8,128,128]{2,1,0:T(8,128)(2,1)S(1)}, u32[]{:S(2)}, u32[]{:S(2)}) collective-permute-start(bf16[8,128,128]{2,1,0:T(8,128)(2,1)S(1)} %get-tuple-element.86), channel_id=1, source_target_pairs={{0,8},{1,3},{2,10},{3,5},{4,12},{5,7},{6,14},{7,1},{8,16},{9,11},{... | collective-permute-start | bytes 786440 | tf_op jit(solution)/shard_map/ppermute | solution.py:340
  136.1 2.5 %collective-permute-start.38 = (bf16[8,128,128]{2,1,0:T(8,128)(2,1)S(1)}, bf16[8,128,128]{2,1,0:T(8,128)(2,1)S(1)}, u32[]{:S(2)}, u32[]{:S(2)}) collective-permute-start(bf16[8,128,128]{2,1,0:T(8,128)(2,1)S(1)} %get-tuple-element.86), channel_id=1, source_target_pairs={{0,24},{1,7},{2,26},{3,1},{4,28},{5,3},{6,30},{7,5},{8,0},{9,15},{... | collective-permute-start | bytes 786440 | tf_op jit(solution)/shard_map/ppermute | solution.py:340
  138.6 4.5 %collective-permute-done.37.r2 = bf16[8,128,128]{2,1,0:T(8,128)(2,1)S(1)} collective-permute-done((bf16[8,128,128]{2,1,0:T(8,128)(2,1)S(1)}, bf16[8,128,128]{2,1,0:T(8,128)(2,1)S(1)}, u32[]{:S(2)}, u32[]{:S(2)}) %collective-permute-start.37) | collective-permute-done | bytes 262176 | tf_op jit(solution)/shard_map/ppermute | solution.py:340
  143.4 2.7 %collective-permute-start.39 = (bf16[8,128,128]{2,1,0:T(8,128)(2,1)S(1)}, bf16[8,128,128]{2,1,0:T(8,128)(2,1)S(1)}, u32[]{:S(2)}, u32[]{:S(2)}) collective-permute-start(bf16[8,128,128]{2,1,0:T(8,128)(2,1)S(1)} %shard_map.91.refs_0_), channel_id=1, source_target_pairs={{0,6},{1,25},{2,0},{3,27},{4,2},{5,29},{6,4},{7,31},{8,14},{9,1},{... | collective-permute-start | bytes 786440 | tf_op jit(solution)/shard_map/ppermute | solution.py:340
  147.1 5.8 %collective-permute-done.39.refs_1_ = bf16[8,128,128]{2,1,0:T(8,128)(2,1)S(1)} collective-permute-done((bf16[8,128,128]{2,1,0:T(8,128)(2,1)S(1)}, bf16[8,128,128]{2,1,0:T(8,128)(2,1)S(1)}, u32[]{:S(2)}, u32[]{:S(2)}) %collective-permute-start.39) | collective-permute-done | bytes 262176 | tf_op jit(solution)/shard_map/ppermute | solution.py:340
  158.0 3.5 %shard_map.92 = (f32[8,128,128]{2,1,0:T(8,128)S(1)}, bf16[8,128,128]{2,1,0:T(8,128)(2,1)S(1)}, bf16[8,128,128]{2,1,0:T(8,128)(2,1)S(1)}, bf16[8,128,128]{2,1,0:T(8,128)(2,1)S(1)}, bf16[128,128]{1,0:T(8,128)(2,1)S(1)}) custom-call(s32[769]{0:T(1024)S(1)} %pad_add_fusion.table, bf16[8,128,128]{2,1,0:T(8,128)(2,1)S(1)} %shard_map.91.refs_0_, ...), custom_call_target="tpu_custom_call" | custom-call | tf_op jit(solution)/shard_map/pallas_call | solution.py:418
  162.9 2.5 %collective-permute-start.47 = (bf16[8,128,128]{2,1,0:T(8,128)(2,1)S(1)}, bf16[8,128,128]{2,1,0:T(8,128)(2,1)S(1)}, u32[]{:S(2)}, u32[]{:S(2)}) collective-permute-start(bf16[8,128,128]{2,1,0:T(8,128)(2,1)S(1)} %get-tuple-element.89), channel_id=1, source_target_pairs={{0,64},{32,96},{64,0},{96,32},{1,65},{33,97},{65,1},{97,33},{2,66}... | collective-permute-start | bytes 786440 | tf_op jit(solution)/shard_map/ppermute | solution.py:330
  172.7 4.5 %collective-permute-done.50.e1 = bf16[32,128]{1,0:T(8,128)(2,1)S(1)} collective-permute-done((bf16[32,128]{1,0:T(8,128)(2,1)S(1)}, bf16[32,128]{1,0:T(8,128)(2,1)S(1)}, u32[]{:S(2)}, u32[]{:S(2)}) %collective-permute-start.50) | collective-permute-done | bytes 8224 | tf_op jit(solution)/shard_map/ppermute | solution.py:330
  178.2 2.6 %collective-permute-done.52.e3 = bf16[32,128]{1,0:T(8,128)(2,1)S(1)} collective-permute-done((bf16[32,128]{1,0:T(8,128)(2,1)S(1)}, bf16[32,128]{1,0:T(8,128)(2,1)S(1)}, u32[]{:S(2)}, u32[]{:S(2)}) %collective-permute-start.52) | collective-permute-done | bytes 8224 | tf_op jit(solution)/shard_map/ppermute | solution.py:330
  (100 shorter events, 64.0 us)
Async XLA Ops:
  2.7 21.2 %collective-permute-start.4 = (bf16[1024,128]{1,0:T(8,128)(2,1)S(1)}, bf16[1024,128]{1,0:T(8,128)(2,1)S(1)}, u32[]{:S(2)}, u32[]{:S(2)}) collective-permute-start(bf16[1024,128]{1,0:T(8,128)(2,1)S(1)} %shard_map.79.refs_0_), channel_id=1, source_target_pairs={{0,96},{32,0},{64,32},{96,64},{1,97},{33,1},{65,33},{97,65},{2,98}... | collective-permute-start | bytes 786440 | tf_op jit(solution)/shard_map/ppermute | solution.py:325
  5.9 18.0 %collective-permute-start.5 = (bf16[1024,128]{1,0:T(8,128)(2,1)S(1)}, bf16[1024,128]{1,0:T(8,128)(2,1)S(1)}, u32[]{:S(2)}, u32[]{:S(2)}) collective-permute-start(bf16[1024,128]{1,0:T(8,128)(2,1)S(1)} %shard_map.79.refs_0_), channel_id=1, source_target_pairs={{0,64},{32,96},{64,0},{96,32},{1,65},{33,97},{65,1},{97,33},{2,66}... | collective-permute-start | bytes 786440 | tf_op jit(solution)/shard_map/ppermute | solution.py:325
  6.5 17.4 %collective-permute-start.6 = (bf16[1024,128]{1,0:T(8,128)(2,1)S(1)}, bf16[1024,128]{1,0:T(8,128)(2,1)S(1)}, u32[]{:S(2)}, u32[]{:S(2)}) collective-permute-start(bf16[1024,128]{1,0:T(8,128)(2,1)S(1)} %shard_map.79.refs_0_), channel_id=1, source_target_pairs={{0,32},{32,64},{64,96},{96,0},{1,33},{33,65},{65,97},{97,1},{2,34}... | collective-permute-start | bytes 786440 | tf_op jit(solution)/shard_map/ppermute | solution.py:325
  30.8 8.8 %collective-permute-start.10 = (bf16[8,128,128]{2,1,0:T(8,128)(2,1)S(1)}, bf16[8,128,128]{2,1,0:T(8,128)(2,1)S(1)}, u32[]{:S(2)}, u32[]{:S(2)}) collective-permute-start(bf16[8,128,128]{2,1,0:T(8,128)(2,1)S(1)} %get-tuple-element.65), channel_id=1, source_target_pairs={{0,6},{1,25},{2,0},{3,27},{4,2},{5,29},{6,4},{7,31},{8,14},{9,1},{... | collective-permute-start | bytes 786440 | tf_op jit(solution)/shard_map/ppermute | solution.py:340
  35.7 10.4 %collective-permute-start.8 = (bf16[8,128,128]{2,1,0:T(8,128)(2,1)S(1)}, bf16[8,128,128]{2,1,0:T(8,128)(2,1)S(1)}, u32[]{:S(2)}, u32[]{:S(2)}) collective-permute-start(bf16[8,128,128]{2,1,0:T(8,128)(2,1)S(1)} %get-tuple-element.63), channel_id=1, source_target_pairs={{0,2},{1,9},{2,4},{3,11},{4,6},{5,13},{6,0},{7,15},{8,10},{9,17},{... | collective-permute-start | bytes 786440 | tf_op jit(solution)/shard_map/ppermute | solution.py:340
  35.7 10.4 %collective-permute-start.9 = (bf16[8,128,128]{2,1,0:T(8,128)(2,1)S(1)}, bf16[8,128,128]{2,1,0:T(8,128)(2,1)S(1)}, u32[]{:S(2)}, u32[]{:S(2)}) collective-permute-start(bf16[8,128,128]{2,1,0:T(8,128)(2,1)S(1)} %get-tuple-element.64), channel_id=1, source_target_pairs={{0,4},{1,17},{2,6},{3,19},{4,0},{5,21},{6,2},{7,23},{8,12},{9,25},... | collective-permute-start | bytes 786440 | tf_op jit(solution)/shard_map/ppermute | solution.py:340
  46.2 7.7 %collective-permute-start.11 = (bf16[8,128,128]{2,1,0:T(8,128)(2,1)S(1)}, bf16[8,128,128]{2,1,0:T(8,128)(2,1)S(1)}, u32[]{:S(2)}, u32[]{:S(2)}) collective-permute-start(bf16[8,128,128]{2,1,0:T(8,128)(2,1)S(1)} %get-tuple-element.67), channel_id=1, source_target_pairs={{0,8},{1,3},{2,10},{3,5},{4,12},{5,7},{6,14},{7,1},{8,16},{9,11},{... | collective-permute-start | bytes 786440 | tf_op jit(solution)/shard_map/ppermute | solution.py:340
  47.1 9.9 %collective-permute-start.12 = (bf16[8,128,128]{2,1,0:T(8,128)(2,1)S(1)}, bf16[8,128,128]{2,1,0:T(8,128)(2,1)S(1)}, u32[]{:S(2)}, u32[]{:S(2)}) collective-permute-start(bf16[8,128,128]{2,1,0:T(8,128)(2,1)S(1)} %get-tuple-element.67), channel_id=1, source_target_pairs={{0,16},{1,5},{2,18},{3,7},{4,20},{5,1},{6,22},{7,3},{8,24},{9,13},... | collective-permute-start | bytes 786440 | tf_op jit(solution)/shard_map/ppermute | solution.py:340
  49.9 7.7 %collective-permute-start.13 = (bf16[8,128,128]{2,1,0:T(8,128)(2,1)S(1)}, bf16[8,128,128]{2,1,0:T(8,128)(2,1)S(1)}, u32[]{:S(2)}, u32[]{:S(2)}) collective-permute-start(bf16[8,128,128]{2,1,0:T(8,128)(2,1)S(1)} %get-tuple-element.67), channel_id=1, source_target_pairs={{0,24},{1,7},{2,26},{3,1},{4,28},{5,3},{6,30},{7,5},{8,0},{9,15},{... | collective-permute-start | bytes 786440 | tf_op jit(solution)/shard_map/ppermute | solution.py:340
  58.5 8.0 %collective-permute-start.15 = (bf16[8,128,128]{2,1,0:T(8,128)(2,1)S(1)}, bf16[8,128,128]{2,1,0:T(8,128)(2,1)S(1)}, u32[]{:S(2)}, u32[]{:S(2)}) collective-permute-start(bf16[8,128,128]{2,1,0:T(8,128)(2,1)S(1)} %shard_map.84.refs_0_), channel_id=1, source_target_pairs={{0,4},{1,17},{2,6},{3,19},{4,0},{5,21},{6,2},{7,23},{8,12},{9,25},... | collective-permute-start | bytes 786440 | tf_op jit(solution)/shard_map/ppermute | solution.py:340
  58.5 10.7 %collective-permute-start.16 = (bf16[8,128,128]{2,1,0:T(8,128)(2,1)S(1)}, bf16[8,128,128]{2,1,0:T(8,128)(2,1)S(1)}, u32[]{:S(2)}, u32[]{:S(2)}) collective-permute-start(bf16[8,128,128]{2,1,0:T(8,128)(2,1)S(1)} %shard_map.84.refs_0_), channel_id=1, source_target_pairs={{0,2},{1,9},{2,4},{3,11},{4,6},{5,13},{6,0},{7,15},{8,10},{9,17},{... | collective-permute-start | bytes 786440 | tf_op jit(solution)/shard_map/ppermute | solution.py:340
  59.8 9.4 %collective-permute-start.17 = (bf16[8,128,128]{2,1,0:T(8,128)(2,1)S(1)}, bf16[8,128,128]{2,1,0:T(8,128)(2,1)S(1)}, u32[]{:S(2)}, u32[]{:S(2)}) collective-permute-start(bf16[8,128,128]{2,1,0:T(8,128)(2,1)S(1)} %shard_map.84.refs_0_), channel_id=1, source_target_pairs={{0,1},{1,0},{2,3},{3,2},{4,5},{5,4},{6,7},{7,6},{8,9},{9,8},{10,11... | collective-permute-start | bytes 786440 | tf_op jit(solution)/shard_map/ppermute | solution.py:330
  74.3 24.7 %collective-permute-start.21 = (bf16[8,128,128]{2,1,0:T(8,128)(2,1)S(1)}, bf16[8,128,128]{2,1,0:T(8,128)(2,1)S(1)}, u32[]{:S(2)}, u32[]{:S(2)}) collective-permute-start(bf16[8,128,128]{2,1,0:T(8,128)(2,1)S(1)} %get-tuple-element.69), channel_id=1, source_target_pairs={{0,32},{32,64},{64,96},{96,0},{1,33},{33,65},{65,97},{97,1},{2,34}... | collective-permute-start | bytes 786440 | tf_op jit(solution)/shard_map/ppermute | solution.py:330
  75.5 23.6 %collective-permute-start.22 = (bf16[8,128,128]{2,1,0:T(8,128)(2,1)S(1)}, bf16[8,128,128]{2,1,0:T(8,128)(2,1)S(1)}, u32[]{:S(2)}, u32[]{:S(2)}) collective-permute-start(bf16[8,128,128]{2,1,0:T(8,128)(2,1)S(1)} %get-tuple-element.70), channel_id=1, source_target_pairs={{0,64},{32,96},{64,0},{96,32},{1,65},{33,97},{65,1},{97,33},{2,66}... | collective-permute-start | bytes 786440 | tf_op jit(solution)/shard_map/ppermute | solution.py:330
  80.2 18.9 %collective-permute-start.23 = (bf16[8,128,128]{2,1,0:T(8,128)(2,1)S(1)}, bf16[8,128,128]{2,1,0:T(8,128)(2,1)S(1)}, u32[]{:S(2)}, u32[]{:S(2)}) collective-permute-start(bf16[8,128,128]{2,1,0:T(8,128)(2,1)S(1)} %get-tuple-element.71), channel_id=1, source_target_pairs={{0,96},{32,0},{64,32},{96,64},{1,97},{33,1},{65,33},{97,65},{2,98}... | collective-permute-start | bytes 786440 | tf_op jit(solution)/shard_map/ppermute | solution.py:330
  101.4 8.0 %collective-permute-start.30 = (bf16[1024,128]{1,0:T(8,128)(2,1)S(1)}, bf16[1024,128]{1,0:T(8,128)(2,1)S(1)}, u32[]{:S(2)}, u32[]{:S(2)}) collective-permute-start(bf16[1024,128]{1,0:T(8,128)(2,1)S(1)} %get-tuple-element.78.p0), channel_id=1, source_target_pairs={{0,64},{32,96},{64,0},{96,32},{1,65},{33,97},{65,1},{97,33},{2,66}... | collective-permute-start | bytes 786440 | tf_op jit(solution)/shard_map/ppermute | solution.py:325
  102.8 9.3 %collective-permute-start.31 = (bf16[1024,128]{1,0:T(8,128)(2,1)S(1)}, bf16[1024,128]{1,0:T(8,128)(2,1)S(1)}, u32[]{:S(2)}, u32[]{:S(2)}) collective-permute-start(bf16[1024,128]{1,0:T(8,128)(2,1)S(1)} %get-tuple-element.78.p0), channel_id=1, source_target_pairs={{0,32},{32,64},{64,96},{96,0},{1,33},{33,65},{65,97},{97,1},{2,34}... | collective-permute-start | bytes 786440 | tf_op jit(solution)/shard_map/ppermute | solution.py:325
  119.0 7.7 %collective-permute-start.33 = (bf16[8,128,128]{2,1,0:T(8,128)(2,1)S(1)}, bf16[8,128,128]{2,1,0:T(8,128)(2,1)S(1)}, u32[]{:S(2)}, u32[]{:S(2)}) collective-permute-start(bf16[8,128,128]{2,1,0:T(8,128)(2,1)S(1)} %get-tuple-element.82), channel_id=1, source_target_pairs={{0,2},{1,9},{2,4},{3,11},{4,6},{5,13},{6,0},{7,15},{8,10},{9,17},{... | collective-permute-start | bytes 786440 | tf_op jit(solution)/shard_map/ppermute | solution.py:340
  119.0 10.9 %collective-permute-start.34 = (bf16[8,128,128]{2,1,0:T(8,128)(2,1)S(1)}, bf16[8,128,128]{2,1,0:T(8,128)(2,1)S(1)}, u32[]{:S(2)}, u32[]{:S(2)}) collective-permute-start(bf16[8,128,128]{2,1,0:T(8,128)(2,1)S(1)} %get-tuple-element.83), channel_id=1, source_target_pairs={{0,4},{1,17},{2,6},{3,19},{4,0},{5,21},{6,2},{7,23},{8,12},{9,25},... | collective-permute-start | bytes 786440 | tf_op jit(solution)/shard_map/ppermute | solution.py:340
  122.8 7.5 %collective-permute-start.35 = (bf16[8,128,128]{2,1,0:T(8,128)(2,1)S(1)}, bf16[8,128,128]{2,1,0:T(8,128)(2,1)S(1)}, u32[]{:S(2)}, u32[]{:S(2)}) collective-permute-start(bf16[8,128,128]{2,1,0:T(8,128)(2,1)S(1)} %get-tuple-element.84), channel_id=1, source_target_pairs={{0,6},{1,25},{2,0},{3,27},{4,2},{5,29},{6,4},{7,31},{8,14},{9,1},{... | collective-permute-start | bytes 786440 | tf_op jit(solution)/shard_map/ppermute | solution.py:340
  130.4 8.2 %collective-permute-start.36 = (bf16[8,128,128]{2,1,0:T(8,128)(2,1)S(1)}, bf16[8,128,128]{2,1,0:T(8,128)(2,1)S(1)}, u32[]{:S(2)}, u32[]{:S(2)}) collective-permute-start(bf16[8,128,128]{2,1,0:T(8,128)(2,1)S(1)} %get-tuple-element.86), channel_id=1, source_target_pairs={{0,8},{1,3},{2,10},{3,5},{4,12},{5,7},{6,14},{7,1},{8,16},{9,11},{... | collective-permute-start | bytes 786440 | tf_op jit(solution)/shard_map/ppermute | solution.py:340
  133.6 9.6 %collective-permute-start.37 = (bf16[8,128,128]{2,1,0:T(8,128)(2,1)S(1)}, bf16[8,128,128]{2,1,0:T(8,128)(2,1)S(1)}, u32[]{:S(2)}, u32[]{:S(2)}) collective-permute-start(bf16[8,128,128]{2,1,0:T(8,128)(2,1)S(1)} %get-tuple-element.86), channel_id=1, source_target_pairs={{0,16},{1,5},{2,18},{3,7},{4,20},{5,1},{6,22},{7,3},{8,24},{9,13},... | collective-permute-start | bytes 786440 | tf_op jit(solution)/shard_map/ppermute | solution.py:340
  136.1 7.1 %collective-permute-start.38 = (bf16[8,128,128]{2,1,0:T(8,128)(2,1)S(1)}, bf16[8,128,128]{2,1,0:T(8,128)(2,1)S(1)}, u32[]{:S(2)}, u32[]{:S(2)}) collective-permute-start(bf16[8,128,128]{2,1,0:T(8,128)(2,1)S(1)} %get-tuple-element.86), channel_id=1, source_target_pairs={{0,24},{1,7},{2,26},{3,1},{4,28},{5,3},{6,30},{7,5},{8,0},{9,15},{... | collective-permute-start | bytes 786440 | tf_op jit(solution)/shard_map/ppermute | solution.py:340
  143.4 9.4 %collective-permute-start.39 = (bf16[8,128,128]{2,1,0:T(8,128)(2,1)S(1)}, bf16[8,128,128]{2,1,0:T(8,128)(2,1)S(1)}, u32[]{:S(2)}, u32[]{:S(2)}) collective-permute-start(bf16[8,128,128]{2,1,0:T(8,128)(2,1)S(1)} %shard_map.91.refs_0_), channel_id=1, source_target_pairs={{0,6},{1,25},{2,0},{3,27},{4,2},{5,29},{6,4},{7,31},{8,14},{9,1},{... | collective-permute-start | bytes 786440 | tf_op jit(solution)/shard_map/ppermute | solution.py:340
  146.1 8.0 %collective-permute-start.40 = (bf16[8,128,128]{2,1,0:T(8,128)(2,1)S(1)}, bf16[8,128,128]{2,1,0:T(8,128)(2,1)S(1)}, u32[]{:S(2)}, u32[]{:S(2)}) collective-permute-start(bf16[8,128,128]{2,1,0:T(8,128)(2,1)S(1)} %shard_map.91.refs_0_), channel_id=1, source_target_pairs={{0,4},{1,17},{2,6},{3,19},{4,0},{5,21},{6,2},{7,23},{8,12},{9,25},... | collective-permute-start | bytes 786440 | tf_op jit(solution)/shard_map/ppermute | solution.py:340
  146.1 10.4 %collective-permute-start.41 = (bf16[8,128,128]{2,1,0:T(8,128)(2,1)S(1)}, bf16[8,128,128]{2,1,0:T(8,128)(2,1)S(1)}, u32[]{:S(2)}, u32[]{:S(2)}) collective-permute-start(bf16[8,128,128]{2,1,0:T(8,128)(2,1)S(1)} %shard_map.91.refs_0_), channel_id=1, source_target_pairs={{0,2},{1,9},{2,4},{3,11},{4,6},{5,13},{6,0},{7,15},{8,10},{9,17},{... | collective-permute-start | bytes 786440 | tf_op jit(solution)/shard_map/ppermute | solution.py:340
  147.1 9.4 %collective-permute-start.42 = (bf16[8,128,128]{2,1,0:T(8,128)(2,1)S(1)}, bf16[8,128,128]{2,1,0:T(8,128)(2,1)S(1)}, u32[]{:S(2)}, u32[]{:S(2)}) collective-permute-start(bf16[8,128,128]{2,1,0:T(8,128)(2,1)S(1)} %shard_map.91.refs_0_), channel_id=1, source_target_pairs={{0,1},{1,0},{2,3},{3,2},{4,5},{5,4},{6,7},{7,6},{8,9},{9,8},{10,11... | collective-permute-start | bytes 786440 | tf_op jit(solution)/shard_map/ppermute | solution.py:330
  161.6 19.2 %collective-permute-start.46 = (bf16[8,128,128]{2,1,0:T(8,128)(2,1)S(1)}, bf16[8,128,128]{2,1,0:T(8,128)(2,1)S(1)}, u32[]{:S(2)}, u32[]{:S(2)}) collective-permute-start(bf16[8,128,128]{2,1,0:T(8,128)(2,1)S(1)} %get-tuple-element.88), channel_id=1, source_target_pairs={{0,32},{32,64},{64,96},{96,0},{1,33},{33,65},{65,97},{97,1},{2,34}... | collective-permute-start | bytes 786440 | tf_op jit(solution)/shard_map/ppermute | solution.py:330
  162.9 17.9 %collective-permute-start.47 = (bf16[8,128,128]{2,1,0:T(8,128)(2,1)S(1)}, bf16[8,128,128]{2,1,0:T(8,128)(2,1)S(1)}, u32[]{:S(2)}, u32[]{:S(2)}) collective-permute-start(bf16[8,128,128]{2,1,0:T(8,128)(2,1)S(1)} %get-tuple-element.89), channel_id=1, source_target_pairs={{0,64},{32,96},{64,0},{96,32},{1,65},{33,97},{65,1},{97,33},{2,66}... | collective-permute-start | bytes 786440 | tf_op jit(solution)/shard_map/ppermute | solution.py:330
  165.5 15.4 %collective-permute-start.48 = (bf16[8,128,128]{2,1,0:T(8,128)(2,1)S(1)}, bf16[8,128,128]{2,1,0:T(8,128)(2,1)S(1)}, u32[]{:S(2)}, u32[]{:S(2)}) collective-permute-start(bf16[8,128,128]{2,1,0:T(8,128)(2,1)S(1)} %get-tuple-element.90), channel_id=1, source_target_pairs={{0,96},{32,0},{64,32},{96,64},{1,97},{33,1},{65,33},{97,65},{2,98}... | collective-permute-start | bytes 786440 | tf_op jit(solution)/shard_map/ppermute | solution.py:330
  170.5 6.7 %collective-permute-start.50 = (bf16[32,128]{1,0:T(8,128)(2,1)S(1)}, bf16[32,128]{1,0:T(8,128)(2,1)S(1)}, u32[]{:S(2)}, u32[]{:S(2)}) collective-permute-start(bf16[32,128]{1,0:T(8,128)(2,1)S(1)} %get-tuple-element.93), channel_id=1, source_target_pairs={{0,32},{32,64},{64,96},{96,0},{1,33},{33,65},{65,97},{97,1},{2,34}... | collective-permute-start | bytes 24584 | tf_op jit(solution)/shard_map/ppermute | solution.py:330
  171.5 6.8 %collective-permute-start.51 = (bf16[32,128]{1,0:T(8,128)(2,1)S(1)}, bf16[32,128]{1,0:T(8,128)(2,1)S(1)}, u32[]{:S(2)}, u32[]{:S(2)}) collective-permute-start(bf16[32,128]{1,0:T(8,128)(2,1)S(1)} %get-tuple-element.94), channel_id=1, source_target_pairs={{0,64},{32,96},{64,0},{96,32},{1,65},{33,97},{65,1},{97,33},{2,66}... | collective-permute-start | bytes 24584 | tf_op jit(solution)/shard_map/ppermute | solution.py:330
  (22 other events, 89.7 us)
